TPU v7x, 32 devices: a whole 2x2x4 slice. The times are simulated.
32 devices in a mesh: dp: 8 (over z, core), expert: 4 (over y, x).
Axes of the slice: x: 2, y: 2, z: 4, core: 2. Of those that a mesh axis runs over, the one named last changes fastest.
Arguments:
- tokens: bfloat16 [4096, 2048], P(('dp', 'expert')), may hold values from -6 to 6
- expert_ids: int32 [4096, 8], P(('dp', 'expert')), may hold values from 0 to 127, as said below
- gate_probs: float32 [4096, 8], P(('dp', 'expert')), may hold values from 0.1 to 1
- cotangent: bfloat16 [4096, 2048], P(('dp', 'expert')), may hold values from -1.5 to 1.5
- expert_weights: bfloat16 [2048, 4, 3, 768], P(None, 'expert'), may hold values from -0.21875 to 0.21875
Outputs:
- mixed: bfloat16 [4096, 2048], P(('dp', 'expert'))
- grad_tokens: bfloat16 [4096, 2048], P(('dp', 'expert'))
- grad_gates: float32 [4096, 8], P(('dp', 'expert'))
- grad_weights: bfloat16 [2048, 4, 3, 768], P('dp', 'expert')
Inputs may be any that keep to these rules, and one draw needn't show every extreme that they name: `expert_ids`: each row names 8 different experts. In the rows of one device every expert below 4 is named by 1 to 24 rows, and for every index of dp some such expert is named by exactly 24 rows of each device of that index.
All inputs are finite; a program needn't handle non-finite values.
Results may differ from a plain program's by a relative error of at most 0.0058.
Values may be sent and summed in bfloat16 or wider, within the bound.
No kernel may reach another device: no remote copies, remote signals or barrier semaphores. Data moves between devices by JAX's collectives and lax.ppermute only.
A program may use at most 128 MiB of HBM per device.

v0:
```python
import functools

import jax
import jax.numpy as jnp
from jax import lax
from jax.experimental import pallas as pl
from jax.experimental.pallas import tpu as pltpu
from jax.sharding import PartitionSpec as P

CAP = 24
CORES = 2
F32 = jnp.float32
BF16 = jnp.bfloat16
VMEM = pl.BlockSpec(memory_space=pltpu.VMEM)
HBM = pl.BlockSpec(memory_space=pltpu.HBM)
NT = (((1,), (1,)), ((), ()))
TN = (((0,), (0,)), ((), ()))


def shape_of(dims, dtype=BF16):
    return jax.ShapeDtypeStruct(dims, dtype)


def local_call(body, outs, args, flops, scratch=(), megabytes=24, space=VMEM):
    moved = sum(a.size * a.dtype.itemsize for a in list(args) + list(outs))
    return pl.pallas_call(
        body,
        out_shape=outs,
        in_specs=[space] * len(args),
        out_specs=[VMEM] * len(outs),
        scratch_shapes=list(scratch),
        compiler_params=pltpu.CompilerParams(vmem_limit_bytes=megabytes << 20),
        cost_estimate=pl.CostEstimate(
            flops=int(flops), bytes_accessed=int(moved), transcendentals=0
        ),
    )(*args)


def slot_map(ids, probs, me, experts):
    tokens = ids.shape[1]
    before = (
        lax.broadcasted_iota(jnp.int32, (tokens, tokens), 0)
        < lax.broadcasted_iota(jnp.int32, (tokens, tokens), 1)
    ).astype(BF16)
    named = []
    weight = []
    for m in range(experts):
        hit = ids == jnp.bitwise_xor(me, m)
        named.append(jnp.sum(hit.astype(F32), axis=0, keepdims=True))
        weight.append(jnp.sum(jnp.where(hit, probs, 0.0), axis=0, keepdims=True))
    mask = jnp.concatenate(named, axis=0)
    pos = jnp.dot(mask.astype(BF16), before, preferred_element_type=F32)
    rank = lax.broadcasted_iota(jnp.int32, (CAP, tokens), 0).astype(F32)
    blocks = []
    slot_probs = []
    for m in range(experts):
        hot = jnp.where((rank == pos[m : m + 1]) & (mask[m : m + 1] > 0.5), 1.0, 0.0)
        blocks.append(hot)
        slot_probs.append(jnp.sum(hot * weight[m], axis=1, keepdims=True))
    return jnp.concatenate(blocks, axis=0), jnp.concatenate(slot_probs, axis=0)


def stage_kernel(w_ref, out_ref, sem):
    copies = [
        pltpu.make_async_copy(w_ref.at[j], out_ref.at[j], sem.at[j])
        for j in range(w_ref.shape[0])
    ]
    for copy in copies:
        copy.start()
    for copy in copies:
        copy.wait()


def send_kernel(experts, zs, *refs):
    sources, refs = refs[:4], refs[4:]
    rows_out, feats_out = refs[:experts], refs[experts : experts + zs]
    scratch = refs[experts + zs : experts + zs + 2]
    held, sem = refs[experts + zs + 2 : -1], refs[-1]
    copies = [
        pltpu.make_async_copy(a, b, sem.at[j]) for j, (a, b) in enumerate(zip(sources, held))
    ]
    for copy in copies:
        copy.start()
    for copy in copies:
        copy.wait()
    ids_ref, probs_ref, tok_ref, cot_ref = held
    me = lax.axis_index("expert")
    dp = lax.axis_index("dp")
    z, c = dp // CORES, dp % CORES
    onehot, slot_probs = slot_map(ids_ref[...], probs_ref[...], me, experts)
    pick = onehot.astype(BF16)
    x_rows = jnp.dot(pick, tok_ref[...], preferred_element_type=F32)
    dy_rows = slot_probs * jnp.dot(pick, cot_ref[...], preferred_element_type=F32)
    part = x_rows.shape[1] // (zs * CORES)
    for j, value in enumerate((x_rows, dy_rows)):
        for m in range(experts):
            rows_out[m][j] = value[m * CAP : (m + 1) * CAP].astype(BF16)
        scratch[j][...] = value
        for m in range(zs):
            chip = jnp.bitwise_xor(z, m) * CORES
            for h in range(CORES):
                start = (chip + jnp.bitwise_xor(c, h)) * part
                piece = scratch[j][:, pl.ds(pl.multiple_of(start, part), part)]
                at = (j * CORES + h) * part
                for k in range(experts):
                    feats_out[m][k, :, at : at + part] = piece[
                        k * CAP : (k + 1) * CAP
                    ].astype(BF16)


def stack_rows(blocks):
    return jnp.concatenate([b.astype(F32) for b in blocks], axis=0).astype(BF16)


def ffn_kernel(experts, w_ref, *refs):
    blocks, out_ref = refs[:experts], refs[experts]
    hidden = w_ref.shape[2]
    x = stack_rows([b[0] for b in blocks])
    dy = stack_rows([b[1] for b in blocks])
    gate = jnp.dot(x, w_ref[0], preferred_element_type=F32)
    up = jnp.dot(x, w_ref[1], preferred_element_type=F32)
    s = jax.nn.sigmoid(gate)
    out_ref[:, 0:hidden] = (gate * s * up).astype(BF16)
    grad = jnp.dot(dy, w_ref[2], preferred_element_type=F32)
    out_ref[:, hidden : 2 * hidden] = (grad * up * s * (1.0 + gate * (1.0 - s))).astype(BF16)
    out_ref[:, 2 * hidden :] = (grad * (gate * s)).astype(BF16)


def output_kernel(experts, w_ref, acts_ref, *outs):
    hidden = w_ref.shape[2]
    hid, gg = acts_ref[:, 0:hidden], acts_ref[:, hidden : 2 * hidden]
    ug = acts_ref[:, 2 * hidden :]
    out = lax.dot_general(hid, w_ref[2], NT, preferred_element_type=F32)
    part = lax.dot_general(gg, w_ref[0], NT, preferred_element_type=F32)
    part += lax.dot_general(ug, w_ref[1], NT, preferred_element_type=F32)
    for m in range(experts):
        outs[m][0] = out[m * CAP : (m + 1) * CAP].astype(BF16)
        outs[m][1] = part[m * CAP : (m + 1) * CAP].astype(BF16)


def combine_kernel(experts, ids_ref, probs_ref, cot_ref, *refs):
    blocks, (mixed_ref, gtok_ref, gates_ref) = refs[:experts], refs[experts:]
    ids = ids_ref[...]
    me = lax.axis_index("expert")
    onehot, slot_probs = slot_map(ids, probs_ref[...], me, experts)
    pick = onehot.astype(BF16)
    out = jnp.concatenate([b[0].astype(F32) for b in blocks], axis=0)
    weighted = out * slot_probs
    high = weighted.astype(BF16)
    low = (weighted - high.astype(F32)).astype(BF16)
    mixed = lax.dot_general(pick, high, TN, preferred_element_type=F32)
    mixed += lax.dot_general(pick, low, TN, preferred_element_type=F32)
    mixed_ref[...] = mixed.astype(BF16)
    part = stack_rows([b[1] for b in blocks])
    gtok = lax.dot_general(pick, part, TN, preferred_element_type=F32)
    gtok_ref[...] = gtok.astype(BF16)
    cot_rows = jnp.dot(pick, cot_ref[...], preferred_element_type=F32)
    inner = jnp.sum(out * cot_rows, axis=1, keepdims=True)
    spread = onehot * inner
    gates = jnp.zeros(ids.shape, F32)
    for m in range(experts):
        value = jnp.sum(spread[m * CAP : (m + 1) * CAP], axis=0, keepdims=True)
        gates = jnp.where(ids == jnp.bitwise_xor(me, m), value, gates)
    gates_ref[...] = gates


def regroup_kernel(experts, zs, *refs):
    for k in range(experts):
        for m in range(zs):
            refs[zs + k][m] = refs[m][k]


def grad_sums(feats, acts, at):
    rows_f = stack_rows([f[m] for m in at for f in feats])
    rows_a = acts[0]
    for more in acts[1:]:
        rows_a = jnp.concatenate([rows_a, more], axis=0)
    half = rows_f.shape[1] // 2
    hidden = rows_a.shape[1] // 3
    both = lax.dot_general(
        rows_f[:, :half], rows_a[:, hidden:], TN, preferred_element_type=F32
    )
    down = lax.dot_general(
        rows_f[:, half:], rows_a[:, :hidden], TN, preferred_element_type=F32
    )
    return both, down


def early_grad_kernel(experts, at, *refs):
    feats, acts, total = refs[:experts], refs[experts:-1], refs[-1]
    both, down = grad_sums(feats, [a[...] for a in acts], at)
    total[:, : both.shape[1]] = both
    total[:, both.shape[1] :] = down


def late_grad_kernel(experts, at, *refs):
    feats, (total, *acts), (own, send) = refs[:experts], refs[experts:-2], refs[-2:]
    last = acts[0][...].astype(F32)
    for more in acts[1:]:
        last += more[...].astype(F32)
    both, down = grad_sums(feats, [last.astype(BF16)], at)
    half = both.shape[0] // CORES
    n = both.shape[1]
    own[:, :n] = total[:half, :n] + both[:half]
    own[:, n:] = total[:half, n:] + down[:half]
    send[:, :n] = (total[half:, :n] + both[half:]).astype(BF16)
    send[:, n:] = (total[half:, n:] + down[half:]).astype(BF16)


def final_kernel(own, got, out):
    hidden = out.shape[2]
    for j in range(3):
        at = slice(j * hidden, (j + 1) * hidden)
        out[j] = (own[:, at] + got[:, at].astype(F32)).astype(BF16)


def per_device(tokens, expert_ids, gate_probs, cotangent, expert_weights):
    tok_rows, width = tokens.shape
    experts = lax.axis_size("expert")
    groups = lax.axis_size("dp")
    zs = groups // CORES
    hidden = expert_weights.shape[3]
    rows = experts * CAP
    chip_width = width // zs
    weights = jnp.transpose(expert_weights[:, 0], (1, 0, 2))
    ids, probs = expert_ids.T, gate_probs.T

    def swap_expert(blocks):
        moved = list(blocks)
        for m in range(experts - 1, 0, -1):
            pairs = [(i, i ^ m) for i in range(experts)]
            moved[m] = lax.ppermute(blocks[m], "expert", pairs)
        return moved

    def swap_z(block, m, only=None):
        pairs = []
        for z in range(zs):
            if only is None or z in only:
                pairs += [(z * CORES + c, (z ^ m) * CORES + c) for c in range(CORES)]
        return lax.ppermute(block, "dp", pairs)

    def spread_z(block):
        if zs != 4:
            return [[swap_z(block, m)] for m in range(1, zs)]
        far = swap_z(block, 2)
        near = swap_z(block, 1)
        middle = swap_z(block, 3, (1, 2))
        ends = swap_z(far, 1, (1, 2))
        return [[near], [far], [middle, ends]]

    sent = local_call(
        functools.partial(send_kernel, experts, zs),
        [shape_of((2, CAP, width))] * experts + [shape_of((experts, CAP, 2 * chip_width))] * zs,
        [ids, probs, tokens, cotangent],
        4 * rows * tok_rows * width,
        [pltpu.VMEM((rows, width), F32)] * 2
        + [pltpu.VMEM(a.shape, a.dtype) for a in (ids, probs, tokens, cotangent)]
        + [pltpu.SemaphoreType.DMA((4,))],
        space=HBM,
    )
    (staged,) = local_call(
        stage_kernel,
        [shape_of(weights.shape)],
        [weights],
        0,
        [pltpu.SemaphoreType.DMA((3,))],
        space=HBM,
    )
    blocks = swap_expert(sent[:experts])
    shares = [sent[experts]] + [swap_z(sent[experts + m], m) for m in range(1, zs)]

    (acts,) = local_call(
        functools.partial(ffn_kernel, experts),
        [shape_of((rows, 3 * hidden))],
        [staged, *blocks],
        6 * rows * width * hidden,
    )
    near_far = spread_z(acts)
    results = local_call(
        functools.partial(output_kernel, experts),
        [shape_of((2, CAP, width))] * experts,
        [staged, acts],
        6 * rows * width * hidden,
    )
    back = swap_expert(results)
    by_expert = local_call(
        functools.partial(regroup_kernel, experts, zs),
        [shape_of((zs, CAP, 2 * chip_width))] * experts,
        shares,
        0,
    )
    feats = swap_expert(by_expert)
    mixed, grad_tokens, gates = local_call(
        functools.partial(combine_kernel, experts),
        [shape_of((tok_rows, width)), shape_of((tok_rows, width)), shape_of(ids.shape, F32)],
        [ids, probs, cotangent, *back],
        8 * rows * tok_rows * width,
    )
    early = near_far[:-1]
    (total,) = local_call(
        functools.partial(early_grad_kernel, experts, tuple(range(zs - 1))),
        [shape_of((chip_width, 3 * hidden), F32)],
        [*feats, acts, *[a for piece in early for a in piece]],
        6 * (zs - 1) * rows * chip_width * hidden,
    )
    own, send = local_call(
        functools.partial(late_grad_kernel, experts, (zs - 1,)),
        [
            shape_of((chip_width // CORES, 3 * hidden), F32),
            shape_of((chip_width // CORES, 3 * hidden)),
        ],
        [*feats, total, *near_far[-1]],
        6 * rows * chip_width * hidden,
    )
    got = lax.ppermute(send, "dp", [(i, i ^ 1) for i in range(groups)])
    (grads,) = local_call(
        final_kernel,
        [shape_of((3, width // groups, hidden))],
        [own, got],
        3 * width * hidden // groups,
    )
    grad_weights = jnp.transpose(grads, (1, 0, 2))[:, None]
    return mixed, grad_tokens, gates.T, grad_weights


def solution(mesh):
    both = P(("dp", "expert"), None)
    return jax.shard_map(
        per_device,
        mesh=mesh,
        in_specs=(both, both, both, both, P(None, "expert", None, None)),
        out_specs=(both, both, both, P("dp", "expert", None, None)),
        check_vma=False,
    )
```

profile of v0, /device:TPU:0, one launch (start us, length us, event | category | flops | bytes accessed | tf_op | source)
XLA Modules:
  0.0 94.6 jit_solution(11322861877139480350)
XLA Ops:
  0.6 0.0 copy-start.1
  0.6 1.0 %copy-done.1 = bf16[128,2048]{1,0:T(8,128)(2,1)S(1)} copy-done((bf16[128,2048]{1,0:T(8,128)(2,1)S(1)}, bf16[128,2048]{1,0:T(8,128)(2,1)}, u32[]{:S(2)}) %copy-start.1) | copy-done | bytes 524312
  1.7 0.0 copy-start.3
  1.7 1.0 %copy-done.3 = bf16[128,2048]{1,0:T(8,128)(2,1)S(1)} copy-done((bf16[128,2048]{1,0:T(8,128)(2,1)S(1)}, bf16[128,2048]{1,0:T(8,128)(2,1)}, u32[]{:S(2)}) %copy-start.3) | copy-done | bytes 524312
  2.7 0.0 copy-start.4
  2.7 0.7 copy-done.4
  3.4 0.0 copy-start.6
  3.4 0.7 copy-done.6
  4.1 0.7 shard_map.85
  4.8 3.0 %collective-permute-start = (bf16[2,24,2048]{2,1,0:T(8,128)(2,1)S(1)}, bf16[2,24,2048]{2,1,0:T(8,128)(2,1)S(1)}, u32[]{:S(2)}, u32[]{:S(2)}) collective-permute-start(bf16[2,24,2048]{2,1,0:T(8,128)(2,1)S(1)} %get-tuple-element.26), channel_id=1, source_target_pairs={{0,1},{1,0},{2,3},{3,2},{4,5},{5,4},{6,7},{7,6},{8,9},{9,8},{10,11... | collective-permute-start | bytes 589832 | tf_op jit(solution)/shard_map/ppermute | solution.py:232
  7.8 1.5 %collective-permute-start.1 = (bf16[2,24,2048]{2,1,0:T(8,128)(2,1)S(1)}, bf16[2,24,2048]{2,1,0:T(8,128)(2,1)S(1)}, u32[]{:S(2)}, u32[]{:S(2)}) collective-permute-start(bf16[2,24,2048]{2,1,0:T(8,128)(2,1)S(1)} %get-tuple-element.27), channel_id=1, source_target_pairs={{0,2},{1,3},{2,0},{3,1},{4,6},{5,7},{6,4},{7,5},{8,10},{9,11},{10,... | collective-permute-start | bytes 589832 | tf_op jit(solution)/shard_map/ppermute | solution.py:232
  9.3 0.0 collective-permute-start.2
  9.4 0.0 copy-start
  9.4 3.7 %copy-done = bf16[2048,1,3,768]{3,0,2,1:T(8,128)(2,1)S(1)} copy-done((bf16[2048,1,3,768]{3,0,2,1:T(8,128)(2,1)S(1)}, bf16[2048,1,3,768]{3,0,2,1:T(8,128)(2,1)}, u32[]{:S(2)}) %copy-start) | copy-done | bytes 9437208
  13.0 0.7 shard_map.84.w_ref
  13.7 0.0 collective-permute-done.refs_1_
  13.7 4.7 %collective-permute-done.1.refs_2_ = bf16[2,24,2048]{2,1,0:T(8,128)(2,1)S(1)} collective-permute-done((bf16[2,24,2048]{2,1,0:T(8,128)(2,1)S(1)}, bf16[2,24,2048]{2,1,0:T(8,128)(2,1)S(1)}, u32[]{:S(2)}, u32[]{:S(2)}) %collective-permute-start.1) | collective-permute-done | bytes 196640 | tf_op jit(solution)/shard_map/ppermute | solution.py:232
  18.4 0.0 collective-permute-done.2.refs_3_
  18.4 1.7 %shard_map.86.acts_ref.refs_4_ = bf16[96,2304]{1,0:T(8,128)(2,1)S(1)} custom-call(bf16[3,2048,768]{2,1,0:T(8,128)(2,1)S(1)} %shard_map.84.w_ref, bf16[2,24,2048]{2,1,0:T(8,128)(2,1)S(1)} %get-tuple-element.25.refs_0_, bf16[2,24,2048]{2,1,0:T(8,128)(2,1)S(1)} %collective-permute-done.refs_1_, bf16[2,24,2048]{2,1,0:T(8,128)(2,1)S(1)} %collective-permute-done.1.refs_2_, ...), custom_call_target="tpu_custom_call" | custom-call | flops 905969664 | bytes 10665984 | tf_op jit(solution)/shard_map/pallas_call | solution.py:26
  20.1 2.6 %collective-permute-start.13 = (bf16[96,2304]{1,0:T(8,128)(2,1)S(1)}, bf16[96,2304]{1,0:T(8,128)(2,1)S(1)}, u32[]{:S(2)}, u32[]{:S(2)}) collective-permute-start(bf16[96,2304]{1,0:T(8,128)(2,1)S(1)} %shard_map.86.acts_ref.refs_4_), channel_id=1, source_target_pairs={{0,16},{4,20},{8,24},{12,28},{16,0},{20,4},{24,8},{28,12},{1,17},{... | collective-permute-start | bytes 1327112 | tf_op jit(solution)/shard_map/ppermute | solution.py:240
  22.7 1.6 %collective-permute-start.6 = (bf16[4,24,1024]{2,1,0:T(8,128)(2,1)S(1)}, bf16[4,24,1024]{2,1,0:T(8,128)(2,1)S(1)}, u32[]{:S(2)}, u32[]{:S(2)}) collective-permute-start(bf16[4,24,1024]{2,1,0:T(8,128)(2,1)S(1)} %get-tuple-element.37), channel_id=1, source_target_pairs={{0,8},{4,12},{8,0},{12,4},{16,24},{20,28},{24,16},{28,20},{1,9},{5... | collective-permute-start | bytes 589832 | tf_op jit(solution)/shard_map/ppermute | solution.py:240
  24.3 0.3 collective-permute-start.7
  24.6 2.5 %collective-permute-start.8 = (bf16[4,24,1024]{2,1,0:T(8,128)(2,1)S(1)}, bf16[4,24,1024]{2,1,0:T(8,128)(2,1)S(1)}, u32[]{:S(2)}, u32[]{:S(2)}) collective-permute-start(bf16[4,24,1024]{2,1,0:T(8,128)(2,1)S(1)} %get-tuple-element.39), channel_id=1, source_target_pairs={{0,24},{4,28},{8,16},{12,20},{16,8},{20,12},{24,0},{28,4},{1,25},{... | collective-permute-start | bytes 589832 | tf_op jit(solution)/shard_map/ppermute | solution.py:240
  27.1 0.7 collective-permute-start.12
  27.8 9.7 %collective-permute-done.6.refs_1_ = bf16[4,24,1024]{2,1,0:T(8,128)(2,1)S(1)} collective-permute-done((bf16[4,24,1024]{2,1,0:T(8,128)(2,1)S(1)}, bf16[4,24,1024]{2,1,0:T(8,128)(2,1)S(1)}, u32[]{:S(2)}, u32[]{:S(2)}) %collective-permute-start.6) | collective-permute-done | bytes 196640 | tf_op jit(solution)/shard_map/ppermute | solution.py:240
  37.5 17.6 %collective-permute-done.7.refs_2_ = bf16[4,24,1024]{2,1,0:T(8,128)(2,1)S(1)} collective-permute-done((bf16[4,24,1024]{2,1,0:T(8,128)(2,1)S(1)}, bf16[4,24,1024]{2,1,0:T(8,128)(2,1)S(1)}, u32[]{:S(2)}, u32[]{:S(2)}) %collective-permute-start.7) | collective-permute-done | bytes 196640 | tf_op jit(solution)/shard_map/ppermute | solution.py:240
  55.1 0.0 collective-permute-done.8.refs_3_
  55.1 0.1 shard_map.89
  55.2 1.5 %collective-permute-start.9 = (bf16[4,24,1024]{2,1,0:T(8,128)(2,1)S(1)}, bf16[4,24,1024]{2,1,0:T(8,128)(2,1)S(1)}, u32[]{:S(2)}, u32[]{:S(2)}) collective-permute-start(bf16[4,24,1024]{2,1,0:T(8,128)(2,1)S(1)} %get-tuple-element.41), channel_id=1, source_target_pairs={{0,1},{1,0},{2,3},{3,2},{4,5},{5,4},{6,7},{7,6},{8,9},{9,8},{10,11... | collective-permute-start | bytes 589832 | tf_op jit(solution)/shard_map/ppermute | solution.py:232
  56.7 0.7 collective-permute-start.14
  57.4 0.0 collective-permute-done.13.refs_6_
  57.4 1.3 %collective-permute-start.15 = (bf16[96,2304]{1,0:T(8,128)(2,1)S(1)}, bf16[96,2304]{1,0:T(8,128)(2,1)S(1)}, u32[]{:S(2)}, u32[]{:S(2)}) collective-permute-start(bf16[96,2304]{1,0:T(8,128)(2,1)S(1)} %collective-permute-done.13.refs_6_), channel_id=1, source_target_pairs={{8,0},{12,4},{16,24},{20,28},{9,1},{13,5},{17,25},{21,29},{10,2},{... | collective-permute-start | bytes 1327112 | tf_op jit(solution)/shard_map/ppermute | solution.py:240
  58.7 0.6 collective-permute-start.10
  59.3 2.2 %collective-permute-done.9.refs_1_ = bf16[4,24,1024]{2,1,0:T(8,128)(2,1)S(1)} collective-permute-done((bf16[4,24,1024]{2,1,0:T(8,128)(2,1)S(1)}, bf16[4,24,1024]{2,1,0:T(8,128)(2,1)S(1)}, u32[]{:S(2)}, u32[]{:S(2)}) %collective-permute-start.9) | collective-permute-done | bytes 196640 | tf_op jit(solution)/shard_map/ppermute | solution.py:232
  61.5 0.9 collective-permute-start.11
  62.3 3.8 %collective-permute-done.10.refs_2_ = bf16[4,24,1024]{2,1,0:T(8,128)(2,1)S(1)} collective-permute-done((bf16[4,24,1024]{2,1,0:T(8,128)(2,1)S(1)}, bf16[4,24,1024]{2,1,0:T(8,128)(2,1)S(1)}, u32[]{:S(2)}, u32[]{:S(2)}) %collective-permute-start.10) | collective-permute-done | bytes 196640 | tf_op jit(solution)/shard_map/ppermute | solution.py:232
  66.2 1.8 %collective-permute-done.11.refs_3_ = bf16[4,24,1024]{2,1,0:T(8,128)(2,1)S(1)} collective-permute-done((bf16[4,24,1024]{2,1,0:T(8,128)(2,1)S(1)}, bf16[4,24,1024]{2,1,0:T(8,128)(2,1)S(1)}, u32[]{:S(2)}, u32[]{:S(2)}) %collective-permute-start.11) | collective-permute-done | bytes 196640 | tf_op jit(solution)/shard_map/ppermute | solution.py:232
  68.0 0.0 collective-permute-done.12.refs_5_
  68.0 1.4 %shard_map.90.refs_4_ = f32[512,2304]{1,0:T(8,128)S(1)} custom-call(bf16[4,24,1024]{2,1,0:T(8,128)(2,1)S(1)} %get-tuple-element.40.refs_0_, bf16[4,24,1024]{2,1,0:T(8,128)(2,1)S(1)} %collective-permute-done.9.refs_1_, bf16[4,24,1024]{2,1,0:T(8,128)(2,1)S(1)} %collective-permute-done.10.refs_2_, bf16[4,24,1024]{2,1,0:T(8,128)(2,1)S(1)} %collective-permute-done.11.refs_3_, ...), custom_call_target="tpu_custom_call" | custom-call | flops 679477248 | bytes 6832128 | tf_op jit(solution)/shard_map/pallas_call | solution.py:26
  69.5 0.0 collective-permute-done.14.refs_5_
  69.5 6.4 %collective-permute-done.15.refs_6_ = bf16[96,2304]{1,0:T(8,128)(2,1)S(1)} collective-permute-done((bf16[96,2304]{1,0:T(8,128)(2,1)S(1)}, bf16[96,2304]{1,0:T(8,128)(2,1)S(1)}, u32[]{:S(2)}, u32[]{:S(2)}) %collective-permute-start.15) | collective-permute-done | bytes 442400 | tf_op jit(solution)/shard_map/ppermute | solution.py:240
  75.9 0.8 shard_map.91
  76.7 0.0 copy-start.2
  76.7 0.0 copy-start.5
  76.7 0.0 copy-start.7
  76.8 0.1 collective-permute-start.16
  76.8 3.0 %shard_map.87 = (bf16[2,24,2048]{2,1,0:T(8,128)(2,1)S(1)}, bf16[2,24,2048]{2,1,0:T(8,128)(2,1)S(1)}, bf16[2,24,2048]{2,1,0:T(8,128)(2,1)S(1)}, bf16[2,24,2048]{2,1,0:T(8,128)(2,1)S(1)}) custom-call(bf16[3,2048,768]{2,1,0:T(8,128)(2,1)S(1)} %shard_map.84.w_ref, bf16[96,2304]{1,0:T(8,128)(2,1)S(1)} %shard_map.86.acts_ref.refs_4_), custom_call_target="tpu_custom_call" | custom-call | flops 905969664 | bytes 10665984 | tf_op jit(solution)/shard_map/pallas_call | solution.py:26
  79.8 0.6 collective-permute-start.3
  80.4 0.5 collective-permute-start.4
  81.0 2.4 %collective-permute-start.5 = (bf16[2,24,2048]{2,1,0:T(8,128)(2,1)S(1)}, bf16[2,24,2048]{2,1,0:T(8,128)(2,1)S(1)}, u32[]{:S(2)}, u32[]{:S(2)}) collective-permute-start(bf16[2,24,2048]{2,1,0:T(8,128)(2,1)S(1)} %get-tuple-element.32), channel_id=1, source_target_pairs={{0,3},{1,2},{2,1},{3,0},{4,7},{5,6},{6,5},{7,4},{8,11},{9,10},{10,... | collective-permute-start | bytes 589832 | tf_op jit(solution)/shard_map/ppermute | solution.py:232
  83.3 4.3 %collective-permute-done.3.refs_1_ = bf16[2,24,2048]{2,1,0:T(8,128)(2,1)S(1)} collective-permute-done((bf16[2,24,2048]{2,1,0:T(8,128)(2,1)S(1)}, bf16[2,24,2048]{2,1,0:T(8,128)(2,1)S(1)}, u32[]{:S(2)}, u32[]{:S(2)}) %collective-permute-start.3) | collective-permute-done | bytes 196640 | tf_op jit(solution)/shard_map/ppermute | solution.py:232
  87.6 4.0 %collective-permute-done.4.refs_2_ = bf16[2,24,2048]{2,1,0:T(8,128)(2,1)S(1)} collective-permute-done((bf16[2,24,2048]{2,1,0:T(8,128)(2,1)S(1)}, bf16[2,24,2048]{2,1,0:T(8,128)(2,1)S(1)}, u32[]{:S(2)}, u32[]{:S(2)}) %collective-permute-start.4) | collective-permute-done | bytes 196640 | tf_op jit(solution)/shard_map/ppermute | solution.py:232
  91.7 0.0 collective-permute-done.5.refs_3_
  91.7 0.0 copy-done.2
  91.7 0.0 copy-done.5
  91.7 0.0 copy-done.7
  91.7 1.7 %shard_map.88 = (bf16[128,2048]{1,0:T(8,128)(2,1)}, bf16[128,2048]{1,0:T(8,128)(2,1)}, f32[8,128]{1,0:T(8,128)}) custom-call(s32[8,128]{1,0:T(8,128)S(1)} %bitcast.11, f32[8,128]{1,0:T(8,128)S(1)} %bitcast.13, bf16[128,2048]{1,0:T(8,128)(2,1)S(1)} %copy-done.2, bf16[2,24,2048]{2,1,0:T(8,128)(2,1)S(1)} %get-tuple-element.29.refs_0_, ...), custom_call_target="tpu_custom_call" | custom-call | flops 201326592 | bytes 2371584 | tf_op jit(solution)/shard_map/pallas_call | solution.py:26
  93.4 0.0 collective-permute-done.16.got
  93.4 1.2 %shard_map.92 = bf16[3,256,768]{2,1,0:T(8,128)(2,1)} custom-call(f32[256,2304]{1,0:T(8,128)S(1)} %get-tuple-element.44.own, bf16[256,2304]{1,0:T(8,128)(2,1)S(1)} %collective-permute-done.16.got), custom_call_target="tpu_custom_call" | custom-call | flops 589824 | bytes 4718592 | tf_op jit(solution)/shard_map/pallas_call | solution.py:26
Async XLA Ops:
  0.6 1.0 %copy-start.1 = (bf16[128,2048]{1,0:T(8,128)(2,1)S(1)}, bf16[128,2048]{1,0:T(8,128)(2,1)}, u32[]{:S(2)}) copy-start(bf16[128,2048]{1,0:T(8,128)(2,1)} %cot_ref.1) | copy-start | bytes 1572868
  1.7 1.0 %copy-start.3 = (bf16[128,2048]{1,0:T(8,128)(2,1)S(1)}, bf16[128,2048]{1,0:T(8,128)(2,1)}, u32[]{:S(2)}) copy-start(bf16[128,2048]{1,0:T(8,128)(2,1)} %refs_2_.1) | copy-start | bytes 1572868
  2.7 0.7 copy-start.4
  3.4 0.7 copy-start.6
  4.8 8.9 %collective-permute-start = (bf16[2,24,2048]{2,1,0:T(8,128)(2,1)S(1)}, bf16[2,24,2048]{2,1,0:T(8,128)(2,1)S(1)}, u32[]{:S(2)}, u32[]{:S(2)}) collective-permute-start(bf16[2,24,2048]{2,1,0:T(8,128)(2,1)S(1)} %get-tuple-element.26), channel_id=1, source_target_pairs={{0,1},{1,0},{2,3},{3,2},{4,5},{5,4},{6,7},{7,6},{8,9},{9,8},{10,11... | collective-permute-start | bytes 589832 | tf_op jit(solution)/shard_map/ppermute | solution.py:232
  7.8 10.6 %collective-permute-start.1 = (bf16[2,24,2048]{2,1,0:T(8,128)(2,1)S(1)}, bf16[2,24,2048]{2,1,0:T(8,128)(2,1)S(1)}, u32[]{:S(2)}, u32[]{:S(2)}) collective-permute-start(bf16[2,24,2048]{2,1,0:T(8,128)(2,1)S(1)} %get-tuple-element.27), channel_id=1, source_target_pairs={{0,2},{1,3},{2,0},{3,1},{4,6},{5,7},{6,4},{7,5},{8,10},{9,11},{10,... | collective-permute-start | bytes 589832 | tf_op jit(solution)/shard_map/ppermute | solution.py:232
  9.3 9.1 %collective-permute-start.2 = (bf16[2,24,2048]{2,1,0:T(8,128)(2,1)S(1)}, bf16[2,24,2048]{2,1,0:T(8,128)(2,1)S(1)}, u32[]{:S(2)}, u32[]{:S(2)}) collective-permute-start(bf16[2,24,2048]{2,1,0:T(8,128)(2,1)S(1)} %get-tuple-element.28), channel_id=1, source_target_pairs={{0,3},{1,2},{2,1},{3,0},{4,7},{5,6},{6,5},{7,4},{8,11},{9,10},{10,... | collective-permute-start | bytes 589832 | tf_op jit(solution)/shard_map/ppermute | solution.py:232
  9.4 3.7 %copy-start = (bf16[2048,1,3,768]{3,0,2,1:T(8,128)(2,1)S(1)}, bf16[2048,1,3,768]{3,0,2,1:T(8,128)(2,1)}, u32[]{:S(2)}) copy-start(bf16[2048,1,3,768]{3,0,2,1:T(8,128)(2,1)} %param.9) | copy-start | bytes 28311556
  20.1 37.3 %collective-permute-start.13 = (bf16[96,2304]{1,0:T(8,128)(2,1)S(1)}, bf16[96,2304]{1,0:T(8,128)(2,1)S(1)}, u32[]{:S(2)}, u32[]{:S(2)}) collective-permute-start(bf16[96,2304]{1,0:T(8,128)(2,1)S(1)} %shard_map.86.acts_ref.refs_4_), channel_id=1, source_target_pairs={{0,16},{4,20},{8,24},{12,28},{16,0},{20,4},{24,8},{28,12},{1,17},{... | collective-permute-start | bytes 1327112 | tf_op jit(solution)/shard_map/ppermute | solution.py:240
  22.7 14.8 %collective-permute-start.6 = (bf16[4,24,1024]{2,1,0:T(8,128)(2,1)S(1)}, bf16[4,24,1024]{2,1,0:T(8,128)(2,1)S(1)}, u32[]{:S(2)}, u32[]{:S(2)}) collective-permute-start(bf16[4,24,1024]{2,1,0:T(8,128)(2,1)S(1)} %get-tuple-element.37), channel_id=1, source_target_pairs={{0,8},{4,12},{8,0},{12,4},{16,24},{20,28},{24,16},{28,20},{1,9},{5... | collective-permute-start | bytes 589832 | tf_op jit(solution)/shard_map/ppermute | solution.py:240
  24.3 30.8 %collective-permute-start.7 = (bf16[4,24,1024]{2,1,0:T(8,128)(2,1)S(1)}, bf16[4,24,1024]{2,1,0:T(8,128)(2,1)S(1)}, u32[]{:S(2)}, u32[]{:S(2)}) collective-permute-start(bf16[4,24,1024]{2,1,0:T(8,128)(2,1)S(1)} %get-tuple-element.38), channel_id=1, source_target_pairs={{0,16},{4,20},{8,24},{12,28},{16,0},{20,4},{24,8},{28,12},{1,17},{... | collective-permute-start | bytes 589832 | tf_op jit(solution)/shard_map/ppermute | solution.py:240
  24.6 30.5 %collective-permute-start.8 = (bf16[4,24,1024]{2,1,0:T(8,128)(2,1)S(1)}, bf16[4,24,1024]{2,1,0:T(8,128)(2,1)S(1)}, u32[]{:S(2)}, u32[]{:S(2)}) collective-permute-start(bf16[4,24,1024]{2,1,0:T(8,128)(2,1)S(1)} %get-tuple-element.39), channel_id=1, source_target_pairs={{0,24},{4,28},{8,16},{12,20},{16,8},{20,12},{24,0},{28,4},{1,25},{... | collective-permute-start | bytes 589832 | tf_op jit(solution)/shard_map/ppermute | solution.py:240
  27.1 40.9 %collective-permute-start.12 = (bf16[96,2304]{1,0:T(8,128)(2,1)S(1)}, bf16[96,2304]{1,0:T(8,128)(2,1)S(1)}, u32[]{:S(2)}, u32[]{:S(2)}) collective-permute-start(bf16[96,2304]{1,0:T(8,128)(2,1)S(1)} %shard_map.86.acts_ref.refs_4_), channel_id=1, source_target_pairs={{0,8},{4,12},{8,0},{12,4},{16,24},{20,28},{24,16},{28,20},{1,9},{5... | collective-permute-start | bytes 1327112 | tf_op jit(solution)/shard_map/ppermute | solution.py:240
  55.2 6.3 %collective-permute-start.9 = (bf16[4,24,1024]{2,1,0:T(8,128)(2,1)S(1)}, bf16[4,24,1024]{2,1,0:T(8,128)(2,1)S(1)}, u32[]{:S(2)}, u32[]{:S(2)}) collective-permute-start(bf16[4,24,1024]{2,1,0:T(8,128)(2,1)S(1)} %get-tuple-element.41), channel_id=1, source_target_pairs={{0,1},{1,0},{2,3},{3,2},{4,5},{5,4},{6,7},{7,6},{8,9},{9,8},{10,11... | collective-permute-start | bytes 589832 | tf_op jit(solution)/shard_map/ppermute | solution.py:232
  56.7 12.8 %collective-permute-start.14 = (bf16[96,2304]{1,0:T(8,128)(2,1)S(1)}, bf16[96,2304]{1,0:T(8,128)(2,1)S(1)}, u32[]{:S(2)}, u32[]{:S(2)}) collective-permute-start(bf16[96,2304]{1,0:T(8,128)(2,1)S(1)} %shard_map.86.acts_ref.refs_4_), channel_id=1, source_target_pairs={{8,16},{12,20},{16,8},{20,12},{9,17},{13,21},{17,9},{21,13},{10,18... | collective-permute-start | bytes 1327112 | tf_op jit(solution)/shard_map/ppermute | solution.py:240
  57.4 18.5 %collective-permute-start.15 = (bf16[96,2304]{1,0:T(8,128)(2,1)S(1)}, bf16[96,2304]{1,0:T(8,128)(2,1)S(1)}, u32[]{:S(2)}, u32[]{:S(2)}) collective-permute-start(bf16[96,2304]{1,0:T(8,128)(2,1)S(1)} %collective-permute-done.13.refs_6_), channel_id=1, source_target_pairs={{8,0},{12,4},{16,24},{20,28},{9,1},{13,5},{17,25},{21,29},{10,2},{... | collective-permute-start | bytes 1327112 | tf_op jit(solution)/shard_map/ppermute | solution.py:240
  58.7 7.5 %collective-permute-start.10 = (bf16[4,24,1024]{2,1,0:T(8,128)(2,1)S(1)}, bf16[4,24,1024]{2,1,0:T(8,128)(2,1)S(1)}, u32[]{:S(2)}, u32[]{:S(2)}) collective-permute-start(bf16[4,24,1024]{2,1,0:T(8,128)(2,1)S(1)} %get-tuple-element.42), channel_id=1, source_target_pairs={{0,2},{1,3},{2,0},{3,1},{4,6},{5,7},{6,4},{7,5},{8,10},{9,11},{10,... | collective-permute-start | bytes 589832 | tf_op jit(solution)/shard_map/ppermute | solution.py:232
  61.5 6.6 %collective-permute-start.11 = (bf16[4,24,1024]{2,1,0:T(8,128)(2,1)S(1)}, bf16[4,24,1024]{2,1,0:T(8,128)(2,1)S(1)}, u32[]{:S(2)}, u32[]{:S(2)}) collective-permute-start(bf16[4,24,1024]{2,1,0:T(8,128)(2,1)S(1)} %get-tuple-element.43), channel_id=1, source_target_pairs={{0,3},{1,2},{2,1},{3,0},{4,7},{5,6},{6,5},{7,4},{8,11},{9,10},{10,... | collective-permute-start | bytes 589832 | tf_op jit(solution)/shard_map/ppermute | solution.py:232
  76.7 14.9 %copy-start.2 = (bf16[128,2048]{1,0:T(8,128)(2,1)S(1)}, bf16[128,2048]{1,0:T(8,128)(2,1)}, u32[]{:S(2)}) copy-start(bf16[128,2048]{1,0:T(8,128)(2,1)} %cot_ref.1) | copy-start | bytes 1572868
  76.7 14.9 %copy-start.5 = (s32[128,8]{0,1:T(8,128)S(1)}, s32[128,8]{0,1:T(8,128)}, u32[]{:S(2)}) copy-start(s32[128,8]{0,1:T(8,128)} %param.6) | copy-start | bytes 12292
  76.7 14.9 %copy-start.7 = (f32[128,8]{0,1:T(8,128)S(1)}, f32[128,8]{0,1:T(8,128)}, u32[]{:S(2)}) copy-start(f32[128,8]{0,1:T(8,128)} %param.7) | copy-start | bytes 12292
  76.8 16.7 %collective-permute-start.16 = (bf16[256,2304]{1,0:T(8,128)(2,1)S(1)}, bf16[256,2304]{1,0:T(8,128)(2,1)S(1)}, u32[]{:S(2)}, u32[]{:S(2)}) collective-permute-start(bf16[256,2304]{1,0:T(8,128)(2,1)S(1)} %get-tuple-element.45), channel_id=1, source_target_pairs={{0,4},{4,0},{8,12},{12,8},{16,20},{20,16},{24,28},{28,24},{1,5},{5... | collective-permute-start | bytes 3538952 | tf_op jit(solution)/shard_map/ppermute | solution.py:315
  79.8 7.8 %collective-permute-start.3 = (bf16[2,24,2048]{2,1,0:T(8,128)(2,1)S(1)}, bf16[2,24,2048]{2,1,0:T(8,128)(2,1)S(1)}, u32[]{:S(2)}, u32[]{:S(2)}) collective-permute-start(bf16[2,24,2048]{2,1,0:T(8,128)(2,1)S(1)} %get-tuple-element.30), channel_id=1, source_target_pairs={{0,1},{1,0},{2,3},{3,2},{4,5},{5,4},{6,7},{7,6},{8,9},{9,8},{10,11... | collective-permute-start | bytes 589832 | tf_op jit(solution)/shard_map/ppermute | solution.py:232
  80.4 11.2 %collective-permute-start.4 = (bf16[2,24,2048]{2,1,0:T(8,128)(2,1)S(1)}, bf16[2,24,2048]{2,1,0:T(8,128)(2,1)S(1)}, u32[]{:S(2)}, u32[]{:S(2)}) collective-permute-start(bf16[2,24,2048]{2,1,0:T(8,128)(2,1)S(1)} %get-tuple-element.31), channel_id=1, source_target_pairs={{0,2},{1,3},{2,0},{3,1},{4,6},{5,7},{6,4},{7,5},{8,10},{9,11},{10,... | collective-permute-start | bytes 589832 | tf_op jit(solution)/shard_map/ppermute | solution.py:232
  81.0 10.7 %collective-permute-start.5 = (bf16[2,24,2048]{2,1,0:T(8,128)(2,1)S(1)}, bf16[2,24,2048]{2,1,0:T(8,128)(2,1)S(1)}, u32[]{:S(2)}, u32[]{:S(2)}) collective-permute-start(bf16[2,24,2048]{2,1,0:T(8,128)(2,1)S(1)} %get-tuple-element.32), channel_id=1, source_target_pairs={{0,3},{1,2},{2,1},{3,0},{4,7},{5,6},{6,5},{7,4},{8,11},{9,10},{10,... | collective-permute-start | bytes 589832 | tf_op jit(solution)/shard_map/ppermute | solution.py:232
where the time goes:
time: 94.9 us; the launch traced here: 94.6 us
  waiting for transfers between devices  54.6 us (58%)
  starting transfers between devices  20.9 us (22%)
  Pallas kernels  11.2 us (12%)
  local copies, waits for them, and re-layouts  7.15 us (8%)
    ppermute x7, waiting for transfers between devices, swap_z(): return lax.ppermute(block, 'dp', pairs)  33.7 us
    ppermute x9, waiting for transfers between devices, swap_expert(): moved[m] = lax.ppermute(blocks[m], 'expert', pairs)  20.9 us
    pallas_call x9, Pallas kernels, local_call(): pl.pallas_call(body, out_shape=outs, in_specs=[space] * len(args), out_sp...  11.2 us
    ppermute x9, starting transfers between devices, swap_expert(): moved[m] = lax.ppermute(blocks[m], 'expert', pairs)  11.2 us
    ppermute x7, starting transfers between devices, swap_z(): return lax.ppermute(block, 'dp', pairs)  9.69 us
    unnamed x16, local copies, waits for them, and re-layouts  7.15 us
  transfers between devices with their start and end apart: 17, of which 9 were waited for; matrix products, arithmetic and copies ran while one was open for 0% of the time, Pallas kernels for 7%

commit v1 on v0

--- a/solution.py
+++ b/solution.py
@@ -9,6 +9,8 @@
 
 CAP = 24
 CORES = 2
+PIECES = 2
+SEND_MB = 24
 F32 = jnp.float32
 BF16 = jnp.bfloat16
 VMEM = pl.BlockSpec(memory_space=pltpu.VMEM)
@@ -23,7 +25,7 @@
 
 def local_call(body, outs, args, flops, scratch=(), megabytes=24, space=VMEM):
     moved = sum(a.size * a.dtype.itemsize for a in list(args) + list(outs))
-    return pl.pallas_call(
+    call = pl.pallas_call(
         body,
         out_shape=outs,
         in_specs=[space] * len(args),
@@ -33,7 +35,10 @@
         cost_estimate=pl.CostEstimate(
             flops=int(flops), bytes_accessed=int(moved), transcendentals=0
         ),
-    )(*args)
+    )
+    if space is HBM:
+        args = [pltpu.with_memory_space_constraint(a, pltpu.HBM) for a in args]
+    return call(*args)
 
 
 def slot_map(ids, probs, me, experts):
@@ -112,24 +117,42 @@
     return jnp.concatenate([b.astype(F32) for b in blocks], axis=0).astype(BF16)
 
 
-def ffn_kernel(experts, w_ref, *refs):
-    blocks, out_ref = refs[:experts], refs[experts]
+def put_columns(outs, cuts, lo, value):
+    hi = lo + value.shape[1]
+    for out, (at, end) in zip(outs, cuts):
+        a, b = max(at, lo), min(end, hi)
+        if a < b:
+            out[:, a - at : b - at] = value[:, a - lo : b - lo]
+
+
+def get_columns(refs, cuts, lo, hi):
+    parts = []
+    for ref, (at, end) in zip(refs, cuts):
+        a, b = max(at, lo), min(end, hi)
+        if a < b:
+            parts.append(ref[:, a - at : b - at])
+    return parts[0] if len(parts) == 1 else jnp.concatenate(parts, axis=1)
+
+
+def ffn_kernel(experts, cuts, w_ref, *refs):
+    blocks, outs = refs[:experts], refs[experts:]
     hidden = w_ref.shape[2]
     x = stack_rows([b[0] for b in blocks])
     dy = stack_rows([b[1] for b in blocks])
     gate = jnp.dot(x, w_ref[0], preferred_element_type=F32)
     up = jnp.dot(x, w_ref[1], preferred_element_type=F32)
     s = jax.nn.sigmoid(gate)
-    out_ref[:, 0:hidden] = (gate * s * up).astype(BF16)
+    put_columns(outs, cuts, 0, (gate * s * up).astype(BF16))
     grad = jnp.dot(dy, w_ref[2], preferred_element_type=F32)
-    out_ref[:, hidden : 2 * hidden] = (grad * up * s * (1.0 + gate * (1.0 - s))).astype(BF16)
-    out_ref[:, 2 * hidden :] = (grad * (gate * s)).astype(BF16)
-
-
-def output_kernel(experts, w_ref, acts_ref, *outs):
+    gate_grad = grad * up * s * (1.0 + gate * (1.0 - s))
+    put_columns(outs, cuts, hidden, gate_grad.astype(BF16))
+    put_columns(outs, cuts, 2 * hidden, (grad * (gate * s)).astype(BF16))
+
+
+def output_kernel(experts, cuts, w_ref, *refs):
+    acts, outs = refs[: len(cuts)], refs[len(cuts) :]
     hidden = w_ref.shape[2]
-    hid, gg = acts_ref[:, 0:hidden], acts_ref[:, hidden : 2 * hidden]
-    ug = acts_ref[:, 2 * hidden :]
+    hid, gg, ug = (get_columns(acts, cuts, j * hidden, (j + 1) * hidden) for j in range(3))
     out = lax.dot_general(hid, w_ref[2], NT, preferred_element_type=F32)
     part = lax.dot_general(gg, w_ref[0], NT, preferred_element_type=F32)
     part += lax.dot_general(ug, w_ref[1], NT, preferred_element_type=F32)
@@ -170,48 +193,54 @@
             refs[zs + k][m] = refs[m][k]
 
 
-def grad_sums(feats, acts, at):
-    rows_f = stack_rows([f[m] for m in at for f in feats])
-    rows_a = acts[0]
-    for more in acts[1:]:
-        rows_a = jnp.concatenate([rows_a, more], axis=0)
+def grad_sums(feats, chips, picks, refs, cut):
+    lo, hi, hidden = cut
+    rows_f = stack_rows([f[m] for m in chips for f in feats])
+    acts = []
+    for n in picks:
+        value = refs[0][...]
+        for more in refs[1:n]:
+            value += more[...]
+        acts.append(value)
+        refs = refs[n:]
+    rows_a = acts[0] if len(acts) == 1 else jnp.concatenate(acts, axis=0)
     half = rows_f.shape[1] // 2
-    hidden = rows_a.shape[1] // 3
-    both = lax.dot_general(
-        rows_f[:, :half], rows_a[:, hidden:], TN, preferred_element_type=F32
-    )
-    down = lax.dot_general(
-        rows_f[:, half:], rows_a[:, :hidden], TN, preferred_element_type=F32
-    )
-    return both, down
-
-
-def early_grad_kernel(experts, at, *refs):
+    sums = []
+    split = min(max(hidden - lo, 0), hi - lo)
+    if split > 0:
+        sums.append(
+            lax.dot_general(rows_f[:, half:], rows_a[:, :split], TN, preferred_element_type=F32)
+        )
+    if split < hi - lo:
+        sums.append(
+            lax.dot_general(rows_f[:, :half], rows_a[:, split:], TN, preferred_element_type=F32)
+        )
+    return sums[0] if len(sums) == 1 else jnp.concatenate(sums, axis=1)
+
+
+def early_grad_kernel(experts, chips, picks, cut, *refs):
     feats, acts, total = refs[:experts], refs[experts:-1], refs[-1]
-    both, down = grad_sums(feats, [a[...] for a in acts], at)
-    total[:, : both.shape[1]] = both
-    total[:, both.shape[1] :] = down
-
-
-def late_grad_kernel(experts, at, *refs):
+    total[...] = grad_sums(feats, chips, picks, acts, cut)
+
+
+def late_grad_kernel(experts, chips, picks, cut, *refs):
     feats, (total, *acts), (own, send) = refs[:experts], refs[experts:-2], refs[-2:]
-    last = acts[0][...].astype(F32)
-    for more in acts[1:]:
-        last += more[...].astype(F32)
-    both, down = grad_sums(feats, [last.astype(BF16)], at)
-    half = both.shape[0] // CORES
-    n = both.shape[1]
-    own[:, :n] = total[:half, :n] + both[:half]
-    own[:, n:] = total[:half, n:] + down[:half]
-    send[:, :n] = (total[half:, :n] + both[half:]).astype(BF16)
-    send[:, n:] = (total[half:, n:] + down[half:]).astype(BF16)
-
-
-def final_kernel(own, got, out):
+    more = grad_sums(feats, chips, picks, acts, cut)
+    half = more.shape[0] // CORES
+    own[...] = total[:half] + more[:half]
+    send[...] = (total[half:] + more[half:]).astype(BF16)
+
+
+def final_kernel(cuts, *refs):
+    n = len(cuts)
+    owns, gots, out = refs[:n], refs[n : 2 * n], refs[-1]
     hidden = out.shape[2]
-    for j in range(3):
-        at = slice(j * hidden, (j + 1) * hidden)
-        out[j] = (own[:, at] + got[:, at].astype(F32)).astype(BF16)
+    for k, (lo, hi) in enumerate(cuts):
+        value = (owns[k][...] + gots[k][...].astype(F32)).astype(BF16)
+        for j in range(3):
+            a, b = max(lo, j * hidden), min(hi, (j + 1) * hidden)
+            if a < b:
+                out[(j + 2) % 3, :, a - j * hidden : b - j * hidden] = value[:, a - lo : b - lo]
 
 
 def per_device(tokens, expert_ids, gate_probs, cotangent, expert_weights):
@@ -242,11 +271,12 @@
     def spread_z(block):
         if zs != 4:
             return [[swap_z(block, m)] for m in range(1, zs)]
-        far = swap_z(block, 2)
         near = swap_z(block, 1)
         middle = swap_z(block, 3, (1, 2))
-        ends = swap_z(far, 1, (1, 2))
-        return [[near], [far], [middle, ends]]
+        through = swap_z(near, 3, (1, 2))
+        ends = swap_z(middle, 1, (1, 2))
+        last = swap_z(through, 1, (1, 2))
+        return [[near], [through, ends], [middle, last]]
 
     sent = local_call(
         functools.partial(send_kernel, experts, zs),
@@ -257,6 +287,7 @@
         + [pltpu.VMEM(a.shape, a.dtype) for a in (ids, probs, tokens, cotangent)]
         + [pltpu.SemaphoreType.DMA((4,))],
         space=HBM,
+        megabytes=SEND_MB,
     )
     (staged,) = local_call(
         stage_kernel,
@@ -269,17 +300,19 @@
     blocks = swap_expert(sent[:experts])
     shares = [sent[experts]] + [swap_z(sent[experts + m], m) for m in range(1, zs)]
 
-    (acts,) = local_call(
-        functools.partial(ffn_kernel, experts),
-        [shape_of((rows, 3 * hidden))],
+    step = 3 * hidden // PIECES
+    cuts = [(k * step, (k + 1) * step) for k in range(PIECES)]
+    acts = local_call(
+        functools.partial(ffn_kernel, experts, cuts),
+        [shape_of((rows, step))] * PIECES,
         [staged, *blocks],
         6 * rows * width * hidden,
     )
-    near_far = spread_z(acts)
+    spread = [spread_z(block) for block in acts]
     results = local_call(
-        functools.partial(output_kernel, experts),
+        functools.partial(output_kernel, experts, cuts),
         [shape_of((2, CAP, width))] * experts,
-        [staged, acts],
+        [staged, *acts],
         6 * rows * width * hidden,
     )
     back = swap_expert(results)
@@ -296,27 +329,34 @@
         [ids, probs, cotangent, *back],
         8 * rows * tok_rows * width,
     )
-    early = near_far[:-1]
-    (total,) = local_call(
-        functools.partial(early_grad_kernel, experts, tuple(range(zs - 1))),
-        [shape_of((chip_width, 3 * hidden), F32)],
-        [*feats, acts, *[a for piece in early for a in piece]],
-        6 * (zs - 1) * rows * chip_width * hidden,
-    )
-    own, send = local_call(
-        functools.partial(late_grad_kernel, experts, (zs - 1,)),
-        [
-            shape_of((chip_width // CORES, 3 * hidden), F32),
-            shape_of((chip_width // CORES, 3 * hidden)),
-        ],
-        [*feats, total, *near_far[-1]],
-        6 * rows * chip_width * hidden,
-    )
-    got = lax.ppermute(send, "dp", [(i, i ^ 1) for i in range(groups)])
+    owns, gots = [], []
+    for k in range(PIECES):
+        cut = (*cuts[k], hidden)
+        pieces = [[acts[k]]] + spread[k][:-1]
+        (total,) = local_call(
+            functools.partial(
+                early_grad_kernel, experts, tuple(range(zs - 1)), tuple(map(len, pieces)), cut
+            ),
+            [shape_of((chip_width, step), F32)],
+            [*feats, *[a for piece in pieces for a in piece]],
+            2 * (zs - 1) * rows * chip_width * step,
+        )
+        pieces = spread[k][-1]
+        own, send = local_call(
+            functools.partial(late_grad_kernel, experts, (zs - 1,), (len(pieces),), cut),
+            [
+                shape_of((chip_width // CORES, step), F32),
+                shape_of((chip_width // CORES, step)),
+            ],
+            [*feats, total, *pieces],
+            2 * rows * chip_width * step,
+        )
+        gots.append(lax.ppermute(send, "dp", [(i, i ^ 1) for i in range(groups)]))
+        owns.append(own)
     (grads,) = local_call(
-        final_kernel,
+        functools.partial(final_kernel, cuts),
         [shape_of((3, width // groups, hidden))],
-        [own, got],
+        [*owns, *gots],
         3 * width * hidden // groups,
     )
     grad_weights = jnp.transpose(grads, (1, 0, 2))[:, None]

time: 94.9 us -> 80.3 us (0.85)
  waiting for transfers between devices: 54.6 us -> 30.4 us
  starting transfers between devices: 20.9 us -> 32.7 us
  local copies, waits for them, and re-layouts: 7.15 us -> 0.02 us
  Pallas kernels: 11.2 us -> 16 us
    ppermute x7 -> x13, waiting for transfers between devices: 33.7 us -> 20.3 us  [swap_z(): return lax.ppermute(block, 'dp', pairs)]
    ppermute x9, waiting for transfers between devices: 20.9 us -> 10.1 us  [swap_expert(): moved[m] = lax.ppermute(blocks[m], 'expert', pairs)]
    ppermute x7 -> x13, starting transfers between devices: 9.69 us -> 18.9 us  [swap_z(): return lax.ppermute(block, 'dp', pairs)]
    unnamed x16 -> x6, local copies, waits for them, and re-layouts: 7.15 us -> 0.02 us
    pallas_call x9 -> x11, Pallas kernels: 11.2 us -> 16 us  [local_call(): return call(*args)]
    ppermute x9, starting transfers between devices: 11.2 us -> 13.7 us  [swap_expert(): moved[m] = lax.ppermute(blocks[m], 'expert', pairs)]
  transfers between devices with their start and end apart: 17 -> 24, of which waited for: 9 -> 11; matrix products, arithmetic and copies ran while one was open for 0% -> 0% of each run, Pallas kernels for 7% -> 16%
where the time goes in v1:
time: 80.3 us; the launch traced here: 80 us
  starting transfers between devices  32.7 us (41%)
  waiting for transfers between devices  30.4 us (38%)
  Pallas kernels  16 us (20%)
  between operations  0.88 us (1%)
    ppermute x13, waiting for transfers between devices, swap_z(): return lax.ppermute(block, 'dp', pairs)  20.3 us
    ppermute x13, starting transfers between devices, swap_z(): return lax.ppermute(block, 'dp', pairs)  18.9 us
    pallas_call x11, Pallas kernels, local_call(): return call(*args)  16 us
    ppermute x9, starting transfers between devices, swap_expert(): moved[m] = lax.ppermute(blocks[m], 'expert', pairs)  13.7 us
    ppermute x9, waiting for transfers between devices, swap_expert(): moved[m] = lax.ppermute(blocks[m], 'expert', pairs)  10.1 us
  transfers between devices with their start and end apart: 24, of which 11 were waited for; matrix products, arithmetic and copies ran while one was open for 0% of the time, Pallas kernels for 16%

profile of v1, /device:TPU:0, one launch (start us, length us, event | category | flops | bytes accessed | tf_op | source)
XLA Modules:
  0.0 80.0 jit_solution(11647942585476492876)
XLA Ops:
  0.6 1.8 %shard_map.85 = (bf16[2,24,2048]{2,1,0:T(8,128)(2,1)S(1)}, bf16[2,24,2048]{2,1,0:T(8,128)(2,1)S(1)}, bf16[2,24,2048]{2,1,0:T(8,128)(2,1)S(1)}, bf16[2,24,2048]{2...) custom-call(s32[8,128]{1,0:T(8,128)} %bitcast.9, ...), custom_call_target="tpu_custom_call" | custom-call | flops 100663296 | bytes 2629632 | tf_op jit(solution)/shard_map/pallas_call | solution.py:41
  2.5 3.0 %collective-permute-start = (bf16[2,24,2048]{2,1,0:T(8,128)(2,1)S(1)}, bf16[2,24,2048]{2,1,0:T(8,128)(2,1)S(1)}, u32[]{:S(2)}, u32[]{:S(2)}) collective-permute-start(bf16[2,24,2048]{2,1,0:T(8,128)(2,1)S(1)} %get-tuple-element.30), channel_id=1, source_target_pairs={{0,1},{1,0},{2,3},{3,2},{4,5},{5,4},{6,7},{7,6},{8,9},{9,8},{10,11... | collective-permute-start | bytes 589832 | tf_op jit(solution)/shard_map/ppermute | solution.py:261
  5.5 1.5 %collective-permute-start.1 = (bf16[2,24,2048]{2,1,0:T(8,128)(2,1)S(1)}, bf16[2,24,2048]{2,1,0:T(8,128)(2,1)S(1)}, u32[]{:S(2)}, u32[]{:S(2)}) collective-permute-start(bf16[2,24,2048]{2,1,0:T(8,128)(2,1)S(1)} %get-tuple-element.31), channel_id=1, source_target_pairs={{0,2},{1,3},{2,0},{3,1},{4,6},{5,7},{6,4},{7,5},{8,10},{9,11},{10,... | collective-permute-start | bytes 589832 | tf_op jit(solution)/shard_map/ppermute | solution.py:261
  7.0 0.0 collective-permute-start.2
  7.0 2.0 %collective-permute-start.6 = (bf16[4,24,1024]{2,1,0:T(8,128)(2,1)S(1)}, bf16[4,24,1024]{2,1,0:T(8,128)(2,1)S(1)}, u32[]{:S(2)}, u32[]{:S(2)}) collective-permute-start(bf16[4,24,1024]{2,1,0:T(8,128)(2,1)S(1)} %get-tuple-element.43), channel_id=1, source_target_pairs={{0,8},{4,12},{8,0},{12,4},{16,24},{20,28},{24,16},{28,20},{1,9},{5... | collective-permute-start | bytes 589832 | tf_op jit(solution)/shard_map/ppermute | solution.py:269
  9.1 2.6 %collective-permute-start.7 = (bf16[4,24,1024]{2,1,0:T(8,128)(2,1)S(1)}, bf16[4,24,1024]{2,1,0:T(8,128)(2,1)S(1)}, u32[]{:S(2)}, u32[]{:S(2)}) collective-permute-start(bf16[4,24,1024]{2,1,0:T(8,128)(2,1)S(1)} %get-tuple-element.44), channel_id=1, source_target_pairs={{0,16},{4,20},{8,24},{12,28},{16,0},{20,4},{24,8},{28,12},{1,17},{... | collective-permute-start | bytes 589832 | tf_op jit(solution)/shard_map/ppermute | solution.py:269
  11.7 0.0 collective-permute-done.refs_1_
  11.7 3.7 %collective-permute-start.8 = (bf16[4,24,1024]{2,1,0:T(8,128)(2,1)S(1)}, bf16[4,24,1024]{2,1,0:T(8,128)(2,1)S(1)}, u32[]{:S(2)}, u32[]{:S(2)}) collective-permute-start(bf16[4,24,1024]{2,1,0:T(8,128)(2,1)S(1)} %get-tuple-element.45), channel_id=1, source_target_pairs={{0,24},{4,28},{8,16},{12,20},{16,8},{20,12},{24,0},{28,4},{1,25},{... | collective-permute-start | bytes 589832 | tf_op jit(solution)/shard_map/ppermute | solution.py:269
  15.4 3.8 %shard_map.84.w_ref = bf16[3,2048,768]{2,1,0:T(8,128)(2,1)S(1)} custom-call(bf16[3,2048,768]{2,1,0:T(8,128)(2,1)} %bitcast.13), custom_call_target="tpu_custom_call" | custom-call | bytes 18874368 | tf_op jit(solution)/shard_map/pallas_call | solution.py:41
  19.2 0.0 collective-permute-done.1.refs_2_
  19.2 0.0 collective-permute-done.2.refs_3_
  19.2 1.7 %shard_map.86 = (bf16[96,1152]{1,0:T(8,128)(2,1)S(1)}, bf16[96,1152]{1,0:T(8,128)(2,1)S(1)}) custom-call(bf16[3,2048,768]{2,1,0:T(8,128)(2,1)S(1)} %shard_map.84.w_ref, bf16[2,24,2048]{2,1,0:T(8,128)(2,1)S(1)} %get-tuple-element.29.refs_0_, bf16[2,24,2048]{2,1,0:T(8,128)(2,1)S(1)} %collective-permute-done.refs_1_, ...), custom_call_target="tpu_custom_call" | custom-call | flops 905969664 | bytes 10665984 | tf_op jit(solution)/shard_map/pallas_call | solution.py:41
  20.9 0.1 collective-permute-start.17
  21.0 0.0 collective-permute-done.6.refs_1_
  21.0 5.1 %collective-permute-done.7.refs_2_ = bf16[4,24,1024]{2,1,0:T(8,128)(2,1)S(1)} collective-permute-done((bf16[4,24,1024]{2,1,0:T(8,128)(2,1)S(1)}, bf16[4,24,1024]{2,1,0:T(8,128)(2,1)S(1)}, u32[]{:S(2)}, u32[]{:S(2)}) %collective-permute-start.7) | collective-permute-done | bytes 196640 | tf_op jit(solution)/shard_map/ppermute | solution.py:269
  26.1 0.0 collective-permute-done.8.refs_3_
  26.1 0.1 shard_map.89
  26.1 1.6 %collective-permute-start.9 = (bf16[4,24,1024]{2,1,0:T(8,128)(2,1)S(1)}, bf16[4,24,1024]{2,1,0:T(8,128)(2,1)S(1)}, u32[]{:S(2)}, u32[]{:S(2)}) collective-permute-start(bf16[4,24,1024]{2,1,0:T(8,128)(2,1)S(1)} %get-tuple-element.47), channel_id=1, source_target_pairs={{0,1},{1,0},{2,3},{3,2},{4,5},{5,4},{6,7},{7,6},{8,9},{9,8},{10,11... | collective-permute-start | bytes 589832 | tf_op jit(solution)/shard_map/ppermute | solution.py:261
  27.7 2.7 %collective-permute-start.12 = (bf16[96,1152]{1,0:T(8,128)(2,1)S(1)}, bf16[96,1152]{1,0:T(8,128)(2,1)S(1)}, u32[]{:S(2)}, u32[]{:S(2)}) collective-permute-start(bf16[96,1152]{1,0:T(8,128)(2,1)S(1)} %get-tuple-element.33.refs_0_.refs_4_), channel_id=1, source_target_pairs={{0,8},{4,12},{8,0},{12,4},{16,24},{20,28},{24,16},{28,20},{1,9},{5... | collective-permute-start | bytes 663560 | tf_op jit(solution)/shard_map/ppermute | solution.py:269
  30.4 0.7 collective-permute-start.19
  31.0 0.7 collective-permute-start.14
  31.7 0.2 collective-permute-done.9.refs_1_
  31.9 1.5 %collective-permute-start.10 = (bf16[4,24,1024]{2,1,0:T(8,128)(2,1)S(1)}, bf16[4,24,1024]{2,1,0:T(8,128)(2,1)S(1)}, u32[]{:S(2)}, u32[]{:S(2)}) collective-permute-start(bf16[4,24,1024]{2,1,0:T(8,128)(2,1)S(1)} %get-tuple-element.48), channel_id=1, source_target_pairs={{0,2},{1,3},{2,0},{3,1},{4,6},{5,7},{6,4},{7,5},{8,10},{9,11},{10,... | collective-permute-start | bytes 589832 | tf_op jit(solution)/shard_map/ppermute | solution.py:261
  33.4 0.0 collective-permute-done.17.refs_5_
  33.4 0.7 collective-permute-start.18
  34.1 0.2 collective-permute-done.12.refs_5_
  34.3 0.7 collective-permute-start.13
  34.9 0.0 collective-permute-done.19.refs_5_
  35.0 1.3 %collective-permute-start.20 = (bf16[96,1152]{1,0:T(8,128)(2,1)S(1)}, bf16[96,1152]{1,0:T(8,128)(2,1)S(1)}, u32[]{:S(2)}, u32[]{:S(2)}) collective-permute-start(bf16[96,1152]{1,0:T(8,128)(2,1)S(1)} %collective-permute-done.19.refs_5_), channel_id=1, source_target_pairs={{8,0},{12,4},{16,24},{20,28},{9,1},{13,5},{17,25},{21,29},{10,2},{... | collective-permute-start | bytes 663560 | tf_op jit(solution)/shard_map/ppermute | solution.py:269
  36.3 1.3 %collective-permute-done.10.refs_2_ = bf16[4,24,1024]{2,1,0:T(8,128)(2,1)S(1)} collective-permute-done((bf16[4,24,1024]{2,1,0:T(8,128)(2,1)S(1)}, bf16[4,24,1024]{2,1,0:T(8,128)(2,1)S(1)}, u32[]{:S(2)}, u32[]{:S(2)}) %collective-permute-start.10) | collective-permute-done | bytes 196640 | tf_op jit(solution)/shard_map/ppermute | solution.py:261
  37.5 2.5 %collective-permute-start.11 = (bf16[4,24,1024]{2,1,0:T(8,128)(2,1)S(1)}, bf16[4,24,1024]{2,1,0:T(8,128)(2,1)S(1)}, u32[]{:S(2)}, u32[]{:S(2)}) collective-permute-start(bf16[4,24,1024]{2,1,0:T(8,128)(2,1)S(1)} %get-tuple-element.49), channel_id=1, source_target_pairs={{0,3},{1,2},{2,1},{3,0},{4,7},{5,6},{6,5},{7,4},{8,11},{9,10},{10,... | collective-permute-start | bytes 589832 | tf_op jit(solution)/shard_map/ppermute | solution.py:261
  40.0 0.0 collective-permute-done.14.refs_5_
  40.0 1.3 %collective-permute-start.15 = (bf16[96,1152]{1,0:T(8,128)(2,1)S(1)}, bf16[96,1152]{1,0:T(8,128)(2,1)S(1)}, u32[]{:S(2)}, u32[]{:S(2)}) collective-permute-start(bf16[96,1152]{1,0:T(8,128)(2,1)S(1)} %collective-permute-done.14.refs_5_), channel_id=1, source_target_pairs={{8,0},{12,4},{16,24},{20,28},{9,1},{13,5},{17,25},{21,29},{10,2},{... | collective-permute-start | bytes 663560 | tf_op jit(solution)/shard_map/ppermute | solution.py:269
  41.3 0.0 collective-permute-done.18.refs_6_
  41.3 1.3 %collective-permute-start.21 = (bf16[96,1152]{1,0:T(8,128)(2,1)S(1)}, bf16[96,1152]{1,0:T(8,128)(2,1)S(1)}, u32[]{:S(2)}, u32[]{:S(2)}) collective-permute-start(bf16[96,1152]{1,0:T(8,128)(2,1)S(1)} %collective-permute-done.18.refs_6_), channel_id=1, source_target_pairs={{8,0},{12,4},{16,24},{20,28},{9,1},{13,5},{17,25},{21,29},{10,2},{... | collective-permute-start | bytes 663560 | tf_op jit(solution)/shard_map/ppermute | solution.py:269
  42.6 0.0 collective-permute-done.13.refs_6_
  42.6 1.3 %collective-permute-start.16 = (bf16[96,1152]{1,0:T(8,128)(2,1)S(1)}, bf16[96,1152]{1,0:T(8,128)(2,1)S(1)}, u32[]{:S(2)}, u32[]{:S(2)}) collective-permute-start(bf16[96,1152]{1,0:T(8,128)(2,1)S(1)} %collective-permute-done.13.refs_6_), channel_id=1, source_target_pairs={{8,0},{12,4},{16,24},{20,28},{9,1},{13,5},{17,25},{21,29},{10,2},{... | collective-permute-start | bytes 663560 | tf_op jit(solution)/shard_map/ppermute | solution.py:269
  43.9 0.2 collective-permute-done.11.refs_3_
  44.1 7.1 %collective-permute-done.20.refs_7_ = bf16[96,1152]{1,0:T(8,128)(2,1)S(1)} collective-permute-done((bf16[96,1152]{1,0:T(8,128)(2,1)S(1)}, bf16[96,1152]{1,0:T(8,128)(2,1)S(1)}, u32[]{:S(2)}, u32[]{:S(2)}) %collective-permute-start.20) | collective-permute-done | bytes 221216 | tf_op jit(solution)/shard_map/ppermute | solution.py:269
  51.2 0.9 %shard_map.92.refs_4_ = f32[512,1152]{1,0:T(8,128)S(1)} custom-call(bf16[4,24,1024]{2,1,0:T(8,128)(2,1)S(1)} %get-tuple-element.46.refs_0_, bf16[4,24,1024]{2,1,0:T(8,128)(2,1)S(1)} %collective-permute-done.9.refs_1_, bf16[4,24,1024]{2,1,0:T(8,128)(2,1)S(1)} %collective-permute-done.10.refs_2_, bf16[4,24,1024]{2,1,0:T(8,128)(2,1)S(1)} %collective-permute-done.11.refs_3_, ...), custom_call_target="tpu_custom_call" | custom-call | flops 339738624 | bytes 4030464 | tf_op jit(solution)/shard_map/pallas_call | solution.py:41
  52.1 3.9 %collective-permute-done.15.refs_7_ = bf16[96,1152]{1,0:T(8,128)(2,1)S(1)} collective-permute-done((bf16[96,1152]{1,0:T(8,128)(2,1)S(1)}, bf16[96,1152]{1,0:T(8,128)(2,1)S(1)}, u32[]{:S(2)}, u32[]{:S(2)}) %collective-permute-start.15) | collective-permute-done | bytes 221216 | tf_op jit(solution)/shard_map/ppermute | solution.py:269
  55.9 0.9 %shard_map.90.refs_4_ = f32[512,1152]{1,0:T(8,128)S(1)} custom-call(bf16[4,24,1024]{2,1,0:T(8,128)(2,1)S(1)} %get-tuple-element.46.refs_0_, bf16[4,24,1024]{2,1,0:T(8,128)(2,1)S(1)} %collective-permute-done.9.refs_1_, bf16[4,24,1024]{2,1,0:T(8,128)(2,1)S(1)} %collective-permute-done.10.refs_2_, bf16[4,24,1024]{2,1,0:T(8,128)(2,1)S(1)} %collective-permute-done.11.refs_3_, ...), custom_call_target="tpu_custom_call" | custom-call | flops 339738624 | bytes 4030464 | tf_op jit(solution)/shard_map/pallas_call | solution.py:41
  56.8 2.3 %collective-permute-done.21.refs_6_ = bf16[96,1152]{1,0:T(8,128)(2,1)S(1)} collective-permute-done((bf16[96,1152]{1,0:T(8,128)(2,1)S(1)}, bf16[96,1152]{1,0:T(8,128)(2,1)S(1)}, u32[]{:S(2)}, u32[]{:S(2)}) %collective-permute-start.21) | collective-permute-done | bytes 221216 | tf_op jit(solution)/shard_map/ppermute | solution.py:269
  59.1 0.5 shard_map.93
  59.6 0.1 collective-permute-start.23
  59.7 1.8 %collective-permute-done.16.refs_6_ = bf16[96,1152]{1,0:T(8,128)(2,1)S(1)} collective-permute-done((bf16[96,1152]{1,0:T(8,128)(2,1)S(1)}, bf16[96,1152]{1,0:T(8,128)(2,1)S(1)}, u32[]{:S(2)}, u32[]{:S(2)}) %collective-permute-start.16) | collective-permute-done | bytes 221216 | tf_op jit(solution)/shard_map/ppermute | solution.py:269
  61.5 0.5 shard_map.91
  62.0 0.0 copy-start
  62.0 0.0 copy-start.1
  62.0 0.0 copy-start.2
  62.0 0.1 collective-permute-start.22
  62.1 3.0 %shard_map.87 = (bf16[2,24,2048]{2,1,0:T(8,128)(2,1)S(1)}, bf16[2,24,2048]{2,1,0:T(8,128)(2,1)S(1)}, bf16[2,24,2048]{2,1,0:T(8,128)(2,1)S(1)}, bf16[2,24,2048]{2,1,0:T(8,128)(2,1)S(1)}) custom-call(bf16[3,2048,768]{2,1,0:T(8,128)(2,1)S(1)} %shard_map.84.w_ref, bf16[96,1152]{1,0:T(8,128)(2,1)S(1)} %get-tuple-element.33.refs_0_.refs_4_, ...), custom_call_target="tpu_custom_call" | custom-call | flops 905969664 | bytes 10665984 | tf_op jit(solution)/shard_map/pallas_call | solution.py:41
  65.0 0.8 collective-permute-start.3
  65.8 1.5 %collective-permute-start.4 = (bf16[2,24,2048]{2,1,0:T(8,128)(2,1)S(1)}, bf16[2,24,2048]{2,1,0:T(8,128)(2,1)S(1)}, u32[]{:S(2)}, u32[]{:S(2)}) collective-permute-start(bf16[2,24,2048]{2,1,0:T(8,128)(2,1)S(1)} %get-tuple-element.37), channel_id=1, source_target_pairs={{0,2},{1,3},{2,0},{3,1},{4,6},{5,7},{6,4},{7,5},{8,10},{9,11},{10,... | collective-permute-start | bytes 589832 | tf_op jit(solution)/shard_map/ppermute | solution.py:261
  67.3 1.3 %collective-permute-start.5 = (bf16[2,24,2048]{2,1,0:T(8,128)(2,1)S(1)}, bf16[2,24,2048]{2,1,0:T(8,128)(2,1)S(1)}, u32[]{:S(2)}, u32[]{:S(2)}) collective-permute-start(bf16[2,24,2048]{2,1,0:T(8,128)(2,1)S(1)} %get-tuple-element.38), channel_id=1, source_target_pairs={{0,3},{1,2},{2,1},{3,0},{4,7},{5,6},{6,5},{7,4},{8,11},{9,10},{10,... | collective-permute-start | bytes 589832 | tf_op jit(solution)/shard_map/ppermute | solution.py:261
  68.6 4.3 %collective-permute-done.3.refs_1_ = bf16[2,24,2048]{2,1,0:T(8,128)(2,1)S(1)} collective-permute-done((bf16[2,24,2048]{2,1,0:T(8,128)(2,1)S(1)}, bf16[2,24,2048]{2,1,0:T(8,128)(2,1)S(1)}, u32[]{:S(2)}, u32[]{:S(2)}) %collective-permute-start.3) | collective-permute-done | bytes 196640 | tf_op jit(solution)/shard_map/ppermute | solution.py:261
  72.9 4.2 %collective-permute-done.4.refs_2_ = bf16[2,24,2048]{2,1,0:T(8,128)(2,1)S(1)} collective-permute-done((bf16[2,24,2048]{2,1,0:T(8,128)(2,1)S(1)}, bf16[2,24,2048]{2,1,0:T(8,128)(2,1)S(1)}, u32[]{:S(2)}, u32[]{:S(2)}) %collective-permute-start.4) | collective-permute-done | bytes 196640 | tf_op jit(solution)/shard_map/ppermute | solution.py:261
  77.0 0.0 collective-permute-done.5.refs_3_
  77.0 0.0 copy-done
  77.0 0.0 copy-done.1
  77.1 1.7 %shard_map.88 = (bf16[128,2048]{1,0:T(8,128)(2,1)}, bf16[128,2048]{1,0:T(8,128)(2,1)}, f32[8,128]{1,0:T(8,128)}) custom-call(s32[8,128]{1,0:T(8,128)S(1)} %bitcast.10, f32[8,128]{1,0:T(8,128)S(1)} %bitcast.12, bf16[128,2048]{1,0:T(8,128)(2,1)S(1)} %copy-done, bf16[2,24,2048]{2,1,0:T(8,128)(2,1)S(1)} %get-tuple-element.35.refs_0_, ...), custom_call_target="tpu_custom_call" | custom-call | flops 201326592 | bytes 2371584 | tf_op jit(solution)/shard_map/pallas_call | solution.py:41
  78.8 0.0 collective-permute-done.23.refs_3_
  78.8 0.0 collective-permute-done.22.refs_2_
  78.8 1.2 %shard_map.94 = bf16[3,256,768]{2,1,0:T(8,128)(2,1)} custom-call(f32[256,1152]{1,0:T(8,128)S(1)} %get-tuple-element.50.refs_0_, f32[256,1152]{1,0:T(8,128)S(1)} %get-tuple-element.51.refs_1_, bf16[256,1152]{1,0:T(8,128)(2,1)S(1)} %collective-permute-done.22.refs_2_, bf16[256,1152]{1,0:T(8,128)(2,1)S(1)} %collective-permute-done.23.refs_3_), custom_call_target="tpu_custom_call" | custom-call | flops 589824 | bytes 4718592 | tf_op jit(solution)/shard_map/pallas_call | solution.py:41
  (1 shorter events, 0.0 us)
Async XLA Ops:
  2.5 9.2 %collective-permute-start = (bf16[2,24,2048]{2,1,0:T(8,128)(2,1)S(1)}, bf16[2,24,2048]{2,1,0:T(8,128)(2,1)S(1)}, u32[]{:S(2)}, u32[]{:S(2)}) collective-permute-start(bf16[2,24,2048]{2,1,0:T(8,128)(2,1)S(1)} %get-tuple-element.30), channel_id=1, source_target_pairs={{0,1},{1,0},{2,3},{3,2},{4,5},{5,4},{6,7},{7,6},{8,9},{9,8},{10,11... | collective-permute-start | bytes 589832 | tf_op jit(solution)/shard_map/ppermute | solution.py:261
  5.5 13.7 %collective-permute-start.1 = (bf16[2,24,2048]{2,1,0:T(8,128)(2,1)S(1)}, bf16[2,24,2048]{2,1,0:T(8,128)(2,1)S(1)}, u32[]{:S(2)}, u32[]{:S(2)}) collective-permute-start(bf16[2,24,2048]{2,1,0:T(8,128)(2,1)S(1)} %get-tuple-element.31), channel_id=1, source_target_pairs={{0,2},{1,3},{2,0},{3,1},{4,6},{5,7},{6,4},{7,5},{8,10},{9,11},{10,... | collective-permute-start | bytes 589832 | tf_op jit(solution)/shard_map/ppermute | solution.py:261
  7.0 12.2 %collective-permute-start.2 = (bf16[2,24,2048]{2,1,0:T(8,128)(2,1)S(1)}, bf16[2,24,2048]{2,1,0:T(8,128)(2,1)S(1)}, u32[]{:S(2)}, u32[]{:S(2)}) collective-permute-start(bf16[2,24,2048]{2,1,0:T(8,128)(2,1)S(1)} %get-tuple-element.32), channel_id=1, source_target_pairs={{0,3},{1,2},{2,1},{3,0},{4,7},{5,6},{6,5},{7,4},{8,11},{9,10},{10,... | collective-permute-start | bytes 589832 | tf_op jit(solution)/shard_map/ppermute | solution.py:261
  7.0 13.9 %collective-permute-start.6 = (bf16[4,24,1024]{2,1,0:T(8,128)(2,1)S(1)}, bf16[4,24,1024]{2,1,0:T(8,128)(2,1)S(1)}, u32[]{:S(2)}, u32[]{:S(2)}) collective-permute-start(bf16[4,24,1024]{2,1,0:T(8,128)(2,1)S(1)} %get-tuple-element.43), channel_id=1, source_target_pairs={{0,8},{4,12},{8,0},{12,4},{16,24},{20,28},{24,16},{28,20},{1,9},{5... | collective-permute-start | bytes 589832 | tf_op jit(solution)/shard_map/ppermute | solution.py:269
  9.1 17.0 %collective-permute-start.7 = (bf16[4,24,1024]{2,1,0:T(8,128)(2,1)S(1)}, bf16[4,24,1024]{2,1,0:T(8,128)(2,1)S(1)}, u32[]{:S(2)}, u32[]{:S(2)}) collective-permute-start(bf16[4,24,1024]{2,1,0:T(8,128)(2,1)S(1)} %get-tuple-element.44), channel_id=1, source_target_pairs={{0,16},{4,20},{8,24},{12,28},{16,0},{20,4},{24,8},{28,12},{1,17},{... | collective-permute-start | bytes 589832 | tf_op jit(solution)/shard_map/ppermute | solution.py:269
  11.7 14.4 %collective-permute-start.8 = (bf16[4,24,1024]{2,1,0:T(8,128)(2,1)S(1)}, bf16[4,24,1024]{2,1,0:T(8,128)(2,1)S(1)}, u32[]{:S(2)}, u32[]{:S(2)}) collective-permute-start(bf16[4,24,1024]{2,1,0:T(8,128)(2,1)S(1)} %get-tuple-element.45), channel_id=1, source_target_pairs={{0,24},{4,28},{8,16},{12,20},{16,8},{20,12},{24,0},{28,4},{1,25},{... | collective-permute-start | bytes 589832 | tf_op jit(solution)/shard_map/ppermute | solution.py:269
  20.9 12.5 %collective-permute-start.17 = (bf16[96,1152]{1,0:T(8,128)(2,1)S(1)}, bf16[96,1152]{1,0:T(8,128)(2,1)S(1)}, u32[]{:S(2)}, u32[]{:S(2)}) collective-permute-start(bf16[96,1152]{1,0:T(8,128)(2,1)S(1)} %get-tuple-element.34.refs_1_.refs_4_), channel_id=1, source_target_pairs={{0,8},{4,12},{8,0},{12,4},{16,24},{20,28},{24,16},{28,20},{1,9},{5... | collective-permute-start | bytes 663560 | tf_op jit(solution)/shard_map/ppermute | solution.py:269
  26.1 5.7 %collective-permute-start.9 = (bf16[4,24,1024]{2,1,0:T(8,128)(2,1)S(1)}, bf16[4,24,1024]{2,1,0:T(8,128)(2,1)S(1)}, u32[]{:S(2)}, u32[]{:S(2)}) collective-permute-start(bf16[4,24,1024]{2,1,0:T(8,128)(2,1)S(1)} %get-tuple-element.47), channel_id=1, source_target_pairs={{0,1},{1,0},{2,3},{3,2},{4,5},{5,4},{6,7},{7,6},{8,9},{9,8},{10,11... | collective-permute-start | bytes 589832 | tf_op jit(solution)/shard_map/ppermute | solution.py:261
  27.7 6.6 %collective-permute-start.12 = (bf16[96,1152]{1,0:T(8,128)(2,1)S(1)}, bf16[96,1152]{1,0:T(8,128)(2,1)S(1)}, u32[]{:S(2)}, u32[]{:S(2)}) collective-permute-start(bf16[96,1152]{1,0:T(8,128)(2,1)S(1)} %get-tuple-element.33.refs_0_.refs_4_), channel_id=1, source_target_pairs={{0,8},{4,12},{8,0},{12,4},{16,24},{20,28},{24,16},{28,20},{1,9},{5... | collective-permute-start | bytes 663560 | tf_op jit(solution)/shard_map/ppermute | solution.py:269
  30.4 4.6 %collective-permute-start.19 = (bf16[96,1152]{1,0:T(8,128)(2,1)S(1)}, bf16[96,1152]{1,0:T(8,128)(2,1)S(1)}, u32[]{:S(2)}, u32[]{:S(2)}) collective-permute-start(bf16[96,1152]{1,0:T(8,128)(2,1)S(1)} %get-tuple-element.34.refs_1_.refs_4_), channel_id=1, source_target_pairs={{8,16},{12,20},{16,8},{20,12},{9,17},{13,21},{17,9},{21,13},{10,18... | collective-permute-start | bytes 663560 | tf_op jit(solution)/shard_map/ppermute | solution.py:269
  31.0 9.0 %collective-permute-start.14 = (bf16[96,1152]{1,0:T(8,128)(2,1)S(1)}, bf16[96,1152]{1,0:T(8,128)(2,1)S(1)}, u32[]{:S(2)}, u32[]{:S(2)}) collective-permute-start(bf16[96,1152]{1,0:T(8,128)(2,1)S(1)} %get-tuple-element.33.refs_0_.refs_4_), channel_id=1, source_target_pairs={{8,16},{12,20},{16,8},{20,12},{9,17},{13,21},{17,9},{21,13},{10,18... | collective-permute-start | bytes 663560 | tf_op jit(solution)/shard_map/ppermute | solution.py:269
  31.9 5.7 %collective-permute-start.10 = (bf16[4,24,1024]{2,1,0:T(8,128)(2,1)S(1)}, bf16[4,24,1024]{2,1,0:T(8,128)(2,1)S(1)}, u32[]{:S(2)}, u32[]{:S(2)}) collective-permute-start(bf16[4,24,1024]{2,1,0:T(8,128)(2,1)S(1)} %get-tuple-element.48), channel_id=1, source_target_pairs={{0,2},{1,3},{2,0},{3,1},{4,6},{5,7},{6,4},{7,5},{8,10},{9,11},{10,... | collective-permute-start | bytes 589832 | tf_op jit(solution)/shard_map/ppermute | solution.py:261
  33.4 7.9 %collective-permute-start.18 = (bf16[96,1152]{1,0:T(8,128)(2,1)S(1)}, bf16[96,1152]{1,0:T(8,128)(2,1)S(1)}, u32[]{:S(2)}, u32[]{:S(2)}) collective-permute-start(bf16[96,1152]{1,0:T(8,128)(2,1)S(1)} %collective-permute-done.17.refs_5_), channel_id=1, source_target_pairs={{8,16},{12,20},{16,8},{20,12},{9,17},{13,21},{17,9},{21,13},{10,18... | collective-permute-start | bytes 663560 | tf_op jit(solution)/shard_map/ppermute | solution.py:269
  34.3 8.3 %collective-permute-start.13 = (bf16[96,1152]{1,0:T(8,128)(2,1)S(1)}, bf16[96,1152]{1,0:T(8,128)(2,1)S(1)}, u32[]{:S(2)}, u32[]{:S(2)}) collective-permute-start(bf16[96,1152]{1,0:T(8,128)(2,1)S(1)} %collective-permute-done.12.refs_5_), channel_id=1, source_target_pairs={{8,16},{12,20},{16,8},{20,12},{9,17},{13,21},{17,9},{21,13},{10,18... | collective-permute-start | bytes 663560 | tf_op jit(solution)/shard_map/ppermute | solution.py:269
  35.0 16.2 %collective-permute-start.20 = (bf16[96,1152]{1,0:T(8,128)(2,1)S(1)}, bf16[96,1152]{1,0:T(8,128)(2,1)S(1)}, u32[]{:S(2)}, u32[]{:S(2)}) collective-permute-start(bf16[96,1152]{1,0:T(8,128)(2,1)S(1)} %collective-permute-done.19.refs_5_), channel_id=1, source_target_pairs={{8,0},{12,4},{16,24},{20,28},{9,1},{13,5},{17,25},{21,29},{10,2},{... | collective-permute-start | bytes 663560 | tf_op jit(solution)/shard_map/ppermute | solution.py:269
  37.5 6.6 %collective-permute-start.11 = (bf16[4,24,1024]{2,1,0:T(8,128)(2,1)S(1)}, bf16[4,24,1024]{2,1,0:T(8,128)(2,1)S(1)}, u32[]{:S(2)}, u32[]{:S(2)}) collective-permute-start(bf16[4,24,1024]{2,1,0:T(8,128)(2,1)S(1)} %get-tuple-element.49), channel_id=1, source_target_pairs={{0,3},{1,2},{2,1},{3,0},{4,7},{5,6},{6,5},{7,4},{8,11},{9,10},{10,... | collective-permute-start | bytes 589832 | tf_op jit(solution)/shard_map/ppermute | solution.py:261
  40.0 15.9 %collective-permute-start.15 = (bf16[96,1152]{1,0:T(8,128)(2,1)S(1)}, bf16[96,1152]{1,0:T(8,128)(2,1)S(1)}, u32[]{:S(2)}, u32[]{:S(2)}) collective-permute-start(bf16[96,1152]{1,0:T(8,128)(2,1)S(1)} %collective-permute-done.14.refs_5_), channel_id=1, source_target_pairs={{8,0},{12,4},{16,24},{20,28},{9,1},{13,5},{17,25},{21,29},{10,2},{... | collective-permute-start | bytes 663560 | tf_op jit(solution)/shard_map/ppermute | solution.py:269
  41.3 17.8 %collective-permute-start.21 = (bf16[96,1152]{1,0:T(8,128)(2,1)S(1)}, bf16[96,1152]{1,0:T(8,128)(2,1)S(1)}, u32[]{:S(2)}, u32[]{:S(2)}) collective-permute-start(bf16[96,1152]{1,0:T(8,128)(2,1)S(1)} %collective-permute-done.18.refs_6_), channel_id=1, source_target_pairs={{8,0},{12,4},{16,24},{20,28},{9,1},{13,5},{17,25},{21,29},{10,2},{... | collective-permute-start | bytes 663560 | tf_op jit(solution)/shard_map/ppermute | solution.py:269
  42.6 18.8 %collective-permute-start.16 = (bf16[96,1152]{1,0:T(8,128)(2,1)S(1)}, bf16[96,1152]{1,0:T(8,128)(2,1)S(1)}, u32[]{:S(2)}, u32[]{:S(2)}) collective-permute-start(bf16[96,1152]{1,0:T(8,128)(2,1)S(1)} %collective-permute-done.13.refs_6_), channel_id=1, source_target_pairs={{8,0},{12,4},{16,24},{20,28},{9,1},{13,5},{17,25},{21,29},{10,2},{... | collective-permute-start | bytes 663560 | tf_op jit(solution)/shard_map/ppermute | solution.py:269
  59.6 19.2 %collective-permute-start.23 = (bf16[256,1152]{1,0:T(8,128)(2,1)S(1)}, bf16[256,1152]{1,0:T(8,128)(2,1)S(1)}, u32[]{:S(2)}, u32[]{:S(2)}) collective-permute-start(bf16[256,1152]{1,0:T(8,128)(2,1)S(1)} %get-tuple-element.53), channel_id=1, source_target_pairs={{0,4},{4,0},{8,12},{12,8},{16,20},{20,16},{24,28},{28,24},{1,5},{5... | collective-permute-start | bytes 1769480 | tf_op jit(solution)/shard_map/ppermute | solution.py:354
  62.0 15.1 %copy-start = (bf16[128,2048]{1,0:T(8,128)(2,1)S(1)}, bf16[128,2048]{1,0:T(8,128)(2,1)}, u32[]{:S(2)}) copy-start(bf16[128,2048]{1,0:T(8,128)(2,1)} %cot_ref.1) | copy-start | bytes 1572868
  62.0 15.1 %copy-start.1 = (s32[128,8]{0,1:T(8,128)S(1)}, s32[128,8]{0,1:T(8,128)}, u32[]{:S(2)}) copy-start(s32[128,8]{0,1:T(8,128)} %param.6) | copy-start | bytes 12292
  62.0 15.1 %copy-start.2 = (f32[128,8]{0,1:T(8,128)S(1)}, f32[128,8]{0,1:T(8,128)}, u32[]{:S(2)}) copy-start(f32[128,8]{0,1:T(8,128)} %param.7) | copy-start | bytes 12292
  62.0 16.8 %collective-permute-start.22 = (bf16[256,1152]{1,0:T(8,128)(2,1)S(1)}, bf16[256,1152]{1,0:T(8,128)(2,1)S(1)}, u32[]{:S(2)}, u32[]{:S(2)}) collective-permute-start(bf16[256,1152]{1,0:T(8,128)(2,1)S(1)} %get-tuple-element.52), channel_id=1, source_target_pairs={{0,4},{4,0},{8,12},{12,8},{16,20},{20,16},{24,28},{28,24},{1,5},{5... | collective-permute-start | bytes 1769480 | tf_op jit(solution)/shard_map/ppermute | solution.py:354
  65.0 7.8 %collective-permute-start.3 = (bf16[2,24,2048]{2,1,0:T(8,128)(2,1)S(1)}, bf16[2,24,2048]{2,1,0:T(8,128)(2,1)S(1)}, u32[]{:S(2)}, u32[]{:S(2)}) collective-permute-start(bf16[2,24,2048]{2,1,0:T(8,128)(2,1)S(1)} %get-tuple-element.36), channel_id=1, source_target_pairs={{0,1},{1,0},{2,3},{3,2},{4,5},{5,4},{6,7},{7,6},{8,9},{9,8},{10,11... | collective-permute-start | bytes 589832 | tf_op jit(solution)/shard_map/ppermute | solution.py:261
  65.8 11.2 %collective-permute-start.4 = (bf16[2,24,2048]{2,1,0:T(8,128)(2,1)S(1)}, bf16[2,24,2048]{2,1,0:T(8,128)(2,1)S(1)}, u32[]{:S(2)}, u32[]{:S(2)}) collective-permute-start(bf16[2,24,2048]{2,1,0:T(8,128)(2,1)S(1)} %get-tuple-element.37), channel_id=1, source_target_pairs={{0,2},{1,3},{2,0},{3,1},{4,6},{5,7},{6,4},{7,5},{8,10},{9,11},{10,... | collective-permute-start | bytes 589832 | tf_op jit(solution)/shard_map/ppermute | solution.py:261
  67.3 9.7 %collective-permute-start.5 = (bf16[2,24,2048]{2,1,0:T(8,128)(2,1)S(1)}, bf16[2,24,2048]{2,1,0:T(8,128)(2,1)S(1)}, u32[]{:S(2)}, u32[]{:S(2)}) collective-permute-start(bf16[2,24,2048]{2,1,0:T(8,128)(2,1)S(1)} %get-tuple-element.38), channel_id=1, source_target_pairs={{0,3},{1,2},{2,1},{3,0},{4,7},{5,6},{6,5},{7,4},{8,11},{9,10},{10,... | collective-permute-start | bytes 589832 | tf_op jit(solution)/shard_map/ppermute | solution.py:261

commit v2 on v1

--- a/solution.py
+++ b/solution.py
@@ -188,14 +188,24 @@
 
 
 def regroup_kernel(experts, zs, *refs):
+    results, shares, outs = refs[:experts], refs[experts : experts + zs], refs[experts + zs :]
+    wide = shares[0].shape[2]
     for k in range(experts):
+        outs[k][:2] = results[k][...]
         for m in range(zs):
-            refs[zs + k][m] = refs[m][k]
-
-
-def grad_sums(feats, chips, picks, refs, cut):
+            row, at = divmod(m * wide, results[k].shape[2])
+            outs[k][2 + row, :, at : at + wide] = shares[m][k]
+
+
+def features_of(message, chip, zs):
+    wide = 2 * message.shape[2] // zs
+    row, at = divmod(chip * wide, message.shape[2])
+    return message[2 + row, :, at : at + wide]
+
+
+def grad_sums(feats, chips, zs, picks, refs, cut):
     lo, hi, hidden = cut
-    rows_f = stack_rows([f[m] for m in chips for f in feats])
+    rows_f = stack_rows([features_of(f, m, zs) for m in chips for f in feats])
     acts = []
     for n in picks:
         value = refs[0][...]
@@ -218,14 +228,14 @@
     return sums[0] if len(sums) == 1 else jnp.concatenate(sums, axis=1)
 
 
-def early_grad_kernel(experts, chips, picks, cut, *refs):
+def early_grad_kernel(experts, chips, zs, picks, cut, *refs):
     feats, acts, total = refs[:experts], refs[experts:-1], refs[-1]
-    total[...] = grad_sums(feats, chips, picks, acts, cut)
-
-
-def late_grad_kernel(experts, chips, picks, cut, *refs):
+    total[...] = grad_sums(feats, chips, zs, picks, acts, cut)
+
+
+def late_grad_kernel(experts, chips, zs, picks, cut, *refs):
     feats, (total, *acts), (own, send) = refs[:experts], refs[experts:-2], refs[-2:]
-    more = grad_sums(feats, chips, picks, acts, cut)
+    more = grad_sums(feats, chips, zs, picks, acts, cut)
     half = more.shape[0] // CORES
     own[...] = total[:half] + more[:half]
     send[...] = (total[half:] + more[half:]).astype(BF16)
@@ -274,8 +284,8 @@
         near = swap_z(block, 1)
         middle = swap_z(block, 3, (1, 2))
         through = swap_z(near, 3, (1, 2))
-        ends = swap_z(middle, 1, (1, 2))
-        last = swap_z(through, 1, (1, 2))
+        ends = swap_z(middle, 1)
+        last = swap_z(through, 1)
         return [[near], [through, ends], [middle, last]]
 
     sent = local_call(
@@ -315,14 +325,13 @@
         [staged, *acts],
         6 * rows * width * hidden,
     )
-    back = swap_expert(results)
-    by_expert = local_call(
+    messages = local_call(
         functools.partial(regroup_kernel, experts, zs),
-        [shape_of((zs, CAP, 2 * chip_width))] * experts,
-        shares,
+        [shape_of((4, CAP, width))] * experts,
+        [*results, *shares],
         0,
     )
-    feats = swap_expert(by_expert)
+    back = feats = swap_expert(messages)
     mixed, grad_tokens, gates = local_call(
         functools.partial(combine_kernel, experts),
         [shape_of((tok_rows, width)), shape_of((tok_rows, width)), shape_of(ids.shape, F32)],
@@ -335,7 +344,12 @@
         pieces = [[acts[k]]] + spread[k][:-1]
         (total,) = local_call(
             functools.partial(
-                early_grad_kernel, experts, tuple(range(zs - 1)), tuple(map(len, pieces)), cut
+                early_grad_kernel,
+                experts,
+                tuple(range(zs - 1)),
+                zs,
+                tuple(map(len, pieces)),
+                cut,
             ),
             [shape_of((chip_width, step), F32)],
             [*feats, *[a for piece in pieces for a in piece]],
@@ -343,7 +357,7 @@
         )
         pieces = spread[k][-1]
         own, send = local_call(
-            functools.partial(late_grad_kernel, experts, (zs - 1,), (len(pieces),), cut),
+            functools.partial(late_grad_kernel, experts, (zs - 1,), zs, (len(pieces),), cut),
             [
                 shape_of((chip_width // CORES, step), F32),
                 shape_of((chip_width // CORES, step)),

time: 80.3 us -> 68.6 us (0.85)
  waiting for transfers between devices: 30.4 us -> 15.2 us
  starting transfers between devices: 32.7 us -> 36.2 us
    ppermute x13, waiting for transfers between devices: 20.3 us -> 9.05 us  [swap_z(): return lax.ppermute(block, 'dp', pairs)]
    ppermute x13, starting transfers between devices: 18.9 us -> 28.2 us  [swap_z(): return lax.ppermute(block, 'dp', pairs)]
    ppermute x9 -> x6, starting transfers between devices: 13.7 us -> 7.92 us  [swap_expert(): moved[m] = lax.ppermute(blocks[m], 'expert', pairs)]
    ppermute x9 -> x6, waiting for transfers between devices: 10.1 us -> 5.89 us  [swap_expert(): moved[m] = lax.ppermute(blocks[m], 'expert', pairs)]
  transfers between devices with their start and end apart: 24 -> 21, of which waited for: 11 -> 8; matrix products, arithmetic and copies ran while one was open for 0% -> 0% of each run, Pallas kernels for 16% -> 19%
where the time goes in v2:
time: 68.6 us; the launch traced here: 68.3 us
  starting transfers between devices  36.2 us (53%)
  Pallas kernels  16 us (23%)
  waiting for transfers between devices  15.2 us (22%)
  between operations  0.86 us (1%)
    ppermute x13, starting transfers between devices, swap_z(): return lax.ppermute(block, 'dp', pairs)  28.2 us
    pallas_call x11, Pallas kernels, local_call(): return call(*args)  16 us
    ppermute x13, waiting for transfers between devices, swap_z(): return lax.ppermute(block, 'dp', pairs)  9.05 us
    ppermute x6, starting transfers between devices, swap_expert(): moved[m] = lax.ppermute(blocks[m], 'expert', pairs)  7.92 us
    ppermute x6, waiting for transfers between devices, swap_expert(): moved[m] = lax.ppermute(blocks[m], 'expert', pairs)  5.89 us
  transfers between devices with their start and end apart: 21, of which 8 were waited for; matrix products, arithmetic and copies ran while one was open for 0% of the time, Pallas kernels for 19%

profile of v2, /device:TPU:0, one launch (start us, length us, event | category | flops | bytes accessed | tf_op | source)
XLA Modules:
  0.0 68.3 jit_solution(4527815476277934622)
XLA Ops:
  0.6 1.8 %shard_map.85 = (bf16[2,24,2048]{2,1,0:T(8,128)(2,1)S(1)}, bf16[2,24,2048]{2,1,0:T(8,128)(2,1)S(1)}, bf16[2,24,2048]{2,1,0:T(8,128)(2,1)S(1)}, bf16[2,24,2048]{2...) custom-call(s32[8,128]{1,0:T(8,128)} %bitcast.9, ...), custom_call_target="tpu_custom_call" | custom-call | flops 100663296 | bytes 2629632 | tf_op jit(solution)/shard_map/pallas_call | solution.py:41
  2.5 3.0 %collective-permute-start = (bf16[2,24,2048]{2,1,0:T(8,128)(2,1)S(1)}, bf16[2,24,2048]{2,1,0:T(8,128)(2,1)S(1)}, u32[]{:S(2)}, u32[]{:S(2)}) collective-permute-start(bf16[2,24,2048]{2,1,0:T(8,128)(2,1)S(1)} %get-tuple-element.30), channel_id=1, source_target_pairs={{0,1},{1,0},{2,3},{3,2},{4,5},{5,4},{6,7},{7,6},{8,9},{9,8},{10,11... | collective-permute-start | bytes 589832 | tf_op jit(solution)/shard_map/ppermute | solution.py:271
  5.5 1.5 %collective-permute-start.1 = (bf16[2,24,2048]{2,1,0:T(8,128)(2,1)S(1)}, bf16[2,24,2048]{2,1,0:T(8,128)(2,1)S(1)}, u32[]{:S(2)}, u32[]{:S(2)}) collective-permute-start(bf16[2,24,2048]{2,1,0:T(8,128)(2,1)S(1)} %get-tuple-element.31), channel_id=1, source_target_pairs={{0,2},{1,3},{2,0},{3,1},{4,6},{5,7},{6,4},{7,5},{8,10},{9,11},{10,... | collective-permute-start | bytes 589832 | tf_op jit(solution)/shard_map/ppermute | solution.py:271
  7.0 0.0 collective-permute-start.2
  7.1 2.0 %collective-permute-start.3 = (bf16[4,24,1024]{2,1,0:T(8,128)(2,1)S(1)}, bf16[4,24,1024]{2,1,0:T(8,128)(2,1)S(1)}, u32[]{:S(2)}, u32[]{:S(2)}) collective-permute-start(bf16[4,24,1024]{2,1,0:T(8,128)(2,1)S(1)} %get-tuple-element.40), channel_id=1, source_target_pairs={{0,8},{4,12},{8,0},{12,4},{16,24},{20,28},{24,16},{28,20},{1,9},{5... | collective-permute-start | bytes 589832 | tf_op jit(solution)/shard_map/ppermute | solution.py:279
  9.1 2.6 %collective-permute-start.4 = (bf16[4,24,1024]{2,1,0:T(8,128)(2,1)S(1)}, bf16[4,24,1024]{2,1,0:T(8,128)(2,1)S(1)}, u32[]{:S(2)}, u32[]{:S(2)}) collective-permute-start(bf16[4,24,1024]{2,1,0:T(8,128)(2,1)S(1)} %get-tuple-element.41), channel_id=1, source_target_pairs={{0,16},{4,20},{8,24},{12,28},{16,0},{20,4},{24,8},{28,12},{1,17},{... | collective-permute-start | bytes 589832 | tf_op jit(solution)/shard_map/ppermute | solution.py:279
  11.7 3.8 %shard_map.84.w_ref = bf16[3,2048,768]{2,1,0:T(8,128)(2,1)S(1)} custom-call(bf16[3,2048,768]{2,1,0:T(8,128)(2,1)} %bitcast.13), custom_call_target="tpu_custom_call" | custom-call | bytes 18874368 | tf_op jit(solution)/shard_map/pallas_call | solution.py:41
  15.5 0.0 collective-permute-done.refs_1_
  15.5 0.1 collective-permute-start.5
  15.6 0.5 collective-permute-done.1.refs_2_
  16.1 0.0 collective-permute-done.2.refs_3_
  16.1 1.7 %shard_map.86 = (bf16[96,1152]{1,0:T(8,128)(2,1)S(1)}, bf16[96,1152]{1,0:T(8,128)(2,1)S(1)}) custom-call(bf16[3,2048,768]{2,1,0:T(8,128)(2,1)S(1)} %shard_map.84.w_ref, bf16[2,24,2048]{2,1,0:T(8,128)(2,1)S(1)} %get-tuple-element.29.refs_0_, bf16[2,24,2048]{2,1,0:T(8,128)(2,1)S(1)} %collective-permute-done.refs_1_, ...), custom_call_target="tpu_custom_call" | custom-call | flops 905969664 | bytes 10665984 | tf_op jit(solution)/shard_map/pallas_call | solution.py:41
  17.8 0.7 collective-permute-start.11
  18.4 4.5 %collective-permute-start.9 = (bf16[96,1152]{1,0:T(8,128)(2,1)S(1)}, bf16[96,1152]{1,0:T(8,128)(2,1)S(1)}, u32[]{:S(2)}, u32[]{:S(2)}) collective-permute-start(bf16[96,1152]{1,0:T(8,128)(2,1)S(1)} %get-tuple-element.33.refs_0_.refs_4_), channel_id=1, source_target_pairs={{0,8},{4,12},{8,0},{12,4},{16,24},{20,28},{24,16},{28,20},{1,9},{5... | collective-permute-start | bytes 663560 | tf_op jit(solution)/shard_map/ppermute | solution.py:279
  22.9 2.9 %shard_map.87 = (bf16[2,24,2048]{2,1,0:T(8,128)(2,1)S(1)}, bf16[2,24,2048]{2,1,0:T(8,128)(2,1)S(1)}, bf16[2,24,2048]{2,1,0:T(8,128)(2,1)S(1)}, bf16[2,24,2048]{2,1,0:T(8,128)(2,1)S(1)}) custom-call(bf16[3,2048,768]{2,1,0:T(8,128)(2,1)S(1)} %shard_map.84.w_ref, bf16[96,1152]{1,0:T(8,128)(2,1)S(1)} %get-tuple-element.33.refs_0_.refs_4_, ...), custom_call_target="tpu_custom_call" | custom-call | flops 905969664 | bytes 10665984 | tf_op jit(solution)/shard_map/pallas_call | solution.py:41
  25.9 0.0 collective-permute-done.3.refs_5_
  25.9 0.0 collective-permute-done.4.refs_6_
  25.9 0.0 collective-permute-done.5.refs_7_
  25.9 0.1 shard_map.88
  26.0 1.3 %collective-permute-start.6 = (bf16[4,24,2048]{2,1,0:T(8,128)(2,1)S(1)}, bf16[4,24,2048]{2,1,0:T(8,128)(2,1)S(1)}, u32[]{:S(2)}, u32[]{:S(2)}) collective-permute-start(bf16[4,24,2048]{2,1,0:T(8,128)(2,1)S(1)} %get-tuple-element.44), channel_id=1, source_target_pairs={{0,1},{1,0},{2,3},{3,2},{4,5},{5,4},{6,7},{7,6},{8,9},{9,8},{10,11... | collective-permute-start | bytes 1179656 | tf_op jit(solution)/shard_map/ppermute | solution.py:271
  27.3 3.8 %collective-permute-start.14 = (bf16[96,1152]{1,0:T(8,128)(2,1)S(1)}, bf16[96,1152]{1,0:T(8,128)(2,1)S(1)}, u32[]{:S(2)}, u32[]{:S(2)}) collective-permute-start(bf16[96,1152]{1,0:T(8,128)(2,1)S(1)} %get-tuple-element.34.refs_1_.refs_4_), channel_id=1, source_target_pairs={{0,8},{4,12},{8,0},{12,4},{16,24},{20,28},{24,16},{28,20},{1,9},{5... | collective-permute-start | bytes 663560 | tf_op jit(solution)/shard_map/ppermute | solution.py:279
  31.1 0.7 collective-permute-start.16
  31.8 0.0 collective-permute-done.11.refs_5_
  31.8 1.6 %collective-permute-start.7 = (bf16[4,24,2048]{2,1,0:T(8,128)(2,1)S(1)}, bf16[4,24,2048]{2,1,0:T(8,128)(2,1)S(1)}, u32[]{:S(2)}, u32[]{:S(2)}) collective-permute-start(bf16[4,24,2048]{2,1,0:T(8,128)(2,1)S(1)} %get-tuple-element.45), channel_id=1, source_target_pairs={{0,2},{1,3},{2,0},{3,1},{4,6},{5,7},{6,4},{7,5},{8,10},{9,11},{10,... | collective-permute-start | bytes 1179656 | tf_op jit(solution)/shard_map/ppermute | solution.py:271
  33.4 0.0 collective-permute-done.9.refs_5_
  33.4 0.5 collective-permute-start.8
  33.9 1.3 %collective-permute-done.14.refs_5_ = bf16[96,1152]{1,0:T(8,128)(2,1)S(1)} collective-permute-done((bf16[96,1152]{1,0:T(8,128)(2,1)S(1)}, bf16[96,1152]{1,0:T(8,128)(2,1)S(1)}, u32[]{:S(2)}, u32[]{:S(2)}) %collective-permute-start.14) | collective-permute-done | bytes 221216 | tf_op jit(solution)/shard_map/ppermute | solution.py:279
  35.2 0.7 collective-permute-start.15
  35.9 0.0 collective-permute-done.16.refs_5_
  35.9 0.7 collective-permute-start.10
  36.6 0.1 collective-permute-done.6.refs_1_
  36.7 7.6 %collective-permute-start.17 = (bf16[96,1152]{1,0:T(8,128)(2,1)S(1)}, bf16[96,1152]{1,0:T(8,128)(2,1)S(1)}, u32[]{:S(2)}, u32[]{:S(2)}) collective-permute-start(bf16[96,1152]{1,0:T(8,128)(2,1)S(1)} %collective-permute-done.16.refs_5_), channel_id=1, source_target_pairs={{0,8},{4,12},{8,0},{12,4},{16,24},{20,28},{24,16},{28,20},{1,9},{5... | collective-permute-start | bytes 663560 | tf_op jit(solution)/shard_map/ppermute | solution.py:279
  44.3 5.2 %collective-permute-done.7.refs_2_ = bf16[4,24,2048]{2,1,0:T(8,128)(2,1)S(1)} collective-permute-done((bf16[4,24,2048]{2,1,0:T(8,128)(2,1)S(1)}, bf16[4,24,2048]{2,1,0:T(8,128)(2,1)S(1)}, u32[]{:S(2)}, u32[]{:S(2)}) %collective-permute-start.7) | collective-permute-done | bytes 393248 | tf_op jit(solution)/shard_map/ppermute | solution.py:271
  49.5 2.9 %collective-permute-start.12 = (bf16[96,1152]{1,0:T(8,128)(2,1)S(1)}, bf16[96,1152]{1,0:T(8,128)(2,1)S(1)}, u32[]{:S(2)}, u32[]{:S(2)}) collective-permute-start(bf16[96,1152]{1,0:T(8,128)(2,1)S(1)} %collective-permute-done.11.refs_5_), channel_id=1, source_target_pairs={{0,8},{4,12},{8,0},{12,4},{16,24},{20,28},{24,16},{28,20},{1,9},{5... | collective-permute-start | bytes 663560 | tf_op jit(solution)/shard_map/ppermute | solution.py:279
  52.4 0.0 collective-permute-done.15.refs_6_
  52.4 0.0 collective-permute-start.18
  52.4 0.0 collective-permute-done.10.refs_6_
  52.4 2.0 %collective-permute-start.13 = (bf16[96,1152]{1,0:T(8,128)(2,1)S(1)}, bf16[96,1152]{1,0:T(8,128)(2,1)S(1)}, u32[]{:S(2)}, u32[]{:S(2)}) collective-permute-start(bf16[96,1152]{1,0:T(8,128)(2,1)S(1)} %collective-permute-done.10.refs_6_), channel_id=1, source_target_pairs={{0,8},{4,12},{8,0},{12,4},{16,24},{20,28},{24,16},{28,20},{1,9},{5... | collective-permute-start | bytes 663560 | tf_op jit(solution)/shard_map/ppermute | solution.py:279
  54.4 0.0 collective-permute-done.8.refs_3_
  54.4 0.0 collective-permute-done.17.refs_7_
  54.5 0.9 %shard_map.92.refs_4_ = f32[512,1152]{1,0:T(8,128)S(1)} custom-call(bf16[4,24,2048]{2,1,0:T(8,128)(2,1)S(1)} %get-tuple-element.43.refs_0_, bf16[4,24,2048]{2,1,0:T(8,128)(2,1)S(1)} %collective-permute-done.6.refs_1_, bf16[4,24,2048]{2,1,0:T(8,128)(2,1)S(1)} %collective-permute-done.7.refs_2_, bf16[4,24,2048]{2,1,0:T(8,128)(2,1)S(1)} %collective-permute-done.8.refs_3_, ...), custom_call_target="tpu_custom_call" | custom-call | flops 339738624 | bytes 4816896 | tf_op jit(solution)/shard_map/pallas_call | solution.py:41
  55.3 3.4 %collective-permute-done.12.refs_7_ = bf16[96,1152]{1,0:T(8,128)(2,1)S(1)} collective-permute-done((bf16[96,1152]{1,0:T(8,128)(2,1)S(1)}, bf16[96,1152]{1,0:T(8,128)(2,1)S(1)}, u32[]{:S(2)}, u32[]{:S(2)}) %collective-permute-start.12) | collective-permute-done | bytes 221216 | tf_op jit(solution)/shard_map/ppermute | solution.py:279
  58.7 0.9 %shard_map.90.refs_4_ = f32[512,1152]{1,0:T(8,128)S(1)} custom-call(bf16[4,24,2048]{2,1,0:T(8,128)(2,1)S(1)} %get-tuple-element.43.refs_0_, bf16[4,24,2048]{2,1,0:T(8,128)(2,1)S(1)} %collective-permute-done.6.refs_1_, bf16[4,24,2048]{2,1,0:T(8,128)(2,1)S(1)} %collective-permute-done.7.refs_2_, bf16[4,24,2048]{2,1,0:T(8,128)(2,1)S(1)} %collective-permute-done.8.refs_3_, ...), custom_call_target="tpu_custom_call" | custom-call | flops 339738624 | bytes 4816896 | tf_op jit(solution)/shard_map/pallas_call | solution.py:41
  59.6 2.6 %collective-permute-done.18.refs_6_ = bf16[96,1152]{1,0:T(8,128)(2,1)S(1)} collective-permute-done((bf16[96,1152]{1,0:T(8,128)(2,1)S(1)}, bf16[96,1152]{1,0:T(8,128)(2,1)S(1)}, u32[]{:S(2)}, u32[]{:S(2)}) %collective-permute-start.18) | collective-permute-done | bytes 221216 | tf_op jit(solution)/shard_map/ppermute | solution.py:279
  62.1 0.5 shard_map.93
  62.6 0.0 copy-start
  62.6 0.0 copy-start.1
  62.7 0.0 copy-start.2
  62.7 0.1 collective-permute-start.20
  62.7 1.7 %collective-permute-done.13.refs_6_ = bf16[96,1152]{1,0:T(8,128)(2,1)S(1)} collective-permute-done((bf16[96,1152]{1,0:T(8,128)(2,1)S(1)}, bf16[96,1152]{1,0:T(8,128)(2,1)S(1)}, u32[]{:S(2)}, u32[]{:S(2)}) %collective-permute-start.13) | collective-permute-done | bytes 221216 | tf_op jit(solution)/shard_map/ppermute | solution.py:279
  64.5 0.5 shard_map.91
  65.0 0.1 collective-permute-start.19
  65.1 0.0 copy-done
  65.1 0.0 copy-done.1
  65.1 0.0 copy-done.2
  65.1 1.7 %shard_map.89 = (bf16[128,2048]{1,0:T(8,128)(2,1)}, bf16[128,2048]{1,0:T(8,128)(2,1)}, f32[8,128]{1,0:T(8,128)}) custom-call(s32[8,128]{1,0:T(8,128)S(1)} %bitcast.10, f32[8,128]{1,0:T(8,128)S(1)} %bitcast.12, bf16[128,2048]{1,0:T(8,128)(2,1)S(1)} %copy-done, bf16[4,24,2048]{2,1,0:T(8,128)(2,1)S(1)} %get-tuple-element.43.refs_0_, ...), custom_call_target="tpu_custom_call" | custom-call | flops 201326592 | bytes 3158016 | tf_op jit(solution)/shard_map/pallas_call | solution.py:41
  66.8 0.0 collective-permute-done.20.refs_3_
  66.8 0.2 collective-permute-done.19.refs_2_
  67.1 1.2 %shard_map.94 = bf16[3,256,768]{2,1,0:T(8,128)(2,1)} custom-call(f32[256,1152]{1,0:T(8,128)S(1)} %get-tuple-element.50.refs_0_, f32[256,1152]{1,0:T(8,128)S(1)} %get-tuple-element.51.refs_1_, bf16[256,1152]{1,0:T(8,128)(2,1)S(1)} %collective-permute-done.19.refs_2_, bf16[256,1152]{1,0:T(8,128)(2,1)S(1)} %collective-permute-done.20.refs_3_), custom_call_target="tpu_custom_call" | custom-call | flops 589824 | bytes 4718592 | tf_op jit(solution)/shard_map/pallas_call | solution.py:41
Async XLA Ops:
  2.5 13.0 %collective-permute-start = (bf16[2,24,2048]{2,1,0:T(8,128)(2,1)S(1)}, bf16[2,24,2048]{2,1,0:T(8,128)(2,1)S(1)}, u32[]{:S(2)}, u32[]{:S(2)}) collective-permute-start(bf16[2,24,2048]{2,1,0:T(8,128)(2,1)S(1)} %get-tuple-element.30), channel_id=1, source_target_pairs={{0,1},{1,0},{2,3},{3,2},{4,5},{5,4},{6,7},{7,6},{8,9},{9,8},{10,11... | collective-permute-start | bytes 589832 | tf_op jit(solution)/shard_map/ppermute | solution.py:271
  5.5 10.6 %collective-permute-start.1 = (bf16[2,24,2048]{2,1,0:T(8,128)(2,1)S(1)}, bf16[2,24,2048]{2,1,0:T(8,128)(2,1)S(1)}, u32[]{:S(2)}, u32[]{:S(2)}) collective-permute-start(bf16[2,24,2048]{2,1,0:T(8,128)(2,1)S(1)} %get-tuple-element.31), channel_id=1, source_target_pairs={{0,2},{1,3},{2,0},{3,1},{4,6},{5,7},{6,4},{7,5},{8,10},{9,11},{10,... | collective-permute-start | bytes 589832 | tf_op jit(solution)/shard_map/ppermute | solution.py:271
  7.0 9.1 %collective-permute-start.2 = (bf16[2,24,2048]{2,1,0:T(8,128)(2,1)S(1)}, bf16[2,24,2048]{2,1,0:T(8,128)(2,1)S(1)}, u32[]{:S(2)}, u32[]{:S(2)}) collective-permute-start(bf16[2,24,2048]{2,1,0:T(8,128)(2,1)S(1)} %get-tuple-element.32), channel_id=1, source_target_pairs={{0,3},{1,2},{2,1},{3,0},{4,7},{5,6},{6,5},{7,4},{8,11},{9,10},{10,... | collective-permute-start | bytes 589832 | tf_op jit(solution)/shard_map/ppermute | solution.py:271
  7.1 18.8 %collective-permute-start.3 = (bf16[4,24,1024]{2,1,0:T(8,128)(2,1)S(1)}, bf16[4,24,1024]{2,1,0:T(8,128)(2,1)S(1)}, u32[]{:S(2)}, u32[]{:S(2)}) collective-permute-start(bf16[4,24,1024]{2,1,0:T(8,128)(2,1)S(1)} %get-tuple-element.40), channel_id=1, source_target_pairs={{0,8},{4,12},{8,0},{12,4},{16,24},{20,28},{24,16},{28,20},{1,9},{5... | collective-permute-start | bytes 589832 | tf_op jit(solution)/shard_map/ppermute | solution.py:279
  9.1 16.8 %collective-permute-start.4 = (bf16[4,24,1024]{2,1,0:T(8,128)(2,1)S(1)}, bf16[4,24,1024]{2,1,0:T(8,128)(2,1)S(1)}, u32[]{:S(2)}, u32[]{:S(2)}) collective-permute-start(bf16[4,24,1024]{2,1,0:T(8,128)(2,1)S(1)} %get-tuple-element.41), channel_id=1, source_target_pairs={{0,16},{4,20},{8,24},{12,28},{16,0},{20,4},{24,8},{28,12},{1,17},{... | collective-permute-start | bytes 589832 | tf_op jit(solution)/shard_map/ppermute | solution.py:279
  15.5 10.4 %collective-permute-start.5 = (bf16[4,24,1024]{2,1,0:T(8,128)(2,1)S(1)}, bf16[4,24,1024]{2,1,0:T(8,128)(2,1)S(1)}, u32[]{:S(2)}, u32[]{:S(2)}) collective-permute-start(bf16[4,24,1024]{2,1,0:T(8,128)(2,1)S(1)} %get-tuple-element.42), channel_id=1, source_target_pairs={{0,24},{4,28},{8,16},{12,20},{16,8},{20,12},{24,0},{28,4},{1,25},{... | collective-permute-start | bytes 589832 | tf_op jit(solution)/shard_map/ppermute | solution.py:279
  17.8 14.0 %collective-permute-start.11 = (bf16[96,1152]{1,0:T(8,128)(2,1)S(1)}, bf16[96,1152]{1,0:T(8,128)(2,1)S(1)}, u32[]{:S(2)}, u32[]{:S(2)}) collective-permute-start(bf16[96,1152]{1,0:T(8,128)(2,1)S(1)} %get-tuple-element.33.refs_0_.refs_4_), channel_id=1, source_target_pairs={{8,16},{12,20},{16,8},{20,12},{9,17},{13,21},{17,9},{21,13},{10,18... | collective-permute-start | bytes 663560 | tf_op jit(solution)/shard_map/ppermute | solution.py:279
  18.4 14.9 %collective-permute-start.9 = (bf16[96,1152]{1,0:T(8,128)(2,1)S(1)}, bf16[96,1152]{1,0:T(8,128)(2,1)S(1)}, u32[]{:S(2)}, u32[]{:S(2)}) collective-permute-start(bf16[96,1152]{1,0:T(8,128)(2,1)S(1)} %get-tuple-element.33.refs_0_.refs_4_), channel_id=1, source_target_pairs={{0,8},{4,12},{8,0},{12,4},{16,24},{20,28},{24,16},{28,20},{1,9},{5... | collective-permute-start | bytes 663560 | tf_op jit(solution)/shard_map/ppermute | solution.py:279
  26.0 10.7 %collective-permute-start.6 = (bf16[4,24,2048]{2,1,0:T(8,128)(2,1)S(1)}, bf16[4,24,2048]{2,1,0:T(8,128)(2,1)S(1)}, u32[]{:S(2)}, u32[]{:S(2)}) collective-permute-start(bf16[4,24,2048]{2,1,0:T(8,128)(2,1)S(1)} %get-tuple-element.44), channel_id=1, source_target_pairs={{0,1},{1,0},{2,3},{3,2},{4,5},{5,4},{6,7},{7,6},{8,9},{9,8},{10,11... | collective-permute-start | bytes 1179656 | tf_op jit(solution)/shard_map/ppermute | solution.py:271
  27.3 7.9 %collective-permute-start.14 = (bf16[96,1152]{1,0:T(8,128)(2,1)S(1)}, bf16[96,1152]{1,0:T(8,128)(2,1)S(1)}, u32[]{:S(2)}, u32[]{:S(2)}) collective-permute-start(bf16[96,1152]{1,0:T(8,128)(2,1)S(1)} %get-tuple-element.34.refs_1_.refs_4_), channel_id=1, source_target_pairs={{0,8},{4,12},{8,0},{12,4},{16,24},{20,28},{24,16},{28,20},{1,9},{5... | collective-permute-start | bytes 663560 | tf_op jit(solution)/shard_map/ppermute | solution.py:279
  31.1 4.8 %collective-permute-start.16 = (bf16[96,1152]{1,0:T(8,128)(2,1)S(1)}, bf16[96,1152]{1,0:T(8,128)(2,1)S(1)}, u32[]{:S(2)}, u32[]{:S(2)}) collective-permute-start(bf16[96,1152]{1,0:T(8,128)(2,1)S(1)} %get-tuple-element.34.refs_1_.refs_4_), channel_id=1, source_target_pairs={{8,16},{12,20},{16,8},{20,12},{9,17},{13,21},{17,9},{21,13},{10,18... | collective-permute-start | bytes 663560 | tf_op jit(solution)/shard_map/ppermute | solution.py:279
  31.8 17.7 %collective-permute-start.7 = (bf16[4,24,2048]{2,1,0:T(8,128)(2,1)S(1)}, bf16[4,24,2048]{2,1,0:T(8,128)(2,1)S(1)}, u32[]{:S(2)}, u32[]{:S(2)}) collective-permute-start(bf16[4,24,2048]{2,1,0:T(8,128)(2,1)S(1)} %get-tuple-element.45), channel_id=1, source_target_pairs={{0,2},{1,3},{2,0},{3,1},{4,6},{5,7},{6,4},{7,5},{8,10},{9,11},{10,... | collective-permute-start | bytes 1179656 | tf_op jit(solution)/shard_map/ppermute | solution.py:271
  33.4 21.1 %collective-permute-start.8 = (bf16[4,24,2048]{2,1,0:T(8,128)(2,1)S(1)}, bf16[4,24,2048]{2,1,0:T(8,128)(2,1)S(1)}, u32[]{:S(2)}, u32[]{:S(2)}) collective-permute-start(bf16[4,24,2048]{2,1,0:T(8,128)(2,1)S(1)} %get-tuple-element.46), channel_id=1, source_target_pairs={{0,3},{1,2},{2,1},{3,0},{4,7},{5,6},{6,5},{7,4},{8,11},{9,10},{10,... | collective-permute-start | bytes 1179656 | tf_op jit(solution)/shard_map/ppermute | solution.py:271
  35.2 17.2 %collective-permute-start.15 = (bf16[96,1152]{1,0:T(8,128)(2,1)S(1)}, bf16[96,1152]{1,0:T(8,128)(2,1)S(1)}, u32[]{:S(2)}, u32[]{:S(2)}) collective-permute-start(bf16[96,1152]{1,0:T(8,128)(2,1)S(1)} %collective-permute-done.14.refs_5_), channel_id=1, source_target_pairs={{8,16},{12,20},{16,8},{20,12},{9,17},{13,21},{17,9},{21,13},{10,18... | collective-permute-start | bytes 663560 | tf_op jit(solution)/shard_map/ppermute | solution.py:279
  35.9 16.6 %collective-permute-start.10 = (bf16[96,1152]{1,0:T(8,128)(2,1)S(1)}, bf16[96,1152]{1,0:T(8,128)(2,1)S(1)}, u32[]{:S(2)}, u32[]{:S(2)}) collective-permute-start(bf16[96,1152]{1,0:T(8,128)(2,1)S(1)} %collective-permute-done.9.refs_5_), channel_id=1, source_target_pairs={{8,16},{12,20},{16,8},{20,12},{9,17},{13,21},{17,9},{21,13},{10,18... | collective-permute-start | bytes 663560 | tf_op jit(solution)/shard_map/ppermute | solution.py:279
  36.7 17.8 %collective-permute-start.17 = (bf16[96,1152]{1,0:T(8,128)(2,1)S(1)}, bf16[96,1152]{1,0:T(8,128)(2,1)S(1)}, u32[]{:S(2)}, u32[]{:S(2)}) collective-permute-start(bf16[96,1152]{1,0:T(8,128)(2,1)S(1)} %collective-permute-done.16.refs_5_), channel_id=1, source_target_pairs={{0,8},{4,12},{8,0},{12,4},{16,24},{20,28},{24,16},{28,20},{1,9},{5... | collective-permute-start | bytes 663560 | tf_op jit(solution)/shard_map/ppermute | solution.py:279
  49.5 9.2 %collective-permute-start.12 = (bf16[96,1152]{1,0:T(8,128)(2,1)S(1)}, bf16[96,1152]{1,0:T(8,128)(2,1)S(1)}, u32[]{:S(2)}, u32[]{:S(2)}) collective-permute-start(bf16[96,1152]{1,0:T(8,128)(2,1)S(1)} %collective-permute-done.11.refs_5_), channel_id=1, source_target_pairs={{0,8},{4,12},{8,0},{12,4},{16,24},{20,28},{24,16},{28,20},{1,9},{5... | collective-permute-start | bytes 663560 | tf_op jit(solution)/shard_map/ppermute | solution.py:279
  52.4 9.7 %collective-permute-start.18 = (bf16[96,1152]{1,0:T(8,128)(2,1)S(1)}, bf16[96,1152]{1,0:T(8,128)(2,1)S(1)}, u32[]{:S(2)}, u32[]{:S(2)}) collective-permute-start(bf16[96,1152]{1,0:T(8,128)(2,1)S(1)} %collective-permute-done.15.refs_6_), channel_id=1, source_target_pairs={{0,8},{4,12},{8,0},{12,4},{16,24},{20,28},{24,16},{28,20},{1,9},{5... | collective-permute-start | bytes 663560 | tf_op jit(solution)/shard_map/ppermute | solution.py:279
  52.4 12.1 %collective-permute-start.13 = (bf16[96,1152]{1,0:T(8,128)(2,1)S(1)}, bf16[96,1152]{1,0:T(8,128)(2,1)S(1)}, u32[]{:S(2)}, u32[]{:S(2)}) collective-permute-start(bf16[96,1152]{1,0:T(8,128)(2,1)S(1)} %collective-permute-done.10.refs_6_), channel_id=1, source_target_pairs={{0,8},{4,12},{8,0},{12,4},{16,24},{20,28},{24,16},{28,20},{1,9},{5... | collective-permute-start | bytes 663560 | tf_op jit(solution)/shard_map/ppermute | solution.py:279
  62.6 2.5 %copy-start = (bf16[128,2048]{1,0:T(8,128)(2,1)S(1)}, bf16[128,2048]{1,0:T(8,128)(2,1)}, u32[]{:S(2)}) copy-start(bf16[128,2048]{1,0:T(8,128)(2,1)} %cot_ref.1) | copy-start | bytes 1572868
  62.6 2.5 %copy-start.1 = (s32[128,8]{0,1:T(8,128)S(1)}, s32[128,8]{0,1:T(8,128)}, u32[]{:S(2)}) copy-start(s32[128,8]{0,1:T(8,128)} %param.6) | copy-start | bytes 12292
  62.7 2.5 %copy-start.2 = (f32[128,8]{0,1:T(8,128)S(1)}, f32[128,8]{0,1:T(8,128)}, u32[]{:S(2)}) copy-start(f32[128,8]{0,1:T(8,128)} %param.7) | copy-start | bytes 12292
  62.7 4.2 %collective-permute-start.20 = (bf16[256,1152]{1,0:T(8,128)(2,1)S(1)}, bf16[256,1152]{1,0:T(8,128)(2,1)S(1)}, u32[]{:S(2)}, u32[]{:S(2)}) collective-permute-start(bf16[256,1152]{1,0:T(8,128)(2,1)S(1)} %get-tuple-element.53), channel_id=1, source_target_pairs={{0,4},{4,0},{8,12},{12,8},{16,20},{20,16},{24,28},{28,24},{1,5},{5... | collective-permute-start | bytes 1769480 | tf_op jit(solution)/shard_map/ppermute | solution.py:368
  65.0 2.1 %collective-permute-start.19 = (bf16[256,1152]{1,0:T(8,128)(2,1)S(1)}, bf16[256,1152]{1,0:T(8,128)(2,1)S(1)}, u32[]{:S(2)}, u32[]{:S(2)}) collective-permute-start(bf16[256,1152]{1,0:T(8,128)(2,1)S(1)} %get-tuple-element.52), channel_id=1, source_target_pairs={{0,4},{4,0},{8,12},{12,8},{16,20},{20,16},{24,28},{28,24},{1,5},{5... | collective-permute-start | bytes 1769480 | tf_op jit(solution)/shard_map/ppermute | solution.py:368

commit v3 on v2

--- a/solution.py
+++ b/solution.py
@@ -9,7 +9,8 @@
 
 CAP = 24
 CORES = 2
-PIECES = 2
+PARTS = (9, 9)
+PIECES = len(PARTS)
 SEND_MB = 24
 F32 = jnp.float32
 BF16 = jnp.bfloat16
@@ -23,13 +24,16 @@
     return jax.ShapeDtypeStruct(dims, dtype)
 
 
-def local_call(body, outs, args, flops, scratch=(), megabytes=24, space=VMEM):
+def local_call(
+    body, outs, args, flops, scratch=(), megabytes=24, space=VMEM, out=VMEM, reuse=False
+):
     moved = sum(a.size * a.dtype.itemsize for a in list(args) + list(outs))
     call = pl.pallas_call(
         body,
         out_shape=outs,
-        in_specs=[space] * len(args),
-        out_specs=[VMEM] * len(outs),
+        in_specs=[space] * (len(args) - reuse) + [HBM] * reuse,
+        out_specs=[out] * len(outs),
+        input_output_aliases={len(args) - 1: 0} if reuse else {},
         scratch_shapes=list(scratch),
         compiler_params=pltpu.CompilerParams(vmem_limit_bytes=megabytes << 20),
         cost_estimate=pl.CostEstimate(
@@ -203,17 +207,15 @@
     return message[2 + row, :, at : at + wide]
 
 
-def grad_sums(feats, chips, zs, picks, refs, cut):
+def pick_rows(refs):
+    value = refs[0][...]
+    for more in refs[1:]:
+        value += more[...]
+    return value
+
+
+def contract(rows_f, rows_a, cut):
     lo, hi, hidden = cut
-    rows_f = stack_rows([features_of(f, m, zs) for m in chips for f in feats])
-    acts = []
-    for n in picks:
-        value = refs[0][...]
-        for more in refs[1:n]:
-            value += more[...]
-        acts.append(value)
-        refs = refs[n:]
-    rows_a = acts[0] if len(acts) == 1 else jnp.concatenate(acts, axis=0)
     half = rows_f.shape[1] // 2
     sums = []
     split = min(max(hidden - lo, 0), hi - lo)
@@ -228,6 +230,16 @@
     return sums[0] if len(sums) == 1 else jnp.concatenate(sums, axis=1)
 
 
+def grad_sums(feats, chips, zs, picks, refs, cut):
+    rows_f = stack_rows([features_of(f, m, zs) for m in chips for f in feats])
+    acts = []
+    for n in picks:
+        acts.append(pick_rows(refs[:n]))
+        refs = refs[n:]
+    rows_a = acts[0] if len(acts) == 1 else jnp.concatenate(acts, axis=0)
+    return contract(rows_f, rows_a, cut)
+
+
 def early_grad_kernel(experts, chips, zs, picks, cut, *refs):
     feats, acts, total = refs[:experts], refs[experts:-1], refs[-1]
     total[...] = grad_sums(feats, chips, zs, picks, acts, cut)
@@ -241,16 +253,50 @@
     send[...] = (total[half:] + more[half:]).astype(BF16)
 
 
-def final_kernel(cuts, *refs):
-    n = len(cuts)
-    owns, gots, out = refs[:n], refs[n : 2 * n], refs[-1]
-    hidden = out.shape[2]
-    for k, (lo, hi) in enumerate(cuts):
-        value = (owns[k][...] + gots[k][...].astype(F32)).astype(BF16)
-        for j in range(3):
-            a, b = max(lo, j * hidden), min(hi, (j + 1) * hidden)
-            if a < b:
-                out[(j + 2) % 3, :, a - j * hidden : b - j * hidden] = value[:, a - lo : b - lo]
+def last_early_kernel(experts, chips, zs, picks, cut, *refs):
+    feats, acts, (own, send, feat) = refs[:experts], refs[experts:-3], refs[-3:]
+    total = grad_sums(feats, chips, zs, picks, acts, cut)
+    half = total.shape[0] // CORES
+    own[...] = total[:half]
+    send[...] = total[half:].astype(BF16)
+    rows_f = stack_rows([features_of(f, zs - 1, zs) for f in feats])
+    part = rows_f.shape[1] // 4
+    feat[:, :part] = rows_f[:, part : 2 * part]
+    feat[:, part:] = rows_f[:, 3 * part :]
+
+
+def store_piece(value, cut, held, out, sem):
+    lo, hi, hidden = cut
+    held[...] = value.astype(BF16)
+    copies = []
+    for j in range(3):
+        a, b = max(lo, j * hidden), min(hi, (j + 1) * hidden)
+        if a < b:
+            source = held.at[:, a - lo : b - lo]
+            target = out.at[(j + 2) % 3, :, a - j * hidden : b - j * hidden]
+            copies.append(pltpu.make_async_copy(source, target, sem.at[j]))
+    for copy in copies:
+        copy.start()
+    for copy in copies:
+        copy.wait()
+
+
+def first_store_kernel(cut, own, got, *refs):
+    out, held, sem = refs[-3:]
+    store_piece(own[...] + got[...].astype(F32), cut, held, out, sem)
+
+
+def last_store_kernel(experts, zs, picks, cut, *refs):
+    feats, (own, got, other_feat) = refs[:experts], refs[experts : experts + 3]
+    acts = refs[experts + 3 : experts + 3 + 2 * picks]
+    _, out, held, sem = refs[experts + 3 + 2 * picks :]
+    rows_f = stack_rows([features_of(f, zs - 1, zs) for f in feats])
+    part = rows_f.shape[1] // 4
+    mine = jnp.concatenate([rows_f[:, :part], rows_f[:, 2 * part : 3 * part]], axis=1)
+    rows_f = jnp.concatenate([mine, other_feat[...]], axis=0)
+    rows_a = jnp.concatenate([pick_rows(acts[:picks]), pick_rows(acts[picks:])], axis=0)
+    total = own[...] + got[...].astype(F32) + contract(rows_f, rows_a, cut)
+    store_piece(total, cut, held, out, sem)
 
 
 def per_device(tokens, expert_ids, gate_probs, cotangent, expert_weights):
@@ -310,11 +356,13 @@
     blocks = swap_expert(sent[:experts])
     shares = [sent[experts]] + [swap_z(sent[experts + m], m) for m in range(1, zs)]
 
-    step = 3 * hidden // PIECES
-    cuts = [(k * step, (k + 1) * step) for k in range(PIECES)]
+    unit = 3 * hidden // sum(PARTS)
+    ends = [unit * sum(PARTS[:k]) for k in range(PIECES + 1)]
+    cuts = list(zip(ends[:-1], ends[1:]))
+    steps = [hi - lo for lo, hi in cuts]
     acts = local_call(
         functools.partial(ffn_kernel, experts, cuts),
-        [shape_of((rows, step))] * PIECES,
+        [shape_of((rows, step)) for step in steps],
         [staged, *blocks],
         6 * rows * width * hidden,
     )
@@ -338,41 +386,57 @@
         [ids, probs, cotangent, *back],
         8 * rows * tok_rows * width,
     )
-    owns, gots = [], []
+
+    def swap_core(block):
+        return lax.ppermute(block, "dp", [(i, i ^ 1) for i in range(groups)])
+
+    part = chip_width // CORES
+    grads = None
     for k in range(PIECES):
         cut = (*cuts[k], hidden)
+        step = steps[k]
         pieces = [[acts[k]]] + spread[k][:-1]
-        (total,) = local_call(
-            functools.partial(
-                early_grad_kernel,
-                experts,
-                tuple(range(zs - 1)),
-                zs,
-                tuple(map(len, pieces)),
-                cut,
-            ),
-            [shape_of((chip_width, step), F32)],
-            [*feats, *[a for piece in pieces for a in piece]],
-            2 * (zs - 1) * rows * chip_width * step,
+        counts = tuple(map(len, pieces))
+        pieces = [*feats, *[a for piece in pieces for a in piece]]
+        farthest = spread[k][-1]
+        flops = 2 * rows * chip_width * step
+        body = early_grad_kernel if k + 1 < PIECES else last_early_kernel
+        body = functools.partial(body, experts, tuple(range(zs - 1)), zs, counts, cut)
+        store_scratch = [pltpu.VMEM((part, step), BF16), pltpu.SemaphoreType.DMA((3,))]
+        result = [shape_of((3, part, hidden))]
+        if k + 1 < PIECES:
+            (total,) = local_call(
+                body, [shape_of((chip_width, step), F32)], pieces, (zs - 1) * flops
+            )
+            own, send = local_call(
+                functools.partial(late_grad_kernel, experts, (zs - 1,), zs, (len(farthest),), cut),
+                [shape_of((part, step), F32), shape_of((part, step))],
+                [*feats, total, *farthest],
+                flops,
+            )
+            store = functools.partial(first_store_kernel, cut)
+            inputs = [own, swap_core(send)]
+        else:
+            own, send, feat = local_call(
+                body,
+                [
+                    shape_of((part, step), F32),
+                    shape_of((part, step)),
+                    shape_of((rows, chip_width)),
+                ],
+                pieces,
+                (zs - 1) * flops,
+            )
+            got = swap_core(send)
+            other = swap_core(feat)
+            across = [swap_core(a) for a in farthest]
+            store = functools.partial(last_store_kernel, experts, zs, len(farthest), cut)
+            inputs = [*feats, own, got, other, *farthest, *across]
+        if grads is not None:
+            inputs.append(grads)
+        (grads,) = local_call(
+            store, result, inputs, flops, store_scratch, out=HBM, reuse=grads is not None
         )
-        pieces = spread[k][-1]
-        own, send = local_call(
-            functools.partial(late_grad_kernel, experts, (zs - 1,), zs, (len(pieces),), cut),
-            [
-                shape_of((chip_width // CORES, step), F32),
-                shape_of((chip_width // CORES, step)),
-            ],
-            [*feats, total, *pieces],
-            2 * rows * chip_width * step,
-        )
-        gots.append(lax.ppermute(send, "dp", [(i, i ^ 1) for i in range(groups)]))
-        owns.append(own)
-    (grads,) = local_call(
-        functools.partial(final_kernel, cuts),
-        [shape_of((3, width // groups, hidden))],
-        [*owns, *gots],
-        3 * width * hidden // groups,
-    )
     grad_weights = jnp.transpose(grads, (1, 0, 2))[:, None]
     return mixed, grad_tokens, gates.T, grad_weights
 

time: 68.6 us -> 67.5 us (0.984)
  waiting for transfers between devices: 15.2 us -> 13.9 us
    ppermute x6, waiting for transfers between devices: 5.89 us -> 0.95 us  [swap_expert(): moved[m] = lax.ppermute(blocks[m], 'expert', pairs)]
    ppermute x13, waiting for transfers between devices: 9.05 us -> 12.9 us  [swap_z(): return lax.ppermute(block, 'dp', pairs)]
    ppermute x13, starting transfers between devices: 28.2 us -> 25.2 us  [swap_z(): return lax.ppermute(block, 'dp', pairs)]
    ppermute x6, starting transfers between devices: 7.92 us -> 10.1 us  [swap_expert(): moved[m] = lax.ppermute(blocks[m], 'expert', pairs)]
  transfers between devices with their start and end apart: 21 -> 24, of which waited for: 8 -> 6; matrix products, arithmetic and copies ran while one was open for 0% -> 0% of each run, Pallas kernels for 19% -> 20%
where the time goes in v3:
time: 67.5 us; the launch traced here: 67.3 us
  starting transfers between devices  36.1 us (53%)
  Pallas kernels  16.5 us (24%)
  waiting for transfers between devices  13.9 us (21%)
  between operations  0.87 us (1%)
    ppermute x13, starting transfers between devices, swap_z(): return lax.ppermute(block, 'dp', pairs)  25.2 us
    pallas_call x11, Pallas kernels, local_call(): return call(*args)  16.5 us
    ppermute x13, waiting for transfers between devices, swap_z(): return lax.ppermute(block, 'dp', pairs)  12.9 us
    ppermute x6, starting transfers between devices, swap_expert(): moved[m] = lax.ppermute(blocks[m], 'expert', pairs)  10.1 us
  transfers between devices with their start and end apart: 24, of which 6 were waited for; matrix products, arithmetic and copies ran while one was open for 0% of the time, Pallas kernels for 20%

profile of v3, /device:TPU:0, one launch (start us, length us, event | category | flops | bytes accessed | tf_op | source)
XLA Modules:
  0.0 67.3 jit_solution(6399392977560859902)
XLA Ops:
  0.6 1.8 %shard_map.85 = (bf16[2,24,2048]{2,1,0:T(8,128)(2,1)S(1)}, bf16[2,24,2048]{2,1,0:T(8,128)(2,1)S(1)}, bf16[2,24,2048]{2,1,0:T(8,128)(2,1)S(1)}, bf16[2,24,2048]{2...) custom-call(s32[8,128]{1,0:T(8,128)} %bitcast.9, ...), custom_call_target="tpu_custom_call" | custom-call | flops 100663296 | bytes 2629632 | tf_op jit(solution)/shard_map/pallas_call | solution.py:45
  2.5 3.0 %collective-permute-start = (bf16[2,24,2048]{2,1,0:T(8,128)(2,1)S(1)}, bf16[2,24,2048]{2,1,0:T(8,128)(2,1)S(1)}, u32[]{:S(2)}, u32[]{:S(2)}) collective-permute-start(bf16[2,24,2048]{2,1,0:T(8,128)(2,1)S(1)} %get-tuple-element.31), channel_id=1, source_target_pairs={{0,1},{1,0},{2,3},{3,2},{4,5},{5,4},{6,7},{7,6},{8,9},{9,8},{10,11... | collective-permute-start | bytes 589832 | tf_op jit(solution)/shard_map/ppermute | solution.py:317
  5.5 1.5 %collective-permute-start.1 = (bf16[2,24,2048]{2,1,0:T(8,128)(2,1)S(1)}, bf16[2,24,2048]{2,1,0:T(8,128)(2,1)S(1)}, u32[]{:S(2)}, u32[]{:S(2)}) collective-permute-start(bf16[2,24,2048]{2,1,0:T(8,128)(2,1)S(1)} %get-tuple-element.32), channel_id=1, source_target_pairs={{0,2},{1,3},{2,0},{3,1},{4,6},{5,7},{6,4},{7,5},{8,10},{9,11},{10,... | collective-permute-start | bytes 589832 | tf_op jit(solution)/shard_map/ppermute | solution.py:317
  7.0 0.0 collective-permute-start.2
  7.0 2.0 %collective-permute-start.3 = (bf16[4,24,1024]{2,1,0:T(8,128)(2,1)S(1)}, bf16[4,24,1024]{2,1,0:T(8,128)(2,1)S(1)}, u32[]{:S(2)}, u32[]{:S(2)}) collective-permute-start(bf16[4,24,1024]{2,1,0:T(8,128)(2,1)S(1)} %get-tuple-element.41), channel_id=1, source_target_pairs={{0,8},{4,12},{8,0},{12,4},{16,24},{20,28},{24,16},{28,20},{1,9},{5... | collective-permute-start | bytes 589832 | tf_op jit(solution)/shard_map/ppermute | solution.py:325
  9.1 2.6 %collective-permute-start.4 = (bf16[4,24,1024]{2,1,0:T(8,128)(2,1)S(1)}, bf16[4,24,1024]{2,1,0:T(8,128)(2,1)S(1)}, u32[]{:S(2)}, u32[]{:S(2)}) collective-permute-start(bf16[4,24,1024]{2,1,0:T(8,128)(2,1)S(1)} %get-tuple-element.42), channel_id=1, source_target_pairs={{0,16},{4,20},{8,24},{12,28},{16,0},{20,4},{24,8},{28,12},{1,17},{... | collective-permute-start | bytes 589832 | tf_op jit(solution)/shard_map/ppermute | solution.py:325
  11.7 0.0 collective-permute-done.refs_1_
  11.7 3.7 %collective-permute-start.5 = (bf16[4,24,1024]{2,1,0:T(8,128)(2,1)S(1)}, bf16[4,24,1024]{2,1,0:T(8,128)(2,1)S(1)}, u32[]{:S(2)}, u32[]{:S(2)}) collective-permute-start(bf16[4,24,1024]{2,1,0:T(8,128)(2,1)S(1)} %get-tuple-element.43), channel_id=1, source_target_pairs={{0,24},{4,28},{8,16},{12,20},{16,8},{20,12},{24,0},{28,4},{1,25},{... | collective-permute-start | bytes 589832 | tf_op jit(solution)/shard_map/ppermute | solution.py:325
  15.4 3.8 %shard_map.84.w_ref = bf16[3,2048,768]{2,1,0:T(8,128)(2,1)S(1)} custom-call(bf16[3,2048,768]{2,1,0:T(8,128)(2,1)} %bitcast.13), custom_call_target="tpu_custom_call" | custom-call | bytes 18874368 | tf_op jit(solution)/shard_map/pallas_call | solution.py:45
  19.2 0.0 collective-permute-done.1.refs_2_
  19.2 0.0 collective-permute-done.2.refs_3_
  19.2 1.7 %shard_map.86 = (bf16[96,1152]{1,0:T(8,128)(2,1)S(1)}, bf16[96,1152]{1,0:T(8,128)(2,1)S(1)}) custom-call(bf16[3,2048,768]{2,1,0:T(8,128)(2,1)S(1)} %shard_map.84.w_ref, bf16[2,24,2048]{2,1,0:T(8,128)(2,1)S(1)} %get-tuple-element.30.refs_0_, bf16[2,24,2048]{2,1,0:T(8,128)(2,1)S(1)} %collective-permute-done.refs_1_, ...), custom_call_target="tpu_custom_call" | custom-call | flops 905969664 | bytes 10665984 | tf_op jit(solution)/shard_map/pallas_call | solution.py:45
  20.9 0.7 %collective-permute-start.20 = (bf16[96,1152]{1,0:T(8,128)(2,1)S(1)}, bf16[96,1152]{1,0:T(8,128)(2,1)S(1)}, u32[]{:S(2)}, u32[]{:S(2)}) collective-permute-start(bf16[96,1152]{1,0:T(8,128)(2,1)S(1)} %get-tuple-element.34.refs_0_.refs_4_), channel_id=1, source_target_pairs={{8,16},{12,20},{16,8},{20,12},{9,17},{13,21},{17,9},{21,13},{10,18... | collective-permute-start | bytes 663560 | tf_op jit(solution)/shard_map/ppermute | solution.py:325
  21.6 1.3 %collective-permute-start.18 = (bf16[96,1152]{1,0:T(8,128)(2,1)S(1)}, bf16[96,1152]{1,0:T(8,128)(2,1)S(1)}, u32[]{:S(2)}, u32[]{:S(2)}) collective-permute-start(bf16[96,1152]{1,0:T(8,128)(2,1)S(1)} %get-tuple-element.34.refs_0_.refs_4_), channel_id=1, source_target_pairs={{0,8},{4,12},{8,0},{12,4},{16,24},{20,28},{24,16},{28,20},{1,9},{5... | collective-permute-start | bytes 663560 | tf_op jit(solution)/shard_map/ppermute | solution.py:325
  22.9 0.0 collective-permute-done.3.refs_5_
  22.9 0.7 collective-permute-start.11
  23.6 3.0 %shard_map.87 = (bf16[2,24,2048]{2,1,0:T(8,128)(2,1)S(1)}, bf16[2,24,2048]{2,1,0:T(8,128)(2,1)S(1)}, bf16[2,24,2048]{2,1,0:T(8,128)(2,1)S(1)}, bf16[2,24,2048]{2,1,0:T(8,128)(2,1)S(1)}) custom-call(bf16[3,2048,768]{2,1,0:T(8,128)(2,1)S(1)} %shard_map.84.w_ref, bf16[96,1152]{1,0:T(8,128)(2,1)S(1)} %get-tuple-element.34.refs_0_.refs_4_, ...), custom_call_target="tpu_custom_call" | custom-call | flops 905969664 | bytes 10665984 | tf_op jit(solution)/shard_map/pallas_call | solution.py:45
  26.5 0.0 collective-permute-done.4.refs_6_
  26.5 0.0 collective-permute-done.5.refs_7_
  26.6 0.1 shard_map.88
  26.7 1.5 %collective-permute-start.6 = (bf16[4,24,2048]{2,1,0:T(8,128)(2,1)S(1)}, bf16[4,24,2048]{2,1,0:T(8,128)(2,1)S(1)}, u32[]{:S(2)}, u32[]{:S(2)}) collective-permute-start(bf16[4,24,2048]{2,1,0:T(8,128)(2,1)S(1)} %get-tuple-element.45), channel_id=1, source_target_pairs={{0,1},{1,0},{2,3},{3,2},{4,5},{5,4},{6,7},{7,6},{8,9},{9,8},{10,11... | collective-permute-start | bytes 1179656 | tf_op jit(solution)/shard_map/ppermute | solution.py:317
  28.2 1.5 %collective-permute-start.7 = (bf16[4,24,2048]{2,1,0:T(8,128)(2,1)S(1)}, bf16[4,24,2048]{2,1,0:T(8,128)(2,1)S(1)}, u32[]{:S(2)}, u32[]{:S(2)}) collective-permute-start(bf16[4,24,2048]{2,1,0:T(8,128)(2,1)S(1)} %get-tuple-element.46), channel_id=1, source_target_pairs={{0,2},{1,3},{2,0},{3,1},{4,6},{5,7},{6,4},{7,5},{8,10},{9,11},{10,... | collective-permute-start | bytes 1179656 | tf_op jit(solution)/shard_map/ppermute | solution.py:317
  29.7 0.0 collective-permute-done.20.refs_5_
  29.7 5.9 %collective-permute-start.9 = (bf16[96,1152]{1,0:T(8,128)(2,1)S(1)}, bf16[96,1152]{1,0:T(8,128)(2,1)S(1)}, u32[]{:S(2)}, u32[]{:S(2)}) collective-permute-start(bf16[96,1152]{1,0:T(8,128)(2,1)S(1)} %get-tuple-element.35.refs_1_.refs_4_), channel_id=1, source_target_pairs={{0,8},{4,12},{8,0},{12,4},{16,24},{20,28},{24,16},{28,20},{1,9},{5... | collective-permute-start | bytes 663560 | tf_op jit(solution)/shard_map/ppermute | solution.py:325
  35.6 0.0 collective-permute-done.18.refs_5_
  35.6 0.7 collective-permute-start.19
  36.3 0.0 collective-permute-done.11.refs_7_
  36.3 2.5 %collective-permute-start.8 = (bf16[4,24,2048]{2,1,0:T(8,128)(2,1)S(1)}, bf16[4,24,2048]{2,1,0:T(8,128)(2,1)S(1)}, u32[]{:S(2)}, u32[]{:S(2)}) collective-permute-start(bf16[4,24,2048]{2,1,0:T(8,128)(2,1)S(1)} %get-tuple-element.47), channel_id=1, source_target_pairs={{0,3},{1,2},{2,1},{3,0},{4,7},{5,6},{6,5},{7,4},{8,11},{9,10},{10,... | collective-permute-start | bytes 1179656 | tf_op jit(solution)/shard_map/ppermute | solution.py:317
  38.8 1.0 %collective-permute-done.9.refs_5_ = bf16[96,1152]{1,0:T(8,128)(2,1)S(1)} collective-permute-done((bf16[96,1152]{1,0:T(8,128)(2,1)S(1)}, bf16[96,1152]{1,0:T(8,128)(2,1)S(1)}, u32[]{:S(2)}, u32[]{:S(2)}) %collective-permute-start.9) | collective-permute-done | bytes 221216 | tf_op jit(solution)/shard_map/ppermute | solution.py:325
  39.8 2.8 %collective-permute-start.21 = (bf16[96,1152]{1,0:T(8,128)(2,1)S(1)}, bf16[96,1152]{1,0:T(8,128)(2,1)S(1)}, u32[]{:S(2)}, u32[]{:S(2)}) collective-permute-start(bf16[96,1152]{1,0:T(8,128)(2,1)S(1)} %collective-permute-done.20.refs_5_), channel_id=1, source_target_pairs={{0,8},{4,12},{8,0},{12,4},{16,24},{20,28},{24,16},{28,20},{1,9},{5... | collective-permute-start | bytes 663560 | tf_op jit(solution)/shard_map/ppermute | solution.py:325
  42.6 0.0 collective-permute-done.19.refs_6_
  42.6 0.9 %collective-permute-start.22 = (bf16[96,1152]{1,0:T(8,128)(2,1)S(1)}, bf16[96,1152]{1,0:T(8,128)(2,1)S(1)}, u32[]{:S(2)}, u32[]{:S(2)}) collective-permute-start(bf16[96,1152]{1,0:T(8,128)(2,1)S(1)} %collective-permute-done.19.refs_6_), channel_id=1, source_target_pairs={{0,8},{4,12},{8,0},{12,4},{16,24},{20,28},{24,16},{28,20},{1,9},{5... | collective-permute-start | bytes 663560 | tf_op jit(solution)/shard_map/ppermute | solution.py:325
  43.4 0.0 collective-permute-done.6.refs_1_
  43.4 1.2 %collective-permute-start.12 = (bf16[96,1152]{1,0:T(8,128)(2,1)S(1)}, bf16[96,1152]{1,0:T(8,128)(2,1)S(1)}, u32[]{:S(2)}, u32[]{:S(2)}) collective-permute-start(bf16[96,1152]{1,0:T(8,128)(2,1)S(1)} %collective-permute-done.11.refs_7_), channel_id=1, source_target_pairs={{0,8},{4,12},{8,0},{12,4},{16,24},{20,28},{24,16},{28,20},{1,9},{5... | collective-permute-start | bytes 663560 | tf_op jit(solution)/shard_map/ppermute | solution.py:325
  44.6 0.9 %collective-permute-done.7.refs_2_ = bf16[4,24,2048]{2,1,0:T(8,128)(2,1)S(1)} collective-permute-done((bf16[4,24,2048]{2,1,0:T(8,128)(2,1)S(1)}, bf16[4,24,2048]{2,1,0:T(8,128)(2,1)S(1)}, u32[]{:S(2)}, u32[]{:S(2)}) %collective-permute-start.7) | collective-permute-done | bytes 393248 | tf_op jit(solution)/shard_map/ppermute | solution.py:317
  45.5 0.7 collective-permute-start.10
  46.2 0.0 collective-permute-done.8.refs_3_
  46.2 2.6 %collective-permute-done.21.refs_7_ = bf16[96,1152]{1,0:T(8,128)(2,1)S(1)} collective-permute-done((bf16[96,1152]{1,0:T(8,128)(2,1)S(1)}, bf16[96,1152]{1,0:T(8,128)(2,1)S(1)}, u32[]{:S(2)}, u32[]{:S(2)}) %collective-permute-start.21) | collective-permute-done | bytes 221216 | tf_op jit(solution)/shard_map/ppermute | solution.py:325
  48.9 0.9 %shard_map.91.refs_4_ = f32[512,1152]{1,0:T(8,128)S(1)} custom-call(bf16[4,24,2048]{2,1,0:T(8,128)(2,1)S(1)} %get-tuple-element.44.refs_0_, bf16[4,24,2048]{2,1,0:T(8,128)(2,1)S(1)} %collective-permute-done.6.refs_1_, bf16[4,24,2048]{2,1,0:T(8,128)(2,1)S(1)} %collective-permute-done.7.refs_2_, bf16[4,24,2048]{2,1,0:T(8,128)(2,1)S(1)} %collective-permute-done.8.refs_3_, ...), custom_call_target="tpu_custom_call" | custom-call | flops 339738624 | bytes 4816896 | tf_op jit(solution)/shard_map/pallas_call | solution.py:45
  49.7 1.6 %collective-permute-done.22.refs_6_ = bf16[96,1152]{1,0:T(8,128)(2,1)S(1)} collective-permute-done((bf16[96,1152]{1,0:T(8,128)(2,1)S(1)}, bf16[96,1152]{1,0:T(8,128)(2,1)S(1)}, u32[]{:S(2)}, u32[]{:S(2)}) %collective-permute-start.22) | collective-permute-done | bytes 221216 | tf_op jit(solution)/shard_map/ppermute | solution.py:325
  51.4 0.5 shard_map.92
  51.9 0.0 copy-start
  51.9 0.0 copy-start.1
  51.9 0.0 copy-start.2
  51.9 0.1 collective-permute-start.23
  52.0 1.8 %collective-permute-done.12.refs_7_ = bf16[96,1152]{1,0:T(8,128)(2,1)S(1)} collective-permute-done((bf16[96,1152]{1,0:T(8,128)(2,1)S(1)}, bf16[96,1152]{1,0:T(8,128)(2,1)S(1)}, u32[]{:S(2)}, u32[]{:S(2)}) %collective-permute-start.12) | collective-permute-done | bytes 221216 | tf_op jit(solution)/shard_map/ppermute | solution.py:325
  53.7 0.0 collective-permute-done.10.refs_6_
  53.7 0.9 %shard_map.90 = (f32[256,1152]{1,0:T(8,128)S(1)}, bf16[256,1152]{1,0:T(8,128)(2,1)S(1)}, bf16[96,512]{1,0:T(8,128)(2,1)S(1)}) custom-call(bf16[4,24,2048]{2,1,0:T(8,128)(2,1)S(1)} %get-tuple-element.44.refs_0_, bf16[4,24,2048]{2,1,0:T(8,128)(2,1)S(1)} %collective-permute-done.6.refs_1_, bf16[4,24,2048]{2,1,0:T(8,128)(2,1)S(1)} %collective-permute-done.7.refs_2_, ...), custom_call_target="tpu_custom_call" | custom-call | flops 339738624 | bytes 4325376 | tf_op jit(solution)/shard_map/pallas_call | solution.py:45
  54.6 0.1 collective-permute-start.13
  54.7 2.1 %collective-permute-start.15 = (bf16[96,1152]{1,0:T(8,128)(2,1)S(1)}, bf16[96,1152]{1,0:T(8,128)(2,1)S(1)}, u32[]{:S(2)}, u32[]{:S(2)}) collective-permute-start(bf16[96,1152]{1,0:T(8,128)(2,1)S(1)} %collective-permute-done.10.refs_6_), channel_id=1, source_target_pairs={{0,8},{4,12},{8,0},{12,4},{16,24},{20,28},{24,16},{28,20},{1,9},{5... | collective-permute-start | bytes 663560 | tf_op jit(solution)/shard_map/ppermute | solution.py:325
  56.8 0.2 collective-permute-start.16
  56.9 5.9 %collective-permute-done.15.refs_8_ = bf16[96,1152]{1,0:T(8,128)(2,1)S(1)} collective-permute-done((bf16[96,1152]{1,0:T(8,128)(2,1)S(1)}, bf16[96,1152]{1,0:T(8,128)(2,1)S(1)}, u32[]{:S(2)}, u32[]{:S(2)}) %collective-permute-start.15) | collective-permute-done | bytes 221216 | tf_op jit(solution)/shard_map/ppermute | solution.py:325
  62.8 0.0 collective-permute-start.17
  62.8 0.5 collective-permute-start.14
  63.3 0.0 copy-done
  63.3 0.0 copy-done.1
  63.3 1.7 %shard_map.89 = (bf16[128,2048]{1,0:T(8,128)(2,1)}, bf16[128,2048]{1,0:T(8,128)(2,1)}, f32[8,128]{1,0:T(8,128)}) custom-call(s32[8,128]{1,0:T(8,128)S(1)} %bitcast.10, f32[8,128]{1,0:T(8,128)S(1)} %bitcast.12, bf16[128,2048]{1,0:T(8,128)(2,1)S(1)} %copy-done, bf16[4,24,2048]{2,1,0:T(8,128)(2,1)S(1)} %get-tuple-element.44.refs_0_, ...), custom_call_target="tpu_custom_call" | custom-call | flops 201326592 | bytes 3158016 | tf_op jit(solution)/shard_map/pallas_call | solution.py:45
  65.1 0.0 collective-permute-done.23.got
  65.1 0.9 %shard_map.93.refs_11_ = bf16[3,256,768]{2,1,0:T(8,128)(2,1)} custom-call(f32[256,1152]{1,0:T(8,128)S(1)} %get-tuple-element.54.own, bf16[256,1152]{1,0:T(8,128)(2,1)S(1)} %collective-permute-done.23.got), custom_call_target="tpu_custom_call" | custom-call | flops 113246208 | bytes 2949120 | tf_op jit(solution)/shard_map/pallas_call | solution.py:45
  66.0 0.0 collective-permute-done.16.refs_9_
  66.0 0.0 collective-permute-done.14.refs_6_
  66.0 0.0 collective-permute-done.17.refs_10_
  66.0 0.0 collective-permute-done.13.refs_5_
  66.0 1.2 %shard_map.94 = bf16[3,256,768]{2,1,0:T(8,128)(2,1)} custom-call(bf16[4,24,2048]{2,1,0:T(8,128)(2,1)S(1)} %get-tuple-element.44.refs_0_, bf16[4,24,2048]{2,1,0:T(8,128)(2,1)S(1)} %collective-permute-done.6.refs_1_, bf16[4,24,2048]{2,1,0:T(8,128)(2,1)S(1)} %collective-permute-done.7.refs_2_, ...), custom_call_target="tpu_custom_call", output_to_operand_aliasing={{}: (11, {})} | custom-call | flops 113246208 | bytes 6684672 | tf_op jit(solution)/shard_map/pallas_call | solution.py:45
  (1 shorter events, 0.0 us)
Async XLA Ops:
  2.5 9.2 %collective-permute-start = (bf16[2,24,2048]{2,1,0:T(8,128)(2,1)S(1)}, bf16[2,24,2048]{2,1,0:T(8,128)(2,1)S(1)}, u32[]{:S(2)}, u32[]{:S(2)}) collective-permute-start(bf16[2,24,2048]{2,1,0:T(8,128)(2,1)S(1)} %get-tuple-element.31), channel_id=1, source_target_pairs={{0,1},{1,0},{2,3},{3,2},{4,5},{5,4},{6,7},{7,6},{8,9},{9,8},{10,11... | collective-permute-start | bytes 589832 | tf_op jit(solution)/shard_map/ppermute | solution.py:317
  5.5 13.7 %collective-permute-start.1 = (bf16[2,24,2048]{2,1,0:T(8,128)(2,1)S(1)}, bf16[2,24,2048]{2,1,0:T(8,128)(2,1)S(1)}, u32[]{:S(2)}, u32[]{:S(2)}) collective-permute-start(bf16[2,24,2048]{2,1,0:T(8,128)(2,1)S(1)} %get-tuple-element.32), channel_id=1, source_target_pairs={{0,2},{1,3},{2,0},{3,1},{4,6},{5,7},{6,4},{7,5},{8,10},{9,11},{10,... | collective-permute-start | bytes 589832 | tf_op jit(solution)/shard_map/ppermute | solution.py:317
  7.0 12.2 %collective-permute-start.2 = (bf16[2,24,2048]{2,1,0:T(8,128)(2,1)S(1)}, bf16[2,24,2048]{2,1,0:T(8,128)(2,1)S(1)}, u32[]{:S(2)}, u32[]{:S(2)}) collective-permute-start(bf16[2,24,2048]{2,1,0:T(8,128)(2,1)S(1)} %get-tuple-element.33), channel_id=1, source_target_pairs={{0,3},{1,2},{2,1},{3,0},{4,7},{5,6},{6,5},{7,4},{8,11},{9,10},{10,... | collective-permute-start | bytes 589832 | tf_op jit(solution)/shard_map/ppermute | solution.py:317
  7.0 15.9 %collective-permute-start.3 = (bf16[4,24,1024]{2,1,0:T(8,128)(2,1)S(1)}, bf16[4,24,1024]{2,1,0:T(8,128)(2,1)S(1)}, u32[]{:S(2)}, u32[]{:S(2)}) collective-permute-start(bf16[4,24,1024]{2,1,0:T(8,128)(2,1)S(1)} %get-tuple-element.41), channel_id=1, source_target_pairs={{0,8},{4,12},{8,0},{12,4},{16,24},{20,28},{24,16},{28,20},{1,9},{5... | collective-permute-start | bytes 589832 | tf_op jit(solution)/shard_map/ppermute | solution.py:325
  9.1 17.5 %collective-permute-start.4 = (bf16[4,24,1024]{2,1,0:T(8,128)(2,1)S(1)}, bf16[4,24,1024]{2,1,0:T(8,128)(2,1)S(1)}, u32[]{:S(2)}, u32[]{:S(2)}) collective-permute-start(bf16[4,24,1024]{2,1,0:T(8,128)(2,1)S(1)} %get-tuple-element.42), channel_id=1, source_target_pairs={{0,16},{4,20},{8,24},{12,28},{16,0},{20,4},{24,8},{28,12},{1,17},{... | collective-permute-start | bytes 589832 | tf_op jit(solution)/shard_map/ppermute | solution.py:325
  11.7 14.9 %collective-permute-start.5 = (bf16[4,24,1024]{2,1,0:T(8,128)(2,1)S(1)}, bf16[4,24,1024]{2,1,0:T(8,128)(2,1)S(1)}, u32[]{:S(2)}, u32[]{:S(2)}) collective-permute-start(bf16[4,24,1024]{2,1,0:T(8,128)(2,1)S(1)} %get-tuple-element.43), channel_id=1, source_target_pairs={{0,24},{4,28},{8,16},{12,20},{16,8},{20,12},{24,0},{28,4},{1,25},{... | collective-permute-start | bytes 589832 | tf_op jit(solution)/shard_map/ppermute | solution.py:325
  20.9 8.8 %collective-permute-start.20 = (bf16[96,1152]{1,0:T(8,128)(2,1)S(1)}, bf16[96,1152]{1,0:T(8,128)(2,1)S(1)}, u32[]{:S(2)}, u32[]{:S(2)}) collective-permute-start(bf16[96,1152]{1,0:T(8,128)(2,1)S(1)} %get-tuple-element.34.refs_0_.refs_4_), channel_id=1, source_target_pairs={{8,16},{12,20},{16,8},{20,12},{9,17},{13,21},{17,9},{21,13},{10,18... | collective-permute-start | bytes 663560 | tf_op jit(solution)/shard_map/ppermute | solution.py:325
  21.6 14.0 %collective-permute-start.18 = (bf16[96,1152]{1,0:T(8,128)(2,1)S(1)}, bf16[96,1152]{1,0:T(8,128)(2,1)S(1)}, u32[]{:S(2)}, u32[]{:S(2)}) collective-permute-start(bf16[96,1152]{1,0:T(8,128)(2,1)S(1)} %get-tuple-element.34.refs_0_.refs_4_), channel_id=1, source_target_pairs={{0,8},{4,12},{8,0},{12,4},{16,24},{20,28},{24,16},{28,20},{1,9},{5... | collective-permute-start | bytes 663560 | tf_op jit(solution)/shard_map/ppermute | solution.py:325
  22.9 13.4 %collective-permute-start.11 = (bf16[96,1152]{1,0:T(8,128)(2,1)S(1)}, bf16[96,1152]{1,0:T(8,128)(2,1)S(1)}, u32[]{:S(2)}, u32[]{:S(2)}) collective-permute-start(bf16[96,1152]{1,0:T(8,128)(2,1)S(1)} %get-tuple-element.35.refs_1_.refs_4_), channel_id=1, source_target_pairs={{8,16},{12,20},{16,8},{20,12},{9,17},{13,21},{17,9},{21,13},{10,18... | collective-permute-start | bytes 663560 | tf_op jit(solution)/shard_map/ppermute | solution.py:325
  26.7 16.8 %collective-permute-start.6 = (bf16[4,24,2048]{2,1,0:T(8,128)(2,1)S(1)}, bf16[4,24,2048]{2,1,0:T(8,128)(2,1)S(1)}, u32[]{:S(2)}, u32[]{:S(2)}) collective-permute-start(bf16[4,24,2048]{2,1,0:T(8,128)(2,1)S(1)} %get-tuple-element.45), channel_id=1, source_target_pairs={{0,1},{1,0},{2,3},{3,2},{4,5},{5,4},{6,7},{7,6},{8,9},{9,8},{10,11... | collective-permute-start | bytes 1179656 | tf_op jit(solution)/shard_map/ppermute | solution.py:317
  28.2 17.4 %collective-permute-start.7 = (bf16[4,24,2048]{2,1,0:T(8,128)(2,1)S(1)}, bf16[4,24,2048]{2,1,0:T(8,128)(2,1)S(1)}, u32[]{:S(2)}, u32[]{:S(2)}) collective-permute-start(bf16[4,24,2048]{2,1,0:T(8,128)(2,1)S(1)} %get-tuple-element.46), channel_id=1, source_target_pairs={{0,2},{1,3},{2,0},{3,1},{4,6},{5,7},{6,4},{7,5},{8,10},{9,11},{10,... | collective-permute-start | bytes 1179656 | tf_op jit(solution)/shard_map/ppermute | solution.py:317
  29.7 10.1 %collective-permute-start.9 = (bf16[96,1152]{1,0:T(8,128)(2,1)S(1)}, bf16[96,1152]{1,0:T(8,128)(2,1)S(1)}, u32[]{:S(2)}, u32[]{:S(2)}) collective-permute-start(bf16[96,1152]{1,0:T(8,128)(2,1)S(1)} %get-tuple-element.35.refs_1_.refs_4_), channel_id=1, source_target_pairs={{0,8},{4,12},{8,0},{12,4},{16,24},{20,28},{24,16},{28,20},{1,9},{5... | collective-permute-start | bytes 663560 | tf_op jit(solution)/shard_map/ppermute | solution.py:325
  35.6 7.0 %collective-permute-start.19 = (bf16[96,1152]{1,0:T(8,128)(2,1)S(1)}, bf16[96,1152]{1,0:T(8,128)(2,1)S(1)}, u32[]{:S(2)}, u32[]{:S(2)}) collective-permute-start(bf16[96,1152]{1,0:T(8,128)(2,1)S(1)} %collective-permute-done.18.refs_5_), channel_id=1, source_target_pairs={{8,16},{12,20},{16,8},{20,12},{9,17},{13,21},{17,9},{21,13},{10,18... | collective-permute-start | bytes 663560 | tf_op jit(solution)/shard_map/ppermute | solution.py:325
  36.3 9.9 %collective-permute-start.8 = (bf16[4,24,2048]{2,1,0:T(8,128)(2,1)S(1)}, bf16[4,24,2048]{2,1,0:T(8,128)(2,1)S(1)}, u32[]{:S(2)}, u32[]{:S(2)}) collective-permute-start(bf16[4,24,2048]{2,1,0:T(8,128)(2,1)S(1)} %get-tuple-element.47), channel_id=1, source_target_pairs={{0,3},{1,2},{2,1},{3,0},{4,7},{5,6},{6,5},{7,4},{8,11},{9,10},{10,... | collective-permute-start | bytes 1179656 | tf_op jit(solution)/shard_map/ppermute | solution.py:317
  39.8 9.1 %collective-permute-start.21 = (bf16[96,1152]{1,0:T(8,128)(2,1)S(1)}, bf16[96,1152]{1,0:T(8,128)(2,1)S(1)}, u32[]{:S(2)}, u32[]{:S(2)}) collective-permute-start(bf16[96,1152]{1,0:T(8,128)(2,1)S(1)} %collective-permute-done.20.refs_5_), channel_id=1, source_target_pairs={{0,8},{4,12},{8,0},{12,4},{16,24},{20,28},{24,16},{28,20},{1,9},{5... | collective-permute-start | bytes 663560 | tf_op jit(solution)/shard_map/ppermute | solution.py:325
  42.6 8.8 %collective-permute-start.22 = (bf16[96,1152]{1,0:T(8,128)(2,1)S(1)}, bf16[96,1152]{1,0:T(8,128)(2,1)S(1)}, u32[]{:S(2)}, u32[]{:S(2)}) collective-permute-start(bf16[96,1152]{1,0:T(8,128)(2,1)S(1)} %collective-permute-done.19.refs_6_), channel_id=1, source_target_pairs={{0,8},{4,12},{8,0},{12,4},{16,24},{20,28},{24,16},{28,20},{1,9},{5... | collective-permute-start | bytes 663560 | tf_op jit(solution)/shard_map/ppermute | solution.py:325
  43.4 10.3 %collective-permute-start.12 = (bf16[96,1152]{1,0:T(8,128)(2,1)S(1)}, bf16[96,1152]{1,0:T(8,128)(2,1)S(1)}, u32[]{:S(2)}, u32[]{:S(2)}) collective-permute-start(bf16[96,1152]{1,0:T(8,128)(2,1)S(1)} %collective-permute-done.11.refs_7_), channel_id=1, source_target_pairs={{0,8},{4,12},{8,0},{12,4},{16,24},{20,28},{24,16},{28,20},{1,9},{5... | collective-permute-start | bytes 663560 | tf_op jit(solution)/shard_map/ppermute | solution.py:325
  45.5 8.2 %collective-permute-start.10 = (bf16[96,1152]{1,0:T(8,128)(2,1)S(1)}, bf16[96,1152]{1,0:T(8,128)(2,1)S(1)}, u32[]{:S(2)}, u32[]{:S(2)}) collective-permute-start(bf16[96,1152]{1,0:T(8,128)(2,1)S(1)} %collective-permute-done.9.refs_5_), channel_id=1, source_target_pairs={{8,16},{12,20},{16,8},{20,12},{9,17},{13,21},{17,9},{21,13},{10,18... | collective-permute-start | bytes 663560 | tf_op jit(solution)/shard_map/ppermute | solution.py:325
  51.9 11.5 %copy-start = (bf16[128,2048]{1,0:T(8,128)(2,1)S(1)}, bf16[128,2048]{1,0:T(8,128)(2,1)}, u32[]{:S(2)}) copy-start(bf16[128,2048]{1,0:T(8,128)(2,1)} %cot_ref.1) | copy-start | bytes 1572868
  51.9 11.4 %copy-start.1 = (s32[128,8]{0,1:T(8,128)S(1)}, s32[128,8]{0,1:T(8,128)}, u32[]{:S(2)}) copy-start(s32[128,8]{0,1:T(8,128)} %param.6) | copy-start | bytes 12292
  51.9 11.4 %copy-start.2 = (f32[128,8]{0,1:T(8,128)S(1)}, f32[128,8]{0,1:T(8,128)}, u32[]{:S(2)}) copy-start(f32[128,8]{0,1:T(8,128)} %param.7) | copy-start | bytes 12292
  51.9 13.2 %collective-permute-start.23 = (bf16[256,1152]{1,0:T(8,128)(2,1)S(1)}, bf16[256,1152]{1,0:T(8,128)(2,1)S(1)}, u32[]{:S(2)}, u32[]{:S(2)}) collective-permute-start(bf16[256,1152]{1,0:T(8,128)(2,1)S(1)} %get-tuple-element.55), channel_id=1, source_target_pairs={{0,4},{4,0},{8,12},{12,8},{16,20},{20,16},{24,28},{28,24},{1,5},{5... | collective-permute-start | bytes 1769480 | tf_op jit(solution)/shard_map/ppermute | solution.py:391
  54.6 11.4 %collective-permute-start.13 = (bf16[256,1152]{1,0:T(8,128)(2,1)S(1)}, bf16[256,1152]{1,0:T(8,128)(2,1)S(1)}, u32[]{:S(2)}, u32[]{:S(2)}) collective-permute-start(bf16[256,1152]{1,0:T(8,128)(2,1)S(1)} %get-tuple-element.52), channel_id=1, source_target_pairs={{0,4},{4,0},{8,12},{12,8},{16,20},{20,16},{24,28},{28,24},{1,5},{5... | collective-permute-start | bytes 1769480 | tf_op jit(solution)/shard_map/ppermute | solution.py:391
  54.7 8.1 %collective-permute-start.15 = (bf16[96,1152]{1,0:T(8,128)(2,1)S(1)}, bf16[96,1152]{1,0:T(8,128)(2,1)S(1)}, u32[]{:S(2)}, u32[]{:S(2)}) collective-permute-start(bf16[96,1152]{1,0:T(8,128)(2,1)S(1)} %collective-permute-done.10.refs_6_), channel_id=1, source_target_pairs={{0,8},{4,12},{8,0},{12,4},{16,24},{20,28},{24,16},{28,20},{1,9},{5... | collective-permute-start | bytes 663560 | tf_op jit(solution)/shard_map/ppermute | solution.py:325
  56.8 9.2 %collective-permute-start.16 = (bf16[96,1152]{1,0:T(8,128)(2,1)S(1)}, bf16[96,1152]{1,0:T(8,128)(2,1)S(1)}, u32[]{:S(2)}, u32[]{:S(2)}) collective-permute-start(bf16[96,1152]{1,0:T(8,128)(2,1)S(1)} %collective-permute-done.11.refs_7_), channel_id=1, source_target_pairs={{0,4},{4,0},{8,12},{12,8},{16,20},{20,16},{24,28},{28,24},{1,5},{5... | collective-permute-start | bytes 663560 | tf_op jit(solution)/shard_map/ppermute | solution.py:391
  62.8 3.2 %collective-permute-start.17 = (bf16[96,1152]{1,0:T(8,128)(2,1)S(1)}, bf16[96,1152]{1,0:T(8,128)(2,1)S(1)}, u32[]{:S(2)}, u32[]{:S(2)}) collective-permute-start(bf16[96,1152]{1,0:T(8,128)(2,1)S(1)} %collective-permute-done.15.refs_8_), channel_id=1, source_target_pairs={{0,4},{4,0},{8,12},{12,8},{16,20},{20,16},{24,28},{28,24},{1,5},{5... | collective-permute-start | bytes 663560 | tf_op jit(solution)/shard_map/ppermute | solution.py:391
  62.8 3.2 %collective-permute-start.14 = (bf16[96,512]{1,0:T(8,128)(2,1)S(1)}, bf16[96,512]{1,0:T(8,128)(2,1)S(1)}, u32[]{:S(2)}, u32[]{:S(2)}) collective-permute-start(bf16[96,512]{1,0:T(8,128)(2,1)S(1)} %get-tuple-element.53), channel_id=1, source_target_pairs={{0,4},{4,0},{8,12},{12,8},{16,20},{20,16},{24,28},{28,24},{1,5},{5... | collective-permute-start | bytes 294920 | tf_op jit(solution)/shard_map/ppermute | solution.py:391

commit v4 on v3

--- a/solution.py
+++ b/solution.py
@@ -9,7 +9,7 @@
 
 CAP = 24
 CORES = 2
-PARTS = (9, 9)
+PARTS = (10, 8)
 PIECES = len(PARTS)
 SEND_MB = 24
 F32 = jnp.float32
@@ -90,15 +90,17 @@
     ]
     for copy in copies:
         copy.start()
-    for copy in copies:
+    ids_ref, probs_ref, tok_ref, cot_ref = held
+    for copy in copies[:2]:
         copy.wait()
-    ids_ref, probs_ref, tok_ref, cot_ref = held
     me = lax.axis_index("expert")
     dp = lax.axis_index("dp")
     z, c = dp // CORES, dp % CORES
     onehot, slot_probs = slot_map(ids_ref[...], probs_ref[...], me, experts)
     pick = onehot.astype(BF16)
+    copies[2].wait()
     x_rows = jnp.dot(pick, tok_ref[...], preferred_element_type=F32)
+    copies[3].wait()
     dy_rows = slot_probs * jnp.dot(pick, cot_ref[...], preferred_element_type=F32)
     part = x_rows.shape[1] // (zs * CORES)
     for j, value in enumerate((x_rows, dy_rows)):
@@ -157,9 +159,10 @@
     acts, outs = refs[: len(cuts)], refs[len(cuts) :]
     hidden = w_ref.shape[2]
     hid, gg, ug = (get_columns(acts, cuts, j * hidden, (j + 1) * hidden) for j in range(3))
-    out = lax.dot_general(hid, w_ref[2], NT, preferred_element_type=F32)
-    part = lax.dot_general(gg, w_ref[0], NT, preferred_element_type=F32)
-    part += lax.dot_general(ug, w_ref[1], NT, preferred_element_type=F32)
+    out = lax.dot_general(w_ref[2], hid, NT, preferred_element_type=F32).T
+    part = lax.dot_general(w_ref[0], gg, NT, preferred_element_type=F32)
+    part += lax.dot_general(w_ref[1], ug, NT, preferred_element_type=F32)
+    part = part.T
     for m in range(experts):
         outs[m][0] = out[m * CAP : (m + 1) * CAP].astype(BF16)
         outs[m][1] = part[m * CAP : (m + 1) * CAP].astype(BF16)

time: 67.5 us -> 78.7 us (1.17)
  waiting for transfers between devices: 13.9 us -> 26.4 us
  starting transfers between devices: 36.1 us -> 35.2 us
    ppermute x13, waiting for transfers between devices: 12.9 us -> 23 us  [swap_z(): return lax.ppermute(block, 'dp', pairs)]
    ppermute x6, waiting for transfers between devices: 0.95 us -> 3.44 us  [swap_expert(): moved[m] = lax.ppermute(blocks[m], 'expert', pairs)]
    ppermute x6, starting transfers between devices: 10.1 us -> 8.12 us  [swap_expert(): moved[m] = lax.ppermute(blocks[m], 'expert', pairs)]
    ppermute x13, starting transfers between devices: 25.2 us -> 26.2 us  [swap_z(): return lax.ppermute(block, 'dp', pairs)]
  transfers between devices with their start and end apart: 24 -> 24, of which waited for: 6 -> 7; matrix products, arithmetic and copies ran while one was open for 0% -> 0% of each run, Pallas kernels for 20% -> 17%
where the time goes in v4:
time: 78.7 us; the launch traced here: 78.5 us
  starting transfers between devices  35.2 us (45%)
  waiting for transfers between devices  26.4 us (34%)
  Pallas kernels  16.1 us (20%)
  between operations  0.85 us (1%)
    ppermute x13, starting transfers between devices, swap_z(): return lax.ppermute(block, 'dp', pairs)  26.2 us
    ppermute x13, waiting for transfers between devices, swap_z(): return lax.ppermute(block, 'dp', pairs)  23 us
    pallas_call x11, Pallas kernels, local_call(): return call(*args)  16.1 us
    ppermute x6, starting transfers between devices, swap_expert(): moved[m] = lax.ppermute(blocks[m], 'expert', pairs)  8.12 us
    ppermute x6, waiting for transfers between devices, swap_expert(): moved[m] = lax.ppermute(blocks[m], 'expert', pairs)  3.44 us
  transfers between devices with their start and end apart: 24, of which 7 were waited for; matrix products, arithmetic and copies ran while one was open for 0% of the time, Pallas kernels for 17%

profile of v4, /device:TPU:0, one launch (start us, length us, event | category | flops | bytes accessed | tf_op | source)
XLA Modules:
  0.0 78.5 jit_solution(1709186918329969718)
XLA Ops:
  0.6 1.8 %shard_map.85 = (bf16[2,24,2048]{2,1,0:T(8,128)(2,1)S(1)}, bf16[2,24,2048]{2,1,0:T(8,128)(2,1)S(1)}, bf16[2,24,2048]{2,1,0:T(8,128)(2,1)S(1)}, bf16[2,24,2048]{2...) custom-call(s32[8,128]{1,0:T(8,128)} %bitcast.9, ...), custom_call_target="tpu_custom_call" | custom-call | flops 100663296 | bytes 2629632 | tf_op jit(solution)/shard_map/pallas_call | solution.py:45
  2.5 3.0 %collective-permute-start = (bf16[2,24,2048]{2,1,0:T(8,128)(2,1)S(1)}, bf16[2,24,2048]{2,1,0:T(8,128)(2,1)S(1)}, u32[]{:S(2)}, u32[]{:S(2)}) collective-permute-start(bf16[2,24,2048]{2,1,0:T(8,128)(2,1)S(1)} %get-tuple-element.31), channel_id=1, source_target_pairs={{0,1},{1,0},{2,3},{3,2},{4,5},{5,4},{6,7},{7,6},{8,9},{9,8},{10,11... | collective-permute-start | bytes 589832 | tf_op jit(solution)/shard_map/ppermute | solution.py:320
  5.5 1.5 %collective-permute-start.1 = (bf16[2,24,2048]{2,1,0:T(8,128)(2,1)S(1)}, bf16[2,24,2048]{2,1,0:T(8,128)(2,1)S(1)}, u32[]{:S(2)}, u32[]{:S(2)}) collective-permute-start(bf16[2,24,2048]{2,1,0:T(8,128)(2,1)S(1)} %get-tuple-element.32), channel_id=1, source_target_pairs={{0,2},{1,3},{2,0},{3,1},{4,6},{5,7},{6,4},{7,5},{8,10},{9,11},{10,... | collective-permute-start | bytes 589832 | tf_op jit(solution)/shard_map/ppermute | solution.py:320
  7.0 0.0 collective-permute-start.2
  7.0 2.0 %collective-permute-start.3 = (bf16[4,24,1024]{2,1,0:T(8,128)(2,1)S(1)}, bf16[4,24,1024]{2,1,0:T(8,128)(2,1)S(1)}, u32[]{:S(2)}, u32[]{:S(2)}) collective-permute-start(bf16[4,24,1024]{2,1,0:T(8,128)(2,1)S(1)} %get-tuple-element.41), channel_id=1, source_target_pairs={{0,8},{4,12},{8,0},{12,4},{16,24},{20,28},{24,16},{28,20},{1,9},{5... | collective-permute-start | bytes 589832 | tf_op jit(solution)/shard_map/ppermute | solution.py:328
  9.1 3.8 %shard_map.84.w_ref = bf16[3,2048,768]{2,1,0:T(8,128)(2,1)S(1)} custom-call(bf16[3,2048,768]{2,1,0:T(8,128)(2,1)} %bitcast.13), custom_call_target="tpu_custom_call" | custom-call | bytes 18874368 | tf_op jit(solution)/shard_map/pallas_call | solution.py:45
  12.9 0.0 collective-permute-done.refs_1_
  12.9 3.2 %collective-permute-done.1.refs_2_ = bf16[2,24,2048]{2,1,0:T(8,128)(2,1)S(1)} collective-permute-done((bf16[2,24,2048]{2,1,0:T(8,128)(2,1)S(1)}, bf16[2,24,2048]{2,1,0:T(8,128)(2,1)S(1)}, u32[]{:S(2)}, u32[]{:S(2)}) %collective-permute-start.1) | collective-permute-done | bytes 196640 | tf_op jit(solution)/shard_map/ppermute | solution.py:320
  16.1 0.0 collective-permute-done.2.refs_3_
  16.1 1.7 %shard_map.86 = (bf16[96,1280]{1,0:T(8,128)(2,1)S(1)}, bf16[96,1024]{1,0:T(8,128)(2,1)S(1)}) custom-call(bf16[3,2048,768]{2,1,0:T(8,128)(2,1)S(1)} %shard_map.84.w_ref, bf16[2,24,2048]{2,1,0:T(8,128)(2,1)S(1)} %get-tuple-element.30.refs_0_, bf16[2,24,2048]{2,1,0:T(8,128)(2,1)S(1)} %collective-permute-done.refs_1_, ...), custom_call_target="tpu_custom_call" | custom-call | flops 905969664 | bytes 10665984 | tf_op jit(solution)/shard_map/pallas_call | solution.py:45
  17.8 1.6 %collective-permute-start.18 = (bf16[96,1280]{1,0:T(8,128)(2,1)S(1)}, bf16[96,1280]{1,0:T(8,128)(2,1)S(1)}, u32[]{:S(2)}, u32[]{:S(2)}) collective-permute-start(bf16[96,1280]{1,0:T(8,128)(2,1)S(1)} %get-tuple-element.34.refs_0_.refs_4_), channel_id=1, source_target_pairs={{0,8},{4,12},{8,0},{12,4},{16,24},{20,28},{24,16},{28,20},{1,9},{5... | collective-permute-start | bytes 737288 | tf_op jit(solution)/shard_map/ppermute | solution.py:328
  19.4 2.6 %collective-permute-start.4 = (bf16[4,24,1024]{2,1,0:T(8,128)(2,1)S(1)}, bf16[4,24,1024]{2,1,0:T(8,128)(2,1)S(1)}, u32[]{:S(2)}, u32[]{:S(2)}) collective-permute-start(bf16[4,24,1024]{2,1,0:T(8,128)(2,1)S(1)} %get-tuple-element.42), channel_id=1, source_target_pairs={{0,16},{4,20},{8,24},{12,28},{16,0},{20,4},{24,8},{28,12},{1,17},{... | collective-permute-start | bytes 589832 | tf_op jit(solution)/shard_map/ppermute | solution.py:328
  22.0 0.2 collective-permute-start.5
  22.2 0.7 collective-permute-start.11
  22.9 0.0 collective-permute-done.3.refs_5_
  22.9 3.5 %collective-permute-start.9 = (bf16[96,1024]{1,0:T(8,128)(2,1)S(1)}, bf16[96,1024]{1,0:T(8,128)(2,1)S(1)}, u32[]{:S(2)}, u32[]{:S(2)}) collective-permute-start(bf16[96,1024]{1,0:T(8,128)(2,1)S(1)} %get-tuple-element.35.refs_1_.refs_4_), channel_id=1, source_target_pairs={{0,8},{4,12},{8,0},{12,4},{16,24},{20,28},{24,16},{28,20},{1,9},{5... | collective-permute-start | bytes 589832 | tf_op jit(solution)/shard_map/ppermute | solution.py:328
  26.4 9.4 %collective-permute-done.4.refs_6_ = bf16[4,24,1024]{2,1,0:T(8,128)(2,1)S(1)} collective-permute-done((bf16[4,24,1024]{2,1,0:T(8,128)(2,1)S(1)}, bf16[4,24,1024]{2,1,0:T(8,128)(2,1)S(1)}, u32[]{:S(2)}, u32[]{:S(2)}) %collective-permute-start.4) | collective-permute-done | bytes 196640 | tf_op jit(solution)/shard_map/ppermute | solution.py:328
  35.9 0.7 collective-permute-start.20
  36.5 0.0 collective-permute-done.18.refs_5_
  36.5 0.7 collective-permute-start.19
  37.2 2.7 %shard_map.87 = (bf16[2,24,2048]{2,1,0:T(8,128)(2,1)S(1)}, bf16[2,24,2048]{2,1,0:T(8,128)(2,1)S(1)}, bf16[2,24,2048]{2,1,0:T(8,128)(2,1)S(1)}, bf16[2,24,2048]{2,1,0:T(8,128)(2,1)S(1)}) custom-call(bf16[3,2048,768]{2,1,0:T(8,128)(2,1)S(1)} %shard_map.84.w_ref, bf16[96,1280]{1,0:T(8,128)(2,1)S(1)} %get-tuple-element.34.refs_0_.refs_4_, ...), custom_call_target="tpu_custom_call" | custom-call | flops 905969664 | bytes 10665984 | tf_op jit(solution)/shard_map/pallas_call | solution.py:45
  39.9 0.0 collective-permute-done.5.refs_7_
  40.0 0.1 shard_map.88
  40.1 1.3 %collective-permute-start.6 = (bf16[4,24,2048]{2,1,0:T(8,128)(2,1)S(1)}, bf16[4,24,2048]{2,1,0:T(8,128)(2,1)S(1)}, u32[]{:S(2)}, u32[]{:S(2)}) collective-permute-start(bf16[4,24,2048]{2,1,0:T(8,128)(2,1)S(1)} %get-tuple-element.45), channel_id=1, source_target_pairs={{0,1},{1,0},{2,3},{3,2},{4,5},{5,4},{6,7},{7,6},{8,9},{9,8},{10,11... | collective-permute-start | bytes 1179656 | tf_op jit(solution)/shard_map/ppermute | solution.py:320
  41.4 0.0 collective-permute-done.11.refs_7_
  41.4 0.8 %collective-permute-start.7 = (bf16[4,24,2048]{2,1,0:T(8,128)(2,1)S(1)}, bf16[4,24,2048]{2,1,0:T(8,128)(2,1)S(1)}, u32[]{:S(2)}, u32[]{:S(2)}) collective-permute-start(bf16[4,24,2048]{2,1,0:T(8,128)(2,1)S(1)} %get-tuple-element.46), channel_id=1, source_target_pairs={{0,2},{1,3},{2,0},{3,1},{4,6},{5,7},{6,4},{7,5},{8,10},{9,11},{10,... | collective-permute-start | bytes 1179656 | tf_op jit(solution)/shard_map/ppermute | solution.py:320
  42.2 0.0 collective-permute-done.9.refs_5_
  42.2 1.4 %collective-permute-start.8 = (bf16[4,24,2048]{2,1,0:T(8,128)(2,1)S(1)}, bf16[4,24,2048]{2,1,0:T(8,128)(2,1)S(1)}, u32[]{:S(2)}, u32[]{:S(2)}) collective-permute-start(bf16[4,24,2048]{2,1,0:T(8,128)(2,1)S(1)} %get-tuple-element.47), channel_id=1, source_target_pairs={{0,3},{1,2},{2,1},{3,0},{4,7},{5,6},{6,5},{7,4},{8,11},{9,10},{10,... | collective-permute-start | bytes 1179656 | tf_op jit(solution)/shard_map/ppermute | solution.py:320
  43.6 0.0 collective-permute-done.20.refs_5_
  43.6 7.1 %collective-permute-start.21 = (bf16[96,1280]{1,0:T(8,128)(2,1)S(1)}, bf16[96,1280]{1,0:T(8,128)(2,1)S(1)}, u32[]{:S(2)}, u32[]{:S(2)}) collective-permute-start(bf16[96,1280]{1,0:T(8,128)(2,1)S(1)} %collective-permute-done.20.refs_5_), channel_id=1, source_target_pairs={{0,8},{4,12},{8,0},{12,4},{16,24},{20,28},{24,16},{28,20},{1,9},{5... | collective-permute-start | bytes 737288 | tf_op jit(solution)/shard_map/ppermute | solution.py:328
  50.8 0.0 collective-permute-done.19.refs_6_
  50.8 2.8 %collective-permute-start.22 = (bf16[96,1280]{1,0:T(8,128)(2,1)S(1)}, bf16[96,1280]{1,0:T(8,128)(2,1)S(1)}, u32[]{:S(2)}, u32[]{:S(2)}) collective-permute-start(bf16[96,1280]{1,0:T(8,128)(2,1)S(1)} %collective-permute-done.19.refs_6_), channel_id=1, source_target_pairs={{0,8},{4,12},{8,0},{12,4},{16,24},{20,28},{24,16},{28,20},{1,9},{5... | collective-permute-start | bytes 737288 | tf_op jit(solution)/shard_map/ppermute | solution.py:328
  53.6 0.0 collective-permute-done.6.refs_1_
  53.6 0.0 collective-permute-start.12
  53.6 0.2 collective-permute-done.7.refs_2_
  53.8 0.7 collective-permute-start.10
  54.5 0.0 collective-permute-done.8.refs_3_
  54.5 3.0 %collective-permute-done.21.refs_7_ = bf16[96,1280]{1,0:T(8,128)(2,1)S(1)} collective-permute-done((bf16[96,1280]{1,0:T(8,128)(2,1)S(1)}, bf16[96,1280]{1,0:T(8,128)(2,1)S(1)}, u32[]{:S(2)}, u32[]{:S(2)}) %collective-permute-start.21) | collective-permute-done | bytes 245792 | tf_op jit(solution)/shard_map/ppermute | solution.py:328
  57.6 0.9 %shard_map.91.refs_4_ = f32[512,1280]{1,0:T(8,128)S(1)} custom-call(bf16[4,24,2048]{2,1,0:T(8,128)(2,1)S(1)} %get-tuple-element.44.refs_0_, bf16[4,24,2048]{2,1,0:T(8,128)(2,1)S(1)} %collective-permute-done.6.refs_1_, bf16[4,24,2048]{2,1,0:T(8,128)(2,1)S(1)} %collective-permute-done.7.refs_2_, bf16[4,24,2048]{2,1,0:T(8,128)(2,1)S(1)} %collective-permute-done.8.refs_3_, ...), custom_call_target="tpu_custom_call" | custom-call | flops 377487360 | bytes 5177344 | tf_op jit(solution)/shard_map/pallas_call | solution.py:45
  58.5 0.0 copy-start
  58.5 0.0 copy-start.1
  58.5 0.0 copy-start.2
  58.5 3.6 %collective-permute-done.22.refs_6_ = bf16[96,1280]{1,0:T(8,128)(2,1)S(1)} collective-permute-done((bf16[96,1280]{1,0:T(8,128)(2,1)S(1)}, bf16[96,1280]{1,0:T(8,128)(2,1)S(1)}, u32[]{:S(2)}, u32[]{:S(2)}) %collective-permute-start.22) | collective-permute-done | bytes 245792 | tf_op jit(solution)/shard_map/ppermute | solution.py:328
  62.1 0.5 shard_map.92
  62.6 0.1 collective-permute-start.23
  62.7 1.5 %collective-permute-done.12.refs_7_ = bf16[96,1024]{1,0:T(8,128)(2,1)S(1)} collective-permute-done((bf16[96,1024]{1,0:T(8,128)(2,1)S(1)}, bf16[96,1024]{1,0:T(8,128)(2,1)S(1)}, u32[]{:S(2)}, u32[]{:S(2)}) %collective-permute-start.12) | collective-permute-done | bytes 196640 | tf_op jit(solution)/shard_map/ppermute | solution.py:328
  64.2 0.0 collective-permute-done.10.refs_6_
  64.2 0.7 shard_map.90
  65.0 0.1 collective-permute-start.13
  65.0 3.6 %collective-permute-start.15 = (bf16[96,1024]{1,0:T(8,128)(2,1)S(1)}, bf16[96,1024]{1,0:T(8,128)(2,1)S(1)}, u32[]{:S(2)}, u32[]{:S(2)}) collective-permute-start(bf16[96,1024]{1,0:T(8,128)(2,1)S(1)} %collective-permute-done.10.refs_6_), channel_id=1, source_target_pairs={{0,8},{4,12},{8,0},{12,4},{16,24},{20,28},{24,16},{28,20},{1,9},{5... | collective-permute-start | bytes 589832 | tf_op jit(solution)/shard_map/ppermute | solution.py:328
  68.6 0.2 collective-permute-start.16
  68.8 5.3 %collective-permute-done.15.refs_8_ = bf16[96,1024]{1,0:T(8,128)(2,1)S(1)} collective-permute-done((bf16[96,1024]{1,0:T(8,128)(2,1)S(1)}, bf16[96,1024]{1,0:T(8,128)(2,1)S(1)}, u32[]{:S(2)}, u32[]{:S(2)}) %collective-permute-start.15) | collective-permute-done | bytes 196640 | tf_op jit(solution)/shard_map/ppermute | solution.py:328
  74.1 0.0 collective-permute-start.17
  74.1 0.5 collective-permute-start.14
  74.6 0.0 copy-done
  74.6 0.0 copy-done.1
  74.6 1.7 %shard_map.89 = (bf16[128,2048]{1,0:T(8,128)(2,1)}, bf16[128,2048]{1,0:T(8,128)(2,1)}, f32[8,128]{1,0:T(8,128)}) custom-call(s32[8,128]{1,0:T(8,128)S(1)} %bitcast.10, f32[8,128]{1,0:T(8,128)S(1)} %bitcast.12, bf16[128,2048]{1,0:T(8,128)(2,1)S(1)} %copy-done, bf16[4,24,2048]{2,1,0:T(8,128)(2,1)S(1)} %get-tuple-element.44.refs_0_, ...), custom_call_target="tpu_custom_call" | custom-call | flops 201326592 | bytes 3158016 | tf_op jit(solution)/shard_map/pallas_call | solution.py:45
  76.3 0.0 collective-permute-done.23.got
  76.3 1.0 %shard_map.93.refs_11_ = bf16[3,256,768]{2,1,0:T(8,128)(2,1)} custom-call(f32[256,1280]{1,0:T(8,128)S(1)} %get-tuple-element.54.own, bf16[256,1280]{1,0:T(8,128)(2,1)S(1)} %collective-permute-done.23.got), custom_call_target="tpu_custom_call" | custom-call | flops 125829120 | bytes 3145728 | tf_op jit(solution)/shard_map/pallas_call | solution.py:45
  77.3 0.0 collective-permute-done.16.refs_9_
  77.3 0.0 collective-permute-done.14.refs_6_
  77.3 0.0 collective-permute-done.17.refs_10_
  77.3 0.0 collective-permute-done.13.refs_5_
  77.4 1.1 %shard_map.94 = bf16[3,256,768]{2,1,0:T(8,128)(2,1)} custom-call(bf16[4,24,2048]{2,1,0:T(8,128)(2,1)S(1)} %get-tuple-element.44.refs_0_, bf16[4,24,2048]{2,1,0:T(8,128)(2,1)S(1)} %collective-permute-done.6.refs_1_, bf16[4,24,2048]{2,1,0:T(8,128)(2,1)S(1)} %collective-permute-done.7.refs_2_, ...), custom_call_target="tpu_custom_call", output_to_operand_aliasing={{}: (11, {})} | custom-call | flops 100663296 | bytes 6389760 | tf_op jit(solution)/shard_map/pallas_call | solution.py:45
  (1 shorter events, 0.0 us)
Async XLA Ops:
  2.5 10.4 %collective-permute-start = (bf16[2,24,2048]{2,1,0:T(8,128)(2,1)S(1)}, bf16[2,24,2048]{2,1,0:T(8,128)(2,1)S(1)}, u32[]{:S(2)}, u32[]{:S(2)}) collective-permute-start(bf16[2,24,2048]{2,1,0:T(8,128)(2,1)S(1)} %get-tuple-element.31), channel_id=1, source_target_pairs={{0,1},{1,0},{2,3},{3,2},{4,5},{5,4},{6,7},{7,6},{8,9},{9,8},{10,11... | collective-permute-start | bytes 589832 | tf_op jit(solution)/shard_map/ppermute | solution.py:320
  5.5 10.6 %collective-permute-start.1 = (bf16[2,24,2048]{2,1,0:T(8,128)(2,1)S(1)}, bf16[2,24,2048]{2,1,0:T(8,128)(2,1)S(1)}, u32[]{:S(2)}, u32[]{:S(2)}) collective-permute-start(bf16[2,24,2048]{2,1,0:T(8,128)(2,1)S(1)} %get-tuple-element.32), channel_id=1, source_target_pairs={{0,2},{1,3},{2,0},{3,1},{4,6},{5,7},{6,4},{7,5},{8,10},{9,11},{10,... | collective-permute-start | bytes 589832 | tf_op jit(solution)/shard_map/ppermute | solution.py:320
  7.0 9.1 %collective-permute-start.2 = (bf16[2,24,2048]{2,1,0:T(8,128)(2,1)S(1)}, bf16[2,24,2048]{2,1,0:T(8,128)(2,1)S(1)}, u32[]{:S(2)}, u32[]{:S(2)}) collective-permute-start(bf16[2,24,2048]{2,1,0:T(8,128)(2,1)S(1)} %get-tuple-element.33), channel_id=1, source_target_pairs={{0,3},{1,2},{2,1},{3,0},{4,7},{5,6},{6,5},{7,4},{8,11},{9,10},{10,... | collective-permute-start | bytes 589832 | tf_op jit(solution)/shard_map/ppermute | solution.py:320
  7.0 15.8 %collective-permute-start.3 = (bf16[4,24,1024]{2,1,0:T(8,128)(2,1)S(1)}, bf16[4,24,1024]{2,1,0:T(8,128)(2,1)S(1)}, u32[]{:S(2)}, u32[]{:S(2)}) collective-permute-start(bf16[4,24,1024]{2,1,0:T(8,128)(2,1)S(1)} %get-tuple-element.41), channel_id=1, source_target_pairs={{0,8},{4,12},{8,0},{12,4},{16,24},{20,28},{24,16},{28,20},{1,9},{5... | collective-permute-start | bytes 589832 | tf_op jit(solution)/shard_map/ppermute | solution.py:328
  17.8 18.8 %collective-permute-start.18 = (bf16[96,1280]{1,0:T(8,128)(2,1)S(1)}, bf16[96,1280]{1,0:T(8,128)(2,1)S(1)}, u32[]{:S(2)}, u32[]{:S(2)}) collective-permute-start(bf16[96,1280]{1,0:T(8,128)(2,1)S(1)} %get-tuple-element.34.refs_0_.refs_4_), channel_id=1, source_target_pairs={{0,8},{4,12},{8,0},{12,4},{16,24},{20,28},{24,16},{28,20},{1,9},{5... | collective-permute-start | bytes 737288 | tf_op jit(solution)/shard_map/ppermute | solution.py:328
  19.4 16.5 %collective-permute-start.4 = (bf16[4,24,1024]{2,1,0:T(8,128)(2,1)S(1)}, bf16[4,24,1024]{2,1,0:T(8,128)(2,1)S(1)}, u32[]{:S(2)}, u32[]{:S(2)}) collective-permute-start(bf16[4,24,1024]{2,1,0:T(8,128)(2,1)S(1)} %get-tuple-element.42), channel_id=1, source_target_pairs={{0,16},{4,20},{8,24},{12,28},{16,0},{20,4},{24,8},{28,12},{1,17},{... | collective-permute-start | bytes 589832 | tf_op jit(solution)/shard_map/ppermute | solution.py:328
  22.0 18.0 %collective-permute-start.5 = (bf16[4,24,1024]{2,1,0:T(8,128)(2,1)S(1)}, bf16[4,24,1024]{2,1,0:T(8,128)(2,1)S(1)}, u32[]{:S(2)}, u32[]{:S(2)}) collective-permute-start(bf16[4,24,1024]{2,1,0:T(8,128)(2,1)S(1)} %get-tuple-element.43), channel_id=1, source_target_pairs={{0,24},{4,28},{8,16},{12,20},{16,8},{20,12},{24,0},{28,4},{1,25},{... | collective-permute-start | bytes 589832 | tf_op jit(solution)/shard_map/ppermute | solution.py:328
  22.2 19.1 %collective-permute-start.11 = (bf16[96,1024]{1,0:T(8,128)(2,1)S(1)}, bf16[96,1024]{1,0:T(8,128)(2,1)S(1)}, u32[]{:S(2)}, u32[]{:S(2)}) collective-permute-start(bf16[96,1024]{1,0:T(8,128)(2,1)S(1)} %get-tuple-element.35.refs_1_.refs_4_), channel_id=1, source_target_pairs={{8,16},{12,20},{16,8},{20,12},{9,17},{13,21},{17,9},{21,13},{10,18... | collective-permute-start | bytes 589832 | tf_op jit(solution)/shard_map/ppermute | solution.py:328
  22.9 19.3 %collective-permute-start.9 = (bf16[96,1024]{1,0:T(8,128)(2,1)S(1)}, bf16[96,1024]{1,0:T(8,128)(2,1)S(1)}, u32[]{:S(2)}, u32[]{:S(2)}) collective-permute-start(bf16[96,1024]{1,0:T(8,128)(2,1)S(1)} %get-tuple-element.35.refs_1_.refs_4_), channel_id=1, source_target_pairs={{0,8},{4,12},{8,0},{12,4},{16,24},{20,28},{24,16},{28,20},{1,9},{5... | collective-permute-start | bytes 589832 | tf_op jit(solution)/shard_map/ppermute | solution.py:328
  35.9 7.8 %collective-permute-start.20 = (bf16[96,1280]{1,0:T(8,128)(2,1)S(1)}, bf16[96,1280]{1,0:T(8,128)(2,1)S(1)}, u32[]{:S(2)}, u32[]{:S(2)}) collective-permute-start(bf16[96,1280]{1,0:T(8,128)(2,1)S(1)} %get-tuple-element.34.refs_0_.refs_4_), channel_id=1, source_target_pairs={{8,16},{12,20},{16,8},{20,12},{9,17},{13,21},{17,9},{21,13},{10,18... | collective-permute-start | bytes 737288 | tf_op jit(solution)/shard_map/ppermute | solution.py:328
  36.5 14.2 %collective-permute-start.19 = (bf16[96,1280]{1,0:T(8,128)(2,1)S(1)}, bf16[96,1280]{1,0:T(8,128)(2,1)S(1)}, u32[]{:S(2)}, u32[]{:S(2)}) collective-permute-start(bf16[96,1280]{1,0:T(8,128)(2,1)S(1)} %collective-permute-done.18.refs_5_), channel_id=1, source_target_pairs={{8,16},{12,20},{16,8},{20,12},{9,17},{13,21},{17,9},{21,13},{10,18... | collective-permute-start | bytes 737288 | tf_op jit(solution)/shard_map/ppermute | solution.py:328
  40.1 13.5 %collective-permute-start.6 = (bf16[4,24,2048]{2,1,0:T(8,128)(2,1)S(1)}, bf16[4,24,2048]{2,1,0:T(8,128)(2,1)S(1)}, u32[]{:S(2)}, u32[]{:S(2)}) collective-permute-start(bf16[4,24,2048]{2,1,0:T(8,128)(2,1)S(1)} %get-tuple-element.45), channel_id=1, source_target_pairs={{0,1},{1,0},{2,3},{3,2},{4,5},{5,4},{6,7},{7,6},{8,9},{9,8},{10,11... | collective-permute-start | bytes 1179656 | tf_op jit(solution)/shard_map/ppermute | solution.py:320
  41.4 12.5 %collective-permute-start.7 = (bf16[4,24,2048]{2,1,0:T(8,128)(2,1)S(1)}, bf16[4,24,2048]{2,1,0:T(8,128)(2,1)S(1)}, u32[]{:S(2)}, u32[]{:S(2)}) collective-permute-start(bf16[4,24,2048]{2,1,0:T(8,128)(2,1)S(1)} %get-tuple-element.46), channel_id=1, source_target_pairs={{0,2},{1,3},{2,0},{3,1},{4,6},{5,7},{6,4},{7,5},{8,10},{9,11},{10,... | collective-permute-start | bytes 1179656 | tf_op jit(solution)/shard_map/ppermute | solution.py:320
  42.2 12.3 %collective-permute-start.8 = (bf16[4,24,2048]{2,1,0:T(8,128)(2,1)S(1)}, bf16[4,24,2048]{2,1,0:T(8,128)(2,1)S(1)}, u32[]{:S(2)}, u32[]{:S(2)}) collective-permute-start(bf16[4,24,2048]{2,1,0:T(8,128)(2,1)S(1)} %get-tuple-element.47), channel_id=1, source_target_pairs={{0,3},{1,2},{2,1},{3,0},{4,7},{5,6},{6,5},{7,4},{8,11},{9,10},{10,... | collective-permute-start | bytes 1179656 | tf_op jit(solution)/shard_map/ppermute | solution.py:320
  43.6 13.9 %collective-permute-start.21 = (bf16[96,1280]{1,0:T(8,128)(2,1)S(1)}, bf16[96,1280]{1,0:T(8,128)(2,1)S(1)}, u32[]{:S(2)}, u32[]{:S(2)}) collective-permute-start(bf16[96,1280]{1,0:T(8,128)(2,1)S(1)} %collective-permute-done.20.refs_5_), channel_id=1, source_target_pairs={{0,8},{4,12},{8,0},{12,4},{16,24},{20,28},{24,16},{28,20},{1,9},{5... | collective-permute-start | bytes 737288 | tf_op jit(solution)/shard_map/ppermute | solution.py:328
  50.8 11.3 %collective-permute-start.22 = (bf16[96,1280]{1,0:T(8,128)(2,1)S(1)}, bf16[96,1280]{1,0:T(8,128)(2,1)S(1)}, u32[]{:S(2)}, u32[]{:S(2)}) collective-permute-start(bf16[96,1280]{1,0:T(8,128)(2,1)S(1)} %collective-permute-done.19.refs_6_), channel_id=1, source_target_pairs={{0,8},{4,12},{8,0},{12,4},{16,24},{20,28},{24,16},{28,20},{1,9},{5... | collective-permute-start | bytes 737288 | tf_op jit(solution)/shard_map/ppermute | solution.py:328
  53.6 10.6 %collective-permute-start.12 = (bf16[96,1024]{1,0:T(8,128)(2,1)S(1)}, bf16[96,1024]{1,0:T(8,128)(2,1)S(1)}, u32[]{:S(2)}, u32[]{:S(2)}) collective-permute-start(bf16[96,1024]{1,0:T(8,128)(2,1)S(1)} %collective-permute-done.11.refs_7_), channel_id=1, source_target_pairs={{0,8},{4,12},{8,0},{12,4},{16,24},{20,28},{24,16},{28,20},{1,9},{5... | collective-permute-start | bytes 589832 | tf_op jit(solution)/shard_map/ppermute | solution.py:328
  53.8 10.4 %collective-permute-start.10 = (bf16[96,1024]{1,0:T(8,128)(2,1)S(1)}, bf16[96,1024]{1,0:T(8,128)(2,1)S(1)}, u32[]{:S(2)}, u32[]{:S(2)}) collective-permute-start(bf16[96,1024]{1,0:T(8,128)(2,1)S(1)} %collective-permute-done.9.refs_5_), channel_id=1, source_target_pairs={{8,16},{12,20},{16,8},{20,12},{9,17},{13,21},{17,9},{21,13},{10,18... | collective-permute-start | bytes 589832 | tf_op jit(solution)/shard_map/ppermute | solution.py:328
  58.5 16.2 %copy-start = (bf16[128,2048]{1,0:T(8,128)(2,1)S(1)}, bf16[128,2048]{1,0:T(8,128)(2,1)}, u32[]{:S(2)}) copy-start(bf16[128,2048]{1,0:T(8,128)(2,1)} %cot_ref.1) | copy-start | bytes 1572868
  58.5 16.2 %copy-start.1 = (s32[128,8]{0,1:T(8,128)S(1)}, s32[128,8]{0,1:T(8,128)}, u32[]{:S(2)}) copy-start(s32[128,8]{0,1:T(8,128)} %param.6) | copy-start | bytes 12292
  58.5 16.1 %copy-start.2 = (f32[128,8]{0,1:T(8,128)S(1)}, f32[128,8]{0,1:T(8,128)}, u32[]{:S(2)}) copy-start(f32[128,8]{0,1:T(8,128)} %param.7) | copy-start | bytes 12292
  62.6 13.7 %collective-permute-start.23 = (bf16[256,1280]{1,0:T(8,128)(2,1)S(1)}, bf16[256,1280]{1,0:T(8,128)(2,1)S(1)}, u32[]{:S(2)}, u32[]{:S(2)}) collective-permute-start(bf16[256,1280]{1,0:T(8,128)(2,1)S(1)} %get-tuple-element.55), channel_id=1, source_target_pairs={{0,4},{4,0},{8,12},{12,8},{16,20},{20,16},{24,28},{28,24},{1,5},{5... | collective-permute-start | bytes 1966088 | tf_op jit(solution)/shard_map/ppermute | solution.py:394
  65.0 12.4 %collective-permute-start.13 = (bf16[256,1024]{1,0:T(8,128)(2,1)S(1)}, bf16[256,1024]{1,0:T(8,128)(2,1)S(1)}, u32[]{:S(2)}, u32[]{:S(2)}) collective-permute-start(bf16[256,1024]{1,0:T(8,128)(2,1)S(1)} %get-tuple-element.52), channel_id=1, source_target_pairs={{0,4},{4,0},{8,12},{12,8},{16,20},{20,16},{24,28},{28,24},{1,5},{5... | collective-permute-start | bytes 1572872 | tf_op jit(solution)/shard_map/ppermute | solution.py:394
  65.0 9.1 %collective-permute-start.15 = (bf16[96,1024]{1,0:T(8,128)(2,1)S(1)}, bf16[96,1024]{1,0:T(8,128)(2,1)S(1)}, u32[]{:S(2)}, u32[]{:S(2)}) collective-permute-start(bf16[96,1024]{1,0:T(8,128)(2,1)S(1)} %collective-permute-done.10.refs_6_), channel_id=1, source_target_pairs={{0,8},{4,12},{8,0},{12,4},{16,24},{20,28},{24,16},{28,20},{1,9},{5... | collective-permute-start | bytes 589832 | tf_op jit(solution)/shard_map/ppermute | solution.py:328
  68.6 8.7 %collective-permute-start.16 = (bf16[96,1024]{1,0:T(8,128)(2,1)S(1)}, bf16[96,1024]{1,0:T(8,128)(2,1)S(1)}, u32[]{:S(2)}, u32[]{:S(2)}) collective-permute-start(bf16[96,1024]{1,0:T(8,128)(2,1)S(1)} %collective-permute-done.11.refs_7_), channel_id=1, source_target_pairs={{0,4},{4,0},{8,12},{12,8},{16,20},{20,16},{24,28},{28,24},{1,5},{5... | collective-permute-start | bytes 589832 | tf_op jit(solution)/shard_map/ppermute | solution.py:394
  74.1 3.2 %collective-permute-start.17 = (bf16[96,1024]{1,0:T(8,128)(2,1)S(1)}, bf16[96,1024]{1,0:T(8,128)(2,1)S(1)}, u32[]{:S(2)}, u32[]{:S(2)}) collective-permute-start(bf16[96,1024]{1,0:T(8,128)(2,1)S(1)} %collective-permute-done.15.refs_8_), channel_id=1, source_target_pairs={{0,4},{4,0},{8,12},{12,8},{16,20},{20,16},{24,28},{28,24},{1,5},{5... | collective-permute-start | bytes 589832 | tf_op jit(solution)/shard_map/ppermute | solution.py:394
  74.1 3.2 %collective-permute-start.14 = (bf16[96,512]{1,0:T(8,128)(2,1)S(1)}, bf16[96,512]{1,0:T(8,128)(2,1)S(1)}, u32[]{:S(2)}, u32[]{:S(2)}) collective-permute-start(bf16[96,512]{1,0:T(8,128)(2,1)S(1)} %get-tuple-element.53), channel_id=1, source_target_pairs={{0,4},{4,0},{8,12},{12,8},{16,20},{20,16},{24,28},{28,24},{1,5},{5... | collective-permute-start | bytes 294920 | tf_op jit(solution)/shard_map/ppermute | solution.py:394
